TPU v7x, 512 devices: a whole 4x8x8 slice. The times are simulated.
512 devices in a mesh: segment: 4 (over x), graph: 128 (over y, z, core).
Axes of the slice: x: 4, y: 8, z: 8, core: 2. Of those that a mesh axis runs over, the one named last changes fastest.
Arguments:
- features: bfloat16 [65536, 1024], P('graph'), may hold values from -6 to 6
- weights: bfloat16 [8, 1024, 1024], P(None, 'graph'), may hold values from -0.75 to 0.75
- history: bfloat16 [8, 8192, 1024], P(None, 'graph'), may hold values from 0 to 1.1953125
- own_adj: bfloat16 [4, 16384, 128], P(None, 'graph'), may hold values from 0 to 0.00390625
- side_adj: bfloat16 [4, 4, 2048, 128], P(None, None, 'graph'), may hold values from 0 to 0.012451172
- hist_adj: bfloat16 [4, 8192, 128], P(None, 'graph'), may hold values from 0 to 0.009338379
- send_ids: int32 [4, 4, 2048], P(None, None, 'graph'), may hold values from 0 to 127, as said below
- hist_ids: int32 [4, 8192], P(None, 'graph'), may hold values from 0 to 63
Outputs:
- layer_out: bfloat16 [8, 65536, 1024], P('segment', 'graph')
Inputs may be any that keep to these rules, and one draw needn't show every extreme that they name: `send_ids`: each list of 16 row numbers for one batch, one partition and one direction has distinct entries.
All inputs are finite; a program needn't handle non-finite values.
Results may differ from a plain program's by a relative error of at most 0.0032.
Values may be sent and summed in bfloat16 or wider, within the bound.
No kernel may reach another device: no remote copies, remote signals or barrier semaphores. Data moves between devices by JAX's collectives and lax.ppermute only.
A program may use at most 64 MiB of HBM per device.

v0:
```python
import jax
import jax.numpy as jnp
from jax import lax
from jax.sharding import PartitionSpec as P

ALPHA = 0.1
LAMBDA = 1.5
OFFSETS = (1, -1, 2, -2)


def shifted(value, axis, steps):
    count = lax.axis_size(axis)
    initial, last = (max(0, -steps), min(count, count - steps))
    return lax.ppermute(value, axis, [(source, source + steps) for source in range(initial, last)])


def propagate(
    current, initial, layer_number, weight, tables, own_tile, side_tile, send_rows, past_rows
):
    edge_count = send_rows.shape[1]
    picked = jnp.take(current, send_rows.reshape(-1), axis=0)
    arrived = []
    for direction in range(len(OFFSETS)):
        outgoing = picked[direction * edge_count : (direction + 1) * edge_count]
        arrived.append(shifted(outgoing, "graph", OFFSETS[direction]))
    layer_table = lax.dynamic_index_in_dim(tables, layer_number, 0, keepdims=False)
    arrived.append(jnp.take(layer_table, past_rows, axis=0))
    gathered_rows = jnp.concatenate(arrived, axis=0)
    aggregate = jnp.dot(own_tile, current, preferred_element_type=jnp.float32)
    aggregate = aggregate + lax.dot_general(
        side_tile, gathered_rows, (((0,), (0,)), ((), ())), preferred_element_type=jnp.float32
    )
    support = (1.0 - ALPHA) * aggregate + ALPHA * initial.astype(jnp.float32)
    mixing = jnp.dot(support.astype(jnp.bfloat16), weight, preferred_element_type=jnp.float32)
    strength = jnp.log(LAMBDA / (layer_number.astype(jnp.float32) + 1.0) + 1.0)
    return jax.nn.relu((1.0 - strength) * support + strength * mixing).astype(jnp.bfloat16)


def record(output, new_rows, slot_index, batch_index, allowed):
    batch_rows = new_rows.shape[0]
    writable = allowed & (slot_index >= 0) & (slot_index < output.shape[0])
    slot_safe = jnp.clip(slot_index, 0, output.shape[0] - 1)
    offset_row = batch_index * batch_rows
    zero_index = jnp.int32(0)
    previous = lax.dynamic_slice(
        output, (slot_safe, offset_row, zero_index), (1, batch_rows, new_rows.shape[1])
    )
    chosen = jnp.where(writable, new_rows[None], previous)
    return lax.dynamic_update_slice(output, chosen, (slot_safe, offset_row, zero_index))


def batch_tiles(own_adj, side_adj, hist_adj, send_ids, hist_ids, batch_safe):
    batch_rows = own_adj.shape[2]
    side_edges = side_adj.shape[1] * side_adj.shape[2]
    own_tile = lax.dynamic_index_in_dim(own_adj, batch_safe, 0, keepdims=False)
    edge_tile = lax.dynamic_index_in_dim(side_adj, batch_safe, 0, keepdims=False).reshape(
        side_edges, batch_rows
    )
    past_tile = lax.dynamic_index_in_dim(hist_adj, batch_safe, 0, keepdims=False)
    side_tile = jnp.concatenate([edge_tile, past_tile], axis=0)
    send_rows = lax.dynamic_index_in_dim(send_ids, batch_safe, 0, keepdims=False)
    past_rows = lax.dynamic_index_in_dim(hist_ids, batch_safe, 0, keepdims=False)
    return (own_tile, side_tile, send_rows, past_rows)


def shards(features, weights, history, own_adj, side_adj, hist_adj, send_ids, hist_ids):
    segment_pos = lax.axis_index("segment")
    segment_count = lax.axis_size("segment")
    batch_count = own_adj.shape[0]
    batch_rows = own_adj.shape[2]
    layer_total = weights.shape[0]
    kept_slots = layer_total // segment_count
    slot_count = 3
    first_layer = jnp.array([0, 3, 5, 7], jnp.int32)[segment_pos]
    layer_count = jnp.array([3, 2, 2, 1], jnp.int32)[segment_pos]
    weight_base = jnp.minimum(first_layer, layer_total - slot_count)
    resident = lax.all_gather(
        lax.dynamic_slice_in_dim(weights, weight_base, slot_count, 0), "graph", axis=1, tiled=True
    )
    output = jnp.zeros((kept_slots, features.shape[0], features.shape[1]), jnp.bfloat16)
    incoming = jnp.zeros((batch_rows, features.shape[1]), jnp.bfloat16)
    tick_total = batch_count + segment_count - 1
    for moment in range(tick_total):
        batch_now = moment - segment_pos
        running = (batch_now >= 0) & (batch_now < batch_count)
        batch_safe = jnp.clip(batch_now, 0, batch_count - 1)
        initial = lax.dynamic_slice_in_dim(features, batch_safe * batch_rows, batch_rows, 0)
        current = jnp.where(segment_pos == 0, initial, incoming)
        output = record(
            output,
            current,
            first_layer - 1 - kept_slots * segment_pos,
            batch_safe,
            running & (segment_pos > 0),
        )
        own_tile, side_tile, send_rows, past_rows = batch_tiles(
            own_adj, side_adj, hist_adj, send_ids, hist_ids, batch_safe
        )
        for position in range(slot_count):
            layer_number = jnp.minimum(first_layer + position, layer_total - 1)
            weight_slot = jnp.minimum(first_layer - weight_base + position, slot_count - 1)
            weight = lax.dynamic_index_in_dim(resident, weight_slot, 0, keepdims=False)
            updated = propagate(
                current,
                initial,
                layer_number,
                weight,
                history,
                own_tile,
                side_tile,
                send_rows,
                past_rows,
            )
            active = position < layer_count
            current = jnp.where(active, updated, current)
            output = record(
                output,
                current,
                first_layer + position - kept_slots * segment_pos,
                batch_safe,
                running & active,
            )
        if moment + 1 < tick_total:
            incoming = shifted(current, "segment", 1)
    return output


def solution(mesh):
    in_specs = (
        P("graph", None),
        P(None, "graph", None),
        P(None, "graph", None),
        P(None, "graph", None),
        P(None, None, "graph", None),
        P(None, "graph", None),
        P(None, None, "graph"),
        P(None, "graph"),
    )
    out_specs = P("segment", "graph", None)
    return jax.shard_map(shards, mesh=mesh, in_specs=in_specs, out_specs=out_specs, check_vma=False)
```

profile of v0, /device:TPU:34, one launch (start us, length us, event | category | flops | bytes accessed | tf_op | source)
XLA Modules:
  0.0 661.9 jit_solution(17037022333091565794)
XLA Ops:
  17.0 10.3 %collective-permute-start.1 = (bf16[16,1024]{1,0:T(8,128)(2,1)S(1)}, bf16[16,1024]{1,0:T(8,128)(2,1)S(1)}, u32[]{:S(2)}, u32[]{:S(2)}) collective-permute-start(bf16[16,1024]{1,0:T(8,128)(2,1)S(1)} %get-tuple-element.120), channel_id=1, source_target_pairs={{1,0},{2,1},{3,2},{4,3},{5,4},{6,5},{7,6},{8,7},{9,8},{10,9},{11,1... | collective-permute-start | bytes 98312 | tf_op jit(solution)/shard_map/ppermute | solution.py:14
  29.2 7.2 %collective-permute-start.3 = (bf16[16,1024]{1,0:T(8,128)(2,1)S(1)}, bf16[16,1024]{1,0:T(8,128)(2,1)S(1)}, u32[]{:S(2)}, u32[]{:S(2)}) collective-permute-start(bf16[16,1024]{1,0:T(8,128)(2,1)S(1)} %get-tuple-element.118), channel_id=1, source_target_pairs={{2,0},{3,1},{4,2},{5,3},{6,4},{7,5},{8,6},{9,7},{10,8},{11,9},{12,... | collective-permute-start | bytes 98312 | tf_op jit(solution)/shard_map/ppermute | solution.py:14
  46.9 52.8 %all-gather.2.cloned.1.call-done = bf16[3,1024,1024]{2,1,0:T(8,128)(2,1)} async-done(((bf16[3,8,1024]{2,1,0:T(8,128)(2,1)}), bf16[3,1024,1024]{2,1,0:T(8,128)(2,1)}) %all-gather.2.cloned.1.call-update) | async-done | bytes 6291472 | tf_op jit(solution)/shard_map/all_gather | solution.py:77
  105.7 6.7 %collective-permute-start.5 = (bf16[16,1024]{1,0:T(8,128)(2,1)S(1)}, bf16[16,1024]{1,0:T(8,128)(2,1)S(1)}, u32[]{:S(2)}, u32[]{:S(2)}) collective-permute-start(bf16[16,1024]{1,0:T(8,128)(2,1)S(1)} %get-tuple-element.116), channel_id=1, source_target_pairs={{1,0},{2,1},{3,2},{4,3},{5,4},{6,5},{7,6},{8,7},{9,8},{10,9},{11,1... | collective-permute-start | bytes 98312 | tf_op jit(solution)/shard_map/ppermute | solution.py:14
  114.4 7.2 %collective-permute-start.7 = (bf16[16,1024]{1,0:T(8,128)(2,1)S(1)}, bf16[16,1024]{1,0:T(8,128)(2,1)S(1)}, u32[]{:S(2)}, u32[]{:S(2)}) collective-permute-start(bf16[16,1024]{1,0:T(8,128)(2,1)S(1)} %get-tuple-element.114), channel_id=1, source_target_pairs={{2,0},{3,1},{4,2},{5,3},{6,4},{7,5},{8,6},{9,7},{10,8},{11,9},{12,... | collective-permute-start | bytes 98312 | tf_op jit(solution)/shard_map/ppermute | solution.py:14
  129.4 7.0 %collective-permute-start.9 = (bf16[16,1024]{1,0:T(8,128)(2,1)S(1)}, bf16[16,1024]{1,0:T(8,128)(2,1)S(1)}, u32[]{:S(2)}, u32[]{:S(2)}) collective-permute-start(bf16[16,1024]{1,0:T(8,128)(2,1)S(1)} %get-tuple-element.112), channel_id=1, source_target_pairs={{1,0},{2,1},{3,2},{4,3},{5,4},{6,5},{7,6},{8,7},{9,8},{10,9},{11,1... | collective-permute-start | bytes 98312 | tf_op jit(solution)/shard_map/ppermute | solution.py:14
  138.3 7.2 %collective-permute-start.11 = (bf16[16,1024]{1,0:T(8,128)(2,1)S(1)}, bf16[16,1024]{1,0:T(8,128)(2,1)S(1)}, u32[]{:S(2)}, u32[]{:S(2)}) collective-permute-start(bf16[16,1024]{1,0:T(8,128)(2,1)S(1)} %get-tuple-element.110), channel_id=1, source_target_pairs={{2,0},{3,1},{4,2},{5,3},{6,4},{7,5},{8,6},{9,7},{10,8},{11,9},{12,... | collective-permute-start | bytes 98312 | tf_op jit(solution)/shard_map/ppermute | solution.py:14
  150.4 3.4 collective-permute-start.12
  153.9 4.7 collective-permute-done.12
  164.0 7.0 %collective-permute-start.14 = (bf16[16,1024]{1,0:T(8,128)(2,1)S(1)}, bf16[16,1024]{1,0:T(8,128)(2,1)S(1)}, u32[]{:S(2)}, u32[]{:S(2)}) collective-permute-start(bf16[16,1024]{1,0:T(8,128)(2,1)S(1)} %get-tuple-element.108), channel_id=1, source_target_pairs={{1,0},{2,1},{3,2},{4,3},{5,4},{6,5},{7,6},{8,7},{9,8},{10,9},{11,1... | collective-permute-start | bytes 98312 | tf_op jit(solution)/shard_map/ppermute | solution.py:14
  172.9 7.2 %collective-permute-start.16 = (bf16[16,1024]{1,0:T(8,128)(2,1)S(1)}, bf16[16,1024]{1,0:T(8,128)(2,1)S(1)}, u32[]{:S(2)}, u32[]{:S(2)}) collective-permute-start(bf16[16,1024]{1,0:T(8,128)(2,1)S(1)} %get-tuple-element.106), channel_id=1, source_target_pairs={{2,0},{3,1},{4,2},{5,3},{6,4},{7,5},{8,6},{9,7},{10,8},{11,9},{12,... | collective-permute-start | bytes 98312 | tf_op jit(solution)/shard_map/ppermute | solution.py:14
  188.6 7.0 %collective-permute-start.18 = (bf16[16,1024]{1,0:T(8,128)(2,1)S(1)}, bf16[16,1024]{1,0:T(8,128)(2,1)S(1)}, u32[]{:S(2)}, u32[]{:S(2)}) collective-permute-start(bf16[16,1024]{1,0:T(8,128)(2,1)S(1)} %get-tuple-element.104), channel_id=1, source_target_pairs={{1,0},{2,1},{3,2},{4,3},{5,4},{6,5},{7,6},{8,7},{9,8},{10,9},{11,1... | collective-permute-start | bytes 98312 | tf_op jit(solution)/shard_map/ppermute | solution.py:14
  197.5 7.2 %collective-permute-start.20 = (bf16[16,1024]{1,0:T(8,128)(2,1)S(1)}, bf16[16,1024]{1,0:T(8,128)(2,1)S(1)}, u32[]{:S(2)}, u32[]{:S(2)}) collective-permute-start(bf16[16,1024]{1,0:T(8,128)(2,1)S(1)} %get-tuple-element.102), channel_id=1, source_target_pairs={{2,0},{3,1},{4,2},{5,3},{6,4},{7,5},{8,6},{9,7},{10,8},{11,9},{12,... | collective-permute-start | bytes 98312 | tf_op jit(solution)/shard_map/ppermute | solution.py:14
  206.9 2.9 fusion.383
  213.3 7.0 %collective-permute-start.22 = (bf16[16,1024]{1,0:T(8,128)(2,1)S(1)}, bf16[16,1024]{1,0:T(8,128)(2,1)S(1)}, u32[]{:S(2)}, u32[]{:S(2)}) collective-permute-start(bf16[16,1024]{1,0:T(8,128)(2,1)S(1)} %get-tuple-element.100), channel_id=1, source_target_pairs={{1,0},{2,1},{3,2},{4,3},{5,4},{6,5},{7,6},{8,7},{9,8},{10,9},{11,1... | collective-permute-start | bytes 98312 | tf_op jit(solution)/shard_map/ppermute | solution.py:14
  222.2 7.2 %collective-permute-start.24 = (bf16[16,1024]{1,0:T(8,128)(2,1)S(1)}, bf16[16,1024]{1,0:T(8,128)(2,1)S(1)}, u32[]{:S(2)}, u32[]{:S(2)}) collective-permute-start(bf16[16,1024]{1,0:T(8,128)(2,1)S(1)} %get-tuple-element.98), channel_id=1, source_target_pairs={{2,0},{3,1},{4,2},{5,3},{6,4},{7,5},{8,6},{9,7},{10,8},{11,9},{12,... | collective-permute-start | bytes 98312 | tf_op jit(solution)/shard_map/ppermute | solution.py:14
  231.6 2.9 fusion.382
  234.5 3.4 collective-permute-start.25
  237.9 4.8 collective-permute-done.25
  248.1 7.0 %collective-permute-start.27 = (bf16[16,1024]{1,0:T(8,128)(2,1)S(1)}, bf16[16,1024]{1,0:T(8,128)(2,1)S(1)}, u32[]{:S(2)}, u32[]{:S(2)}) collective-permute-start(bf16[16,1024]{1,0:T(8,128)(2,1)S(1)} %get-tuple-element.96), channel_id=1, source_target_pairs={{1,0},{2,1},{3,2},{4,3},{5,4},{6,5},{7,6},{8,7},{9,8},{10,9},{11,1... | collective-permute-start | bytes 98312 | tf_op jit(solution)/shard_map/ppermute | solution.py:14
  257.0 7.4 %collective-permute-start.29 = (bf16[16,1024]{1,0:T(8,128)(2,1)S(1)}, bf16[16,1024]{1,0:T(8,128)(2,1)S(1)}, u32[]{:S(2)}, u32[]{:S(2)}) collective-permute-start(bf16[16,1024]{1,0:T(8,128)(2,1)S(1)} %get-tuple-element.94), channel_id=1, source_target_pairs={{2,0},{3,1},{4,2},{5,3},{6,4},{7,5},{8,6},{9,7},{10,8},{11,9},{12,... | collective-permute-start | bytes 98312 | tf_op jit(solution)/shard_map/ppermute | solution.py:14
  272.8 7.0 %collective-permute-start.31 = (bf16[16,1024]{1,0:T(8,128)(2,1)S(1)}, bf16[16,1024]{1,0:T(8,128)(2,1)S(1)}, u32[]{:S(2)}, u32[]{:S(2)}) collective-permute-start(bf16[16,1024]{1,0:T(8,128)(2,1)S(1)} %get-tuple-element.92), channel_id=1, source_target_pairs={{1,0},{2,1},{3,2},{4,3},{5,4},{6,5},{7,6},{8,7},{9,8},{10,9},{11,1... | collective-permute-start | bytes 98312 | tf_op jit(solution)/shard_map/ppermute | solution.py:14
  281.7 7.2 %collective-permute-start.33 = (bf16[16,1024]{1,0:T(8,128)(2,1)S(1)}, bf16[16,1024]{1,0:T(8,128)(2,1)S(1)}, u32[]{:S(2)}, u32[]{:S(2)}) collective-permute-start(bf16[16,1024]{1,0:T(8,128)(2,1)S(1)} %get-tuple-element.90), channel_id=1, source_target_pairs={{2,0},{3,1},{4,2},{5,3},{6,4},{7,5},{8,6},{9,7},{10,8},{11,9},{12,... | collective-permute-start | bytes 98312 | tf_op jit(solution)/shard_map/ppermute | solution.py:14
  297.5 7.0 %collective-permute-start.35 = (bf16[16,1024]{1,0:T(8,128)(2,1)S(1)}, bf16[16,1024]{1,0:T(8,128)(2,1)S(1)}, u32[]{:S(2)}, u32[]{:S(2)}) collective-permute-start(bf16[16,1024]{1,0:T(8,128)(2,1)S(1)} %get-tuple-element.88), channel_id=1, source_target_pairs={{1,0},{2,1},{3,2},{4,3},{5,4},{6,5},{7,6},{8,7},{9,8},{10,9},{11,1... | collective-permute-start | bytes 98312 | tf_op jit(solution)/shard_map/ppermute | solution.py:14
  306.4 7.2 %collective-permute-start.37 = (bf16[16,1024]{1,0:T(8,128)(2,1)S(1)}, bf16[16,1024]{1,0:T(8,128)(2,1)S(1)}, u32[]{:S(2)}, u32[]{:S(2)}) collective-permute-start(bf16[16,1024]{1,0:T(8,128)(2,1)S(1)} %get-tuple-element.86), channel_id=1, source_target_pairs={{2,0},{3,1},{4,2},{5,3},{6,4},{7,5},{8,6},{9,7},{10,8},{11,9},{12,... | collective-permute-start | bytes 98312 | tf_op jit(solution)/shard_map/ppermute | solution.py:14
  318.7 3.4 collective-permute-start.38
  322.2 4.7 collective-permute-done.38
  332.2 7.0 %collective-permute-start.40 = (bf16[16,1024]{1,0:T(8,128)(2,1)S(1)}, bf16[16,1024]{1,0:T(8,128)(2,1)S(1)}, u32[]{:S(2)}, u32[]{:S(2)}) collective-permute-start(bf16[16,1024]{1,0:T(8,128)(2,1)S(1)} %get-tuple-element.84), channel_id=1, source_target_pairs={{1,0},{2,1},{3,2},{4,3},{5,4},{6,5},{7,6},{8,7},{9,8},{10,9},{11,1... | collective-permute-start | bytes 98312 | tf_op jit(solution)/shard_map/ppermute | solution.py:14
  341.1 7.2 %collective-permute-start.42 = (bf16[16,1024]{1,0:T(8,128)(2,1)S(1)}, bf16[16,1024]{1,0:T(8,128)(2,1)S(1)}, u32[]{:S(2)}, u32[]{:S(2)}) collective-permute-start(bf16[16,1024]{1,0:T(8,128)(2,1)S(1)} %get-tuple-element.82), channel_id=1, source_target_pairs={{2,0},{3,1},{4,2},{5,3},{6,4},{7,5},{8,6},{9,7},{10,8},{11,9},{12,... | collective-permute-start | bytes 98312 | tf_op jit(solution)/shard_map/ppermute | solution.py:14
  350.5 2.9 fusion.376
  356.9 7.0 %collective-permute-start.44 = (bf16[16,1024]{1,0:T(8,128)(2,1)S(1)}, bf16[16,1024]{1,0:T(8,128)(2,1)S(1)}, u32[]{:S(2)}, u32[]{:S(2)}) collective-permute-start(bf16[16,1024]{1,0:T(8,128)(2,1)S(1)} %get-tuple-element.80), channel_id=1, source_target_pairs={{1,0},{2,1},{3,2},{4,3},{5,4},{6,5},{7,6},{8,7},{9,8},{10,9},{11,1... | collective-permute-start | bytes 98312 | tf_op jit(solution)/shard_map/ppermute | solution.py:14
  365.8 7.2 %collective-permute-start.46 = (bf16[16,1024]{1,0:T(8,128)(2,1)S(1)}, bf16[16,1024]{1,0:T(8,128)(2,1)S(1)}, u32[]{:S(2)}, u32[]{:S(2)}) collective-permute-start(bf16[16,1024]{1,0:T(8,128)(2,1)S(1)} %get-tuple-element.78), channel_id=1, source_target_pairs={{2,0},{3,1},{4,2},{5,3},{6,4},{7,5},{8,6},{9,7},{10,8},{11,9},{12,... | collective-permute-start | bytes 98312 | tf_op jit(solution)/shard_map/ppermute | solution.py:14
  375.2 2.9 fusion.375
  381.6 7.0 %collective-permute-start.48 = (bf16[16,1024]{1,0:T(8,128)(2,1)S(1)}, bf16[16,1024]{1,0:T(8,128)(2,1)S(1)}, u32[]{:S(2)}, u32[]{:S(2)}) collective-permute-start(bf16[16,1024]{1,0:T(8,128)(2,1)S(1)} %get-tuple-element.76), channel_id=1, source_target_pairs={{1,0},{2,1},{3,2},{4,3},{5,4},{6,5},{7,6},{8,7},{9,8},{10,9},{11,1... | collective-permute-start | bytes 98312 | tf_op jit(solution)/shard_map/ppermute | solution.py:14
  390.5 7.2 %collective-permute-start.50 = (bf16[16,1024]{1,0:T(8,128)(2,1)S(1)}, bf16[16,1024]{1,0:T(8,128)(2,1)S(1)}, u32[]{:S(2)}, u32[]{:S(2)}) collective-permute-start(bf16[16,1024]{1,0:T(8,128)(2,1)S(1)} %get-tuple-element.74), channel_id=1, source_target_pairs={{2,0},{3,1},{4,2},{5,3},{6,4},{7,5},{8,6},{9,7},{10,8},{11,9},{12,... | collective-permute-start | bytes 98312 | tf_op jit(solution)/shard_map/ppermute | solution.py:14
  399.9 2.9 fusion.374
  402.8 3.4 collective-permute-start.51
  406.2 4.8 collective-permute-done.51
  416.3 7.0 %collective-permute-start.53 = (bf16[16,1024]{1,0:T(8,128)(2,1)S(1)}, bf16[16,1024]{1,0:T(8,128)(2,1)S(1)}, u32[]{:S(2)}, u32[]{:S(2)}) collective-permute-start(bf16[16,1024]{1,0:T(8,128)(2,1)S(1)} %get-tuple-element.72), channel_id=1, source_target_pairs={{1,0},{2,1},{3,2},{4,3},{5,4},{6,5},{7,6},{8,7},{9,8},{10,9},{11,1... | collective-permute-start | bytes 98312 | tf_op jit(solution)/shard_map/ppermute | solution.py:14
  425.2 7.2 %collective-permute-start.55 = (bf16[16,1024]{1,0:T(8,128)(2,1)S(1)}, bf16[16,1024]{1,0:T(8,128)(2,1)S(1)}, u32[]{:S(2)}, u32[]{:S(2)}) collective-permute-start(bf16[16,1024]{1,0:T(8,128)(2,1)S(1)} %get-tuple-element.70), channel_id=1, source_target_pairs={{2,0},{3,1},{4,2},{5,3},{6,4},{7,5},{8,6},{9,7},{10,8},{11,9},{12,... | collective-permute-start | bytes 98312 | tf_op jit(solution)/shard_map/ppermute | solution.py:14
  434.6 2.9 fusion.372
  441.1 7.0 %collective-permute-start.57 = (bf16[16,1024]{1,0:T(8,128)(2,1)S(1)}, bf16[16,1024]{1,0:T(8,128)(2,1)S(1)}, u32[]{:S(2)}, u32[]{:S(2)}) collective-permute-start(bf16[16,1024]{1,0:T(8,128)(2,1)S(1)} %get-tuple-element.68), channel_id=1, source_target_pairs={{1,0},{2,1},{3,2},{4,3},{5,4},{6,5},{7,6},{8,7},{9,8},{10,9},{11,1... | collective-permute-start | bytes 98312 | tf_op jit(solution)/shard_map/ppermute | solution.py:14
  450.0 7.5 %collective-permute-start.59 = (bf16[16,1024]{1,0:T(8,128)(2,1)S(1)}, bf16[16,1024]{1,0:T(8,128)(2,1)S(1)}, u32[]{:S(2)}, u32[]{:S(2)}) collective-permute-start(bf16[16,1024]{1,0:T(8,128)(2,1)S(1)} %get-tuple-element.66), channel_id=1, source_target_pairs={{2,0},{3,1},{4,2},{5,3},{6,4},{7,5},{8,6},{9,7},{10,8},{11,9},{12,... | collective-permute-start | bytes 98312 | tf_op jit(solution)/shard_map/ppermute | solution.py:14
  465.7 7.0 %collective-permute-start.61 = (bf16[16,1024]{1,0:T(8,128)(2,1)S(1)}, bf16[16,1024]{1,0:T(8,128)(2,1)S(1)}, u32[]{:S(2)}, u32[]{:S(2)}) collective-permute-start(bf16[16,1024]{1,0:T(8,128)(2,1)S(1)} %get-tuple-element.64), channel_id=1, source_target_pairs={{1,0},{2,1},{3,2},{4,3},{5,4},{6,5},{7,6},{8,7},{9,8},{10,9},{11,1... | collective-permute-start | bytes 98312 | tf_op jit(solution)/shard_map/ppermute | solution.py:14
  474.6 7.2 %collective-permute-start.63 = (bf16[16,1024]{1,0:T(8,128)(2,1)S(1)}, bf16[16,1024]{1,0:T(8,128)(2,1)S(1)}, u32[]{:S(2)}, u32[]{:S(2)}) collective-permute-start(bf16[16,1024]{1,0:T(8,128)(2,1)S(1)} %get-tuple-element.62), channel_id=1, source_target_pairs={{2,0},{3,1},{4,2},{5,3},{6,4},{7,5},{8,6},{9,7},{10,8},{11,9},{12,... | collective-permute-start | bytes 98312 | tf_op jit(solution)/shard_map/ppermute | solution.py:14
  486.9 3.4 collective-permute-start.64
  490.4 4.7 collective-permute-done.64
  500.5 7.0 %collective-permute-start.66 = (bf16[16,1024]{1,0:T(8,128)(2,1)S(1)}, bf16[16,1024]{1,0:T(8,128)(2,1)S(1)}, u32[]{:S(2)}, u32[]{:S(2)}) collective-permute-start(bf16[16,1024]{1,0:T(8,128)(2,1)S(1)} %get-tuple-element.60), channel_id=1, source_target_pairs={{1,0},{2,1},{3,2},{4,3},{5,4},{6,5},{7,6},{8,7},{9,8},{10,9},{11,1... | collective-permute-start | bytes 98312 | tf_op jit(solution)/shard_map/ppermute | solution.py:14
  509.4 7.2 %collective-permute-start.68 = (bf16[16,1024]{1,0:T(8,128)(2,1)S(1)}, bf16[16,1024]{1,0:T(8,128)(2,1)S(1)}, u32[]{:S(2)}, u32[]{:S(2)}) collective-permute-start(bf16[16,1024]{1,0:T(8,128)(2,1)S(1)} %get-tuple-element.58), channel_id=1, source_target_pairs={{2,0},{3,1},{4,2},{5,3},{6,4},{7,5},{8,6},{9,7},{10,8},{11,9},{12,... | collective-permute-start | bytes 98312 | tf_op jit(solution)/shard_map/ppermute | solution.py:14
  525.1 7.0 %collective-permute-start.70 = (bf16[16,1024]{1,0:T(8,128)(2,1)S(1)}, bf16[16,1024]{1,0:T(8,128)(2,1)S(1)}, u32[]{:S(2)}, u32[]{:S(2)}) collective-permute-start(bf16[16,1024]{1,0:T(8,128)(2,1)S(1)} %get-tuple-element.56), channel_id=1, source_target_pairs={{1,0},{2,1},{3,2},{4,3},{5,4},{6,5},{7,6},{8,7},{9,8},{10,9},{11,1... | collective-permute-start | bytes 98312 | tf_op jit(solution)/shard_map/ppermute | solution.py:14
  534.0 7.2 %collective-permute-start.72 = (bf16[16,1024]{1,0:T(8,128)(2,1)S(1)}, bf16[16,1024]{1,0:T(8,128)(2,1)S(1)}, u32[]{:S(2)}, u32[]{:S(2)}) collective-permute-start(bf16[16,1024]{1,0:T(8,128)(2,1)S(1)} %get-tuple-element.54), channel_id=1, source_target_pairs={{2,0},{3,1},{4,2},{5,3},{6,4},{7,5},{8,6},{9,7},{10,8},{11,9},{12,... | collective-permute-start | bytes 98312 | tf_op jit(solution)/shard_map/ppermute | solution.py:14
  549.8 7.0 %collective-permute-start.74 = (bf16[16,1024]{1,0:T(8,128)(2,1)S(1)}, bf16[16,1024]{1,0:T(8,128)(2,1)S(1)}, u32[]{:S(2)}, u32[]{:S(2)}) collective-permute-start(bf16[16,1024]{1,0:T(8,128)(2,1)S(1)} %get-tuple-element.52), channel_id=1, source_target_pairs={{1,0},{2,1},{3,2},{4,3},{5,4},{6,5},{7,6},{8,7},{9,8},{10,9},{11,1... | collective-permute-start | bytes 98312 | tf_op jit(solution)/shard_map/ppermute | solution.py:14
  558.7 7.2 %collective-permute-start.76 = (bf16[16,1024]{1,0:T(8,128)(2,1)S(1)}, bf16[16,1024]{1,0:T(8,128)(2,1)S(1)}, u32[]{:S(2)}, u32[]{:S(2)}) collective-permute-start(bf16[16,1024]{1,0:T(8,128)(2,1)S(1)} %get-tuple-element.50), channel_id=1, source_target_pairs={{2,0},{3,1},{4,2},{5,3},{6,4},{7,5},{8,6},{9,7},{10,8},{11,9},{12,... | collective-permute-start | bytes 98312 | tf_op jit(solution)/shard_map/ppermute | solution.py:14
  568.1 2.9 fusion.366
  571.0 3.4 collective-permute-start.77
  574.4 4.8 collective-permute-done.77
  584.6 7.0 %collective-permute-start.79 = (bf16[16,1024]{1,0:T(8,128)(2,1)S(1)}, bf16[16,1024]{1,0:T(8,128)(2,1)S(1)}, u32[]{:S(2)}, u32[]{:S(2)}) collective-permute-start(bf16[16,1024]{1,0:T(8,128)(2,1)S(1)} %get-tuple-element.48), channel_id=1, source_target_pairs={{1,0},{2,1},{3,2},{4,3},{5,4},{6,5},{7,6},{8,7},{9,8},{10,9},{11,1... | collective-permute-start | bytes 98312 | tf_op jit(solution)/shard_map/ppermute | solution.py:14
  593.5 7.2 %collective-permute-start.81 = (bf16[16,1024]{1,0:T(8,128)(2,1)S(1)}, bf16[16,1024]{1,0:T(8,128)(2,1)S(1)}, u32[]{:S(2)}, u32[]{:S(2)}) collective-permute-start(bf16[16,1024]{1,0:T(8,128)(2,1)S(1)} %get-tuple-element.46), channel_id=1, source_target_pairs={{2,0},{3,1},{4,2},{5,3},{6,4},{7,5},{8,6},{9,7},{10,8},{11,9},{12,... | collective-permute-start | bytes 98312 | tf_op jit(solution)/shard_map/ppermute | solution.py:14
  602.9 2.9 fusion.364
  609.2 7.0 %collective-permute-start.83 = (bf16[16,1024]{1,0:T(8,128)(2,1)S(1)}, bf16[16,1024]{1,0:T(8,128)(2,1)S(1)}, u32[]{:S(2)}, u32[]{:S(2)}) collective-permute-start(bf16[16,1024]{1,0:T(8,128)(2,1)S(1)} %get-tuple-element.44), channel_id=1, source_target_pairs={{1,0},{2,1},{3,2},{4,3},{5,4},{6,5},{7,6},{8,7},{9,8},{10,9},{11,1... | collective-permute-start | bytes 98312 | tf_op jit(solution)/shard_map/ppermute | solution.py:14
  618.1 7.2 %collective-permute-start.85 = (bf16[16,1024]{1,0:T(8,128)(2,1)S(1)}, bf16[16,1024]{1,0:T(8,128)(2,1)S(1)}, u32[]{:S(2)}, u32[]{:S(2)}) collective-permute-start(bf16[16,1024]{1,0:T(8,128)(2,1)S(1)} %get-tuple-element.42), channel_id=1, source_target_pairs={{2,0},{3,1},{4,2},{5,3},{6,4},{7,5},{8,6},{9,7},{10,8},{11,9},{12,... | collective-permute-start | bytes 98312 | tf_op jit(solution)/shard_map/ppermute | solution.py:14
  627.5 2.9 fusion.363
  633.9 7.0 %collective-permute-start.87 = (bf16[16,1024]{1,0:T(8,128)(2,1)S(1)}, bf16[16,1024]{1,0:T(8,128)(2,1)S(1)}, u32[]{:S(2)}, u32[]{:S(2)}) collective-permute-start(bf16[16,1024]{1,0:T(8,128)(2,1)S(1)} %get-tuple-element.40), channel_id=1, source_target_pairs={{1,0},{2,1},{3,2},{4,3},{5,4},{6,5},{7,6},{8,7},{9,8},{10,9},{11,1... | collective-permute-start | bytes 98312 | tf_op jit(solution)/shard_map/ppermute | solution.py:14
  642.8 7.2 %collective-permute-start.89 = (bf16[16,1024]{1,0:T(8,128)(2,1)S(1)}, bf16[16,1024]{1,0:T(8,128)(2,1)S(1)}, u32[]{:S(2)}, u32[]{:S(2)}) collective-permute-start(bf16[16,1024]{1,0:T(8,128)(2,1)S(1)} %get-tuple-element.38), channel_id=1, source_target_pairs={{2,0},{3,1},{4,2},{5,3},{6,4},{7,5},{8,6},{9,7},{10,8},{11,9},{12,... | collective-permute-start | bytes 98312 | tf_op jit(solution)/shard_map/ppermute | solution.py:14
  (431 shorter events, 208.6 us)
Async XLA Ops:
  6.5 93.2 %all-gather.2.cloned.1.call-start = ((), (), s32[]{:S(2)}) async-start(), calls=%async_computation | async-start | bytes 6340608 | tf_op jit(solution)/shard_map/all_gather | solution.py:77
  15.0 31.4 %collective-permute-start = (bf16[16,1024]{1,0:T(8,128)(2,1)S(1)}, bf16[16,1024]{1,0:T(8,128)(2,1)S(1)}, u32[]{:S(2)}, u32[]{:S(2)}) collective-permute-start(bf16[16,1024]{1,0:T(8,128)(2,1)S(1)} %get-tuple-element.121), channel_id=1, source_target_pairs={{0,1},{1,2},{2,3},{3,4},{4,5},{5,6},{6,7},{7,8},{8,9},{9,10},{10,1... | collective-permute-start | bytes 98312 | tf_op jit(solution)/shard_map/ppermute | solution.py:14
  17.0 29.5 %collective-permute-start.1 = (bf16[16,1024]{1,0:T(8,128)(2,1)S(1)}, bf16[16,1024]{1,0:T(8,128)(2,1)S(1)}, u32[]{:S(2)}, u32[]{:S(2)}) collective-permute-start(bf16[16,1024]{1,0:T(8,128)(2,1)S(1)} %get-tuple-element.120), channel_id=1, source_target_pairs={{1,0},{2,1},{3,2},{4,3},{5,4},{6,5},{7,6},{8,7},{9,8},{10,9},{11,1... | collective-permute-start | bytes 98312 | tf_op jit(solution)/shard_map/ppermute | solution.py:14
  27.2 19.3 %collective-permute-start.2 = (bf16[16,1024]{1,0:T(8,128)(2,1)S(1)}, bf16[16,1024]{1,0:T(8,128)(2,1)S(1)}, u32[]{:S(2)}, u32[]{:S(2)}) collective-permute-start(bf16[16,1024]{1,0:T(8,128)(2,1)S(1)} %get-tuple-element.119), channel_id=1, source_target_pairs={{0,2},{1,3},{2,4},{3,5},{4,6},{5,7},{6,8},{7,9},{8,10},{9,11},{10,... | collective-permute-start | bytes 98312 | tf_op jit(solution)/shard_map/ppermute | solution.py:14
  29.2 17.4 %collective-permute-start.3 = (bf16[16,1024]{1,0:T(8,128)(2,1)S(1)}, bf16[16,1024]{1,0:T(8,128)(2,1)S(1)}, u32[]{:S(2)}, u32[]{:S(2)}) collective-permute-start(bf16[16,1024]{1,0:T(8,128)(2,1)S(1)} %get-tuple-element.118), channel_id=1, source_target_pairs={{2,0},{3,1},{4,2},{5,3},{6,4},{7,5},{8,6},{9,7},{10,8},{11,9},{12,... | collective-permute-start | bytes 98312 | tf_op jit(solution)/shard_map/ppermute | solution.py:14
  103.3 18.3 %collective-permute-start.4 = (bf16[16,1024]{1,0:T(8,128)(2,1)S(1)}, bf16[16,1024]{1,0:T(8,128)(2,1)S(1)}, u32[]{:S(2)}, u32[]{:S(2)}) collective-permute-start(bf16[16,1024]{1,0:T(8,128)(2,1)S(1)} %get-tuple-element.117), channel_id=1, source_target_pairs={{0,1},{1,2},{2,3},{3,4},{4,5},{5,6},{6,7},{7,8},{8,9},{9,10},{10,1... | collective-permute-start | bytes 98312 | tf_op jit(solution)/shard_map/ppermute | solution.py:14
  105.7 16.0 %collective-permute-start.5 = (bf16[16,1024]{1,0:T(8,128)(2,1)S(1)}, bf16[16,1024]{1,0:T(8,128)(2,1)S(1)}, u32[]{:S(2)}, u32[]{:S(2)}) collective-permute-start(bf16[16,1024]{1,0:T(8,128)(2,1)S(1)} %get-tuple-element.116), channel_id=1, source_target_pairs={{1,0},{2,1},{3,2},{4,3},{5,4},{6,5},{7,6},{8,7},{9,8},{10,9},{11,1... | collective-permute-start | bytes 98312 | tf_op jit(solution)/shard_map/ppermute | solution.py:14
  112.5 9.2 %collective-permute-start.6 = (bf16[16,1024]{1,0:T(8,128)(2,1)S(1)}, bf16[16,1024]{1,0:T(8,128)(2,1)S(1)}, u32[]{:S(2)}, u32[]{:S(2)}) collective-permute-start(bf16[16,1024]{1,0:T(8,128)(2,1)S(1)} %get-tuple-element.115), channel_id=1, source_target_pairs={{0,2},{1,3},{2,4},{3,5},{4,6},{5,7},{6,8},{7,9},{8,10},{9,11},{10,... | collective-permute-start | bytes 98312 | tf_op jit(solution)/shard_map/ppermute | solution.py:14
  127.3 18.3 %collective-permute-start.8 = (bf16[16,1024]{1,0:T(8,128)(2,1)S(1)}, bf16[16,1024]{1,0:T(8,128)(2,1)S(1)}, u32[]{:S(2)}, u32[]{:S(2)}) collective-permute-start(bf16[16,1024]{1,0:T(8,128)(2,1)S(1)} %get-tuple-element.113), channel_id=1, source_target_pairs={{0,1},{1,2},{2,3},{3,4},{4,5},{5,6},{6,7},{7,8},{8,9},{9,10},{10,1... | collective-permute-start | bytes 98312 | tf_op jit(solution)/shard_map/ppermute | solution.py:14
  129.4 16.2 %collective-permute-start.9 = (bf16[16,1024]{1,0:T(8,128)(2,1)S(1)}, bf16[16,1024]{1,0:T(8,128)(2,1)S(1)}, u32[]{:S(2)}, u32[]{:S(2)}) collective-permute-start(bf16[16,1024]{1,0:T(8,128)(2,1)S(1)} %get-tuple-element.112), channel_id=1, source_target_pairs={{1,0},{2,1},{3,2},{4,3},{5,4},{6,5},{7,6},{8,7},{9,8},{10,9},{11,1... | collective-permute-start | bytes 98312 | tf_op jit(solution)/shard_map/ppermute | solution.py:14
  136.4 9.2 %collective-permute-start.10 = (bf16[16,1024]{1,0:T(8,128)(2,1)S(1)}, bf16[16,1024]{1,0:T(8,128)(2,1)S(1)}, u32[]{:S(2)}, u32[]{:S(2)}) collective-permute-start(bf16[16,1024]{1,0:T(8,128)(2,1)S(1)} %get-tuple-element.111), channel_id=1, source_target_pairs={{0,2},{1,3},{2,4},{3,5},{4,6},{5,7},{6,8},{7,9},{8,10},{9,11},{10,... | collective-permute-start | bytes 98312 | tf_op jit(solution)/shard_map/ppermute | solution.py:14
  161.3 18.8 %collective-permute-start.13 = (bf16[16,1024]{1,0:T(8,128)(2,1)S(1)}, bf16[16,1024]{1,0:T(8,128)(2,1)S(1)}, u32[]{:S(2)}, u32[]{:S(2)}) collective-permute-start(bf16[16,1024]{1,0:T(8,128)(2,1)S(1)} %get-tuple-element.109), channel_id=1, source_target_pairs={{0,1},{1,2},{2,3},{3,4},{4,5},{5,6},{6,7},{7,8},{8,9},{9,10},{10,1... | collective-permute-start | bytes 98312 | tf_op jit(solution)/shard_map/ppermute | solution.py:14
  164.0 16.2 %collective-permute-start.14 = (bf16[16,1024]{1,0:T(8,128)(2,1)S(1)}, bf16[16,1024]{1,0:T(8,128)(2,1)S(1)}, u32[]{:S(2)}, u32[]{:S(2)}) collective-permute-start(bf16[16,1024]{1,0:T(8,128)(2,1)S(1)} %get-tuple-element.108), channel_id=1, source_target_pairs={{1,0},{2,1},{3,2},{4,3},{5,4},{6,5},{7,6},{8,7},{9,8},{10,9},{11,1... | collective-permute-start | bytes 98312 | tf_op jit(solution)/shard_map/ppermute | solution.py:14
  170.9 9.2 %collective-permute-start.15 = (bf16[16,1024]{1,0:T(8,128)(2,1)S(1)}, bf16[16,1024]{1,0:T(8,128)(2,1)S(1)}, u32[]{:S(2)}, u32[]{:S(2)}) collective-permute-start(bf16[16,1024]{1,0:T(8,128)(2,1)S(1)} %get-tuple-element.107), channel_id=1, source_target_pairs={{0,2},{1,3},{2,4},{3,5},{4,6},{5,7},{6,8},{7,9},{8,10},{9,11},{10,... | collective-permute-start | bytes 98312 | tf_op jit(solution)/shard_map/ppermute | solution.py:14
  186.0 18.8 %collective-permute-start.17 = (bf16[16,1024]{1,0:T(8,128)(2,1)S(1)}, bf16[16,1024]{1,0:T(8,128)(2,1)S(1)}, u32[]{:S(2)}, u32[]{:S(2)}) collective-permute-start(bf16[16,1024]{1,0:T(8,128)(2,1)S(1)} %get-tuple-element.105), channel_id=1, source_target_pairs={{0,1},{1,2},{2,3},{3,4},{4,5},{5,6},{6,7},{7,8},{8,9},{9,10},{10,1... | collective-permute-start | bytes 98312 | tf_op jit(solution)/shard_map/ppermute | solution.py:14
  188.6 16.2 %collective-permute-start.18 = (bf16[16,1024]{1,0:T(8,128)(2,1)S(1)}, bf16[16,1024]{1,0:T(8,128)(2,1)S(1)}, u32[]{:S(2)}, u32[]{:S(2)}) collective-permute-start(bf16[16,1024]{1,0:T(8,128)(2,1)S(1)} %get-tuple-element.104), channel_id=1, source_target_pairs={{1,0},{2,1},{3,2},{4,3},{5,4},{6,5},{7,6},{8,7},{9,8},{10,9},{11,1... | collective-permute-start | bytes 98312 | tf_op jit(solution)/shard_map/ppermute | solution.py:14
  195.6 9.2 %collective-permute-start.19 = (bf16[16,1024]{1,0:T(8,128)(2,1)S(1)}, bf16[16,1024]{1,0:T(8,128)(2,1)S(1)}, u32[]{:S(2)}, u32[]{:S(2)}) collective-permute-start(bf16[16,1024]{1,0:T(8,128)(2,1)S(1)} %get-tuple-element.103), channel_id=1, source_target_pairs={{0,2},{1,3},{2,4},{3,5},{4,6},{5,7},{6,8},{7,9},{8,10},{9,11},{10,... | collective-permute-start | bytes 98312 | tf_op jit(solution)/shard_map/ppermute | solution.py:14
  210.6 18.8 %collective-permute-start.21 = (bf16[16,1024]{1,0:T(8,128)(2,1)S(1)}, bf16[16,1024]{1,0:T(8,128)(2,1)S(1)}, u32[]{:S(2)}, u32[]{:S(2)}) collective-permute-start(bf16[16,1024]{1,0:T(8,128)(2,1)S(1)} %get-tuple-element.101), channel_id=1, source_target_pairs={{0,1},{1,2},{2,3},{3,4},{4,5},{5,6},{6,7},{7,8},{8,9},{9,10},{10,1... | collective-permute-start | bytes 98312 | tf_op jit(solution)/shard_map/ppermute | solution.py:14
  213.3 16.2 %collective-permute-start.22 = (bf16[16,1024]{1,0:T(8,128)(2,1)S(1)}, bf16[16,1024]{1,0:T(8,128)(2,1)S(1)}, u32[]{:S(2)}, u32[]{:S(2)}) collective-permute-start(bf16[16,1024]{1,0:T(8,128)(2,1)S(1)} %get-tuple-element.100), channel_id=1, source_target_pairs={{1,0},{2,1},{3,2},{4,3},{5,4},{6,5},{7,6},{8,7},{9,8},{10,9},{11,1... | collective-permute-start | bytes 98312 | tf_op jit(solution)/shard_map/ppermute | solution.py:14
  220.3 9.2 %collective-permute-start.23 = (bf16[16,1024]{1,0:T(8,128)(2,1)S(1)}, bf16[16,1024]{1,0:T(8,128)(2,1)S(1)}, u32[]{:S(2)}, u32[]{:S(2)}) collective-permute-start(bf16[16,1024]{1,0:T(8,128)(2,1)S(1)} %get-tuple-element.99), channel_id=1, source_target_pairs={{0,2},{1,3},{2,4},{3,5},{4,6},{5,7},{6,8},{7,9},{8,10},{9,11},{10,... | collective-permute-start | bytes 98312 | tf_op jit(solution)/shard_map/ppermute | solution.py:14
  245.4 19.0 %collective-permute-start.26 = (bf16[16,1024]{1,0:T(8,128)(2,1)S(1)}, bf16[16,1024]{1,0:T(8,128)(2,1)S(1)}, u32[]{:S(2)}, u32[]{:S(2)}) collective-permute-start(bf16[16,1024]{1,0:T(8,128)(2,1)S(1)} %get-tuple-element.97), channel_id=1, source_target_pairs={{0,1},{1,2},{2,3},{3,4},{4,5},{5,6},{6,7},{7,8},{8,9},{9,10},{10,1... | collective-permute-start | bytes 98312 | tf_op jit(solution)/shard_map/ppermute | solution.py:14
  248.1 16.4 %collective-permute-start.27 = (bf16[16,1024]{1,0:T(8,128)(2,1)S(1)}, bf16[16,1024]{1,0:T(8,128)(2,1)S(1)}, u32[]{:S(2)}, u32[]{:S(2)}) collective-permute-start(bf16[16,1024]{1,0:T(8,128)(2,1)S(1)} %get-tuple-element.96), channel_id=1, source_target_pairs={{1,0},{2,1},{3,2},{4,3},{5,4},{6,5},{7,6},{8,7},{9,8},{10,9},{11,1... | collective-permute-start | bytes 98312 | tf_op jit(solution)/shard_map/ppermute | solution.py:14
  255.0 9.4 %collective-permute-start.28 = (bf16[16,1024]{1,0:T(8,128)(2,1)S(1)}, bf16[16,1024]{1,0:T(8,128)(2,1)S(1)}, u32[]{:S(2)}, u32[]{:S(2)}) collective-permute-start(bf16[16,1024]{1,0:T(8,128)(2,1)S(1)} %get-tuple-element.95), channel_id=1, source_target_pairs={{0,2},{1,3},{2,4},{3,5},{4,6},{5,7},{6,8},{7,9},{8,10},{9,11},{10,... | collective-permute-start | bytes 98312 | tf_op jit(solution)/shard_map/ppermute | solution.py:14
  270.1 18.9 %collective-permute-start.30 = (bf16[16,1024]{1,0:T(8,128)(2,1)S(1)}, bf16[16,1024]{1,0:T(8,128)(2,1)S(1)}, u32[]{:S(2)}, u32[]{:S(2)}) collective-permute-start(bf16[16,1024]{1,0:T(8,128)(2,1)S(1)} %get-tuple-element.93), channel_id=1, source_target_pairs={{0,1},{1,2},{2,3},{3,4},{4,5},{5,6},{6,7},{7,8},{8,9},{9,10},{10,1... | collective-permute-start | bytes 98312 | tf_op jit(solution)/shard_map/ppermute | solution.py:14
  272.8 16.2 %collective-permute-start.31 = (bf16[16,1024]{1,0:T(8,128)(2,1)S(1)}, bf16[16,1024]{1,0:T(8,128)(2,1)S(1)}, u32[]{:S(2)}, u32[]{:S(2)}) collective-permute-start(bf16[16,1024]{1,0:T(8,128)(2,1)S(1)} %get-tuple-element.92), channel_id=1, source_target_pairs={{1,0},{2,1},{3,2},{4,3},{5,4},{6,5},{7,6},{8,7},{9,8},{10,9},{11,1... | collective-permute-start | bytes 98312 | tf_op jit(solution)/shard_map/ppermute | solution.py:14
  279.8 9.2 %collective-permute-start.32 = (bf16[16,1024]{1,0:T(8,128)(2,1)S(1)}, bf16[16,1024]{1,0:T(8,128)(2,1)S(1)}, u32[]{:S(2)}, u32[]{:S(2)}) collective-permute-start(bf16[16,1024]{1,0:T(8,128)(2,1)S(1)} %get-tuple-element.91), channel_id=1, source_target_pairs={{0,2},{1,3},{2,4},{3,5},{4,6},{5,7},{6,8},{7,9},{8,10},{9,11},{10,... | collective-permute-start | bytes 98312 | tf_op jit(solution)/shard_map/ppermute | solution.py:14
  294.8 18.8 %collective-permute-start.34 = (bf16[16,1024]{1,0:T(8,128)(2,1)S(1)}, bf16[16,1024]{1,0:T(8,128)(2,1)S(1)}, u32[]{:S(2)}, u32[]{:S(2)}) collective-permute-start(bf16[16,1024]{1,0:T(8,128)(2,1)S(1)} %get-tuple-element.89), channel_id=1, source_target_pairs={{0,1},{1,2},{2,3},{3,4},{4,5},{5,6},{6,7},{7,8},{8,9},{9,10},{10,1... | collective-permute-start | bytes 98312 | tf_op jit(solution)/shard_map/ppermute | solution.py:14
  297.5 16.2 %collective-permute-start.35 = (bf16[16,1024]{1,0:T(8,128)(2,1)S(1)}, bf16[16,1024]{1,0:T(8,128)(2,1)S(1)}, u32[]{:S(2)}, u32[]{:S(2)}) collective-permute-start(bf16[16,1024]{1,0:T(8,128)(2,1)S(1)} %get-tuple-element.88), channel_id=1, source_target_pairs={{1,0},{2,1},{3,2},{4,3},{5,4},{6,5},{7,6},{8,7},{9,8},{10,9},{11,1... | collective-permute-start | bytes 98312 | tf_op jit(solution)/shard_map/ppermute | solution.py:14
  304.4 9.2 %collective-permute-start.36 = (bf16[16,1024]{1,0:T(8,128)(2,1)S(1)}, bf16[16,1024]{1,0:T(8,128)(2,1)S(1)}, u32[]{:S(2)}, u32[]{:S(2)}) collective-permute-start(bf16[16,1024]{1,0:T(8,128)(2,1)S(1)} %get-tuple-element.87), channel_id=1, source_target_pairs={{0,2},{1,3},{2,4},{3,5},{4,6},{5,7},{6,8},{7,9},{8,10},{9,11},{10,... | collective-permute-start | bytes 98312 | tf_op jit(solution)/shard_map/ppermute | solution.py:14
  329.6 18.8 %collective-permute-start.39 = (bf16[16,1024]{1,0:T(8,128)(2,1)S(1)}, bf16[16,1024]{1,0:T(8,128)(2,1)S(1)}, u32[]{:S(2)}, u32[]{:S(2)}) collective-permute-start(bf16[16,1024]{1,0:T(8,128)(2,1)S(1)} %get-tuple-element.85), channel_id=1, source_target_pairs={{0,1},{1,2},{2,3},{3,4},{4,5},{5,6},{6,7},{7,8},{8,9},{9,10},{10,1... | collective-permute-start | bytes 98312 | tf_op jit(solution)/shard_map/ppermute | solution.py:14
  332.2 16.2 %collective-permute-start.40 = (bf16[16,1024]{1,0:T(8,128)(2,1)S(1)}, bf16[16,1024]{1,0:T(8,128)(2,1)S(1)}, u32[]{:S(2)}, u32[]{:S(2)}) collective-permute-start(bf16[16,1024]{1,0:T(8,128)(2,1)S(1)} %get-tuple-element.84), channel_id=1, source_target_pairs={{1,0},{2,1},{3,2},{4,3},{5,4},{6,5},{7,6},{8,7},{9,8},{10,9},{11,1... | collective-permute-start | bytes 98312 | tf_op jit(solution)/shard_map/ppermute | solution.py:14
  339.2 9.2 %collective-permute-start.41 = (bf16[16,1024]{1,0:T(8,128)(2,1)S(1)}, bf16[16,1024]{1,0:T(8,128)(2,1)S(1)}, u32[]{:S(2)}, u32[]{:S(2)}) collective-permute-start(bf16[16,1024]{1,0:T(8,128)(2,1)S(1)} %get-tuple-element.83), channel_id=1, source_target_pairs={{0,2},{1,3},{2,4},{3,5},{4,6},{5,7},{6,8},{7,9},{8,10},{9,11},{10,... | collective-permute-start | bytes 98312 | tf_op jit(solution)/shard_map/ppermute | solution.py:14
  354.2 18.8 %collective-permute-start.43 = (bf16[16,1024]{1,0:T(8,128)(2,1)S(1)}, bf16[16,1024]{1,0:T(8,128)(2,1)S(1)}, u32[]{:S(2)}, u32[]{:S(2)}) collective-permute-start(bf16[16,1024]{1,0:T(8,128)(2,1)S(1)} %get-tuple-element.81), channel_id=1, source_target_pairs={{0,1},{1,2},{2,3},{3,4},{4,5},{5,6},{6,7},{7,8},{8,9},{9,10},{10,1... | collective-permute-start | bytes 98312 | tf_op jit(solution)/shard_map/ppermute | solution.py:14
  356.9 16.2 %collective-permute-start.44 = (bf16[16,1024]{1,0:T(8,128)(2,1)S(1)}, bf16[16,1024]{1,0:T(8,128)(2,1)S(1)}, u32[]{:S(2)}, u32[]{:S(2)}) collective-permute-start(bf16[16,1024]{1,0:T(8,128)(2,1)S(1)} %get-tuple-element.80), channel_id=1, source_target_pairs={{1,0},{2,1},{3,2},{4,3},{5,4},{6,5},{7,6},{8,7},{9,8},{10,9},{11,1... | collective-permute-start | bytes 98312 | tf_op jit(solution)/shard_map/ppermute | solution.py:14
  363.9 9.2 %collective-permute-start.45 = (bf16[16,1024]{1,0:T(8,128)(2,1)S(1)}, bf16[16,1024]{1,0:T(8,128)(2,1)S(1)}, u32[]{:S(2)}, u32[]{:S(2)}) collective-permute-start(bf16[16,1024]{1,0:T(8,128)(2,1)S(1)} %get-tuple-element.79), channel_id=1, source_target_pairs={{0,2},{1,3},{2,4},{3,5},{4,6},{5,7},{6,8},{7,9},{8,10},{9,11},{10,... | collective-permute-start | bytes 98312 | tf_op jit(solution)/shard_map/ppermute | solution.py:14
  378.9 18.8 %collective-permute-start.47 = (bf16[16,1024]{1,0:T(8,128)(2,1)S(1)}, bf16[16,1024]{1,0:T(8,128)(2,1)S(1)}, u32[]{:S(2)}, u32[]{:S(2)}) collective-permute-start(bf16[16,1024]{1,0:T(8,128)(2,1)S(1)} %get-tuple-element.77), channel_id=1, source_target_pairs={{0,1},{1,2},{2,3},{3,4},{4,5},{5,6},{6,7},{7,8},{8,9},{9,10},{10,1... | collective-permute-start | bytes 98312 | tf_op jit(solution)/shard_map/ppermute | solution.py:14
  381.6 16.2 %collective-permute-start.48 = (bf16[16,1024]{1,0:T(8,128)(2,1)S(1)}, bf16[16,1024]{1,0:T(8,128)(2,1)S(1)}, u32[]{:S(2)}, u32[]{:S(2)}) collective-permute-start(bf16[16,1024]{1,0:T(8,128)(2,1)S(1)} %get-tuple-element.76), channel_id=1, source_target_pairs={{1,0},{2,1},{3,2},{4,3},{5,4},{6,5},{7,6},{8,7},{9,8},{10,9},{11,1... | collective-permute-start | bytes 98312 | tf_op jit(solution)/shard_map/ppermute | solution.py:14
  388.5 9.2 %collective-permute-start.49 = (bf16[16,1024]{1,0:T(8,128)(2,1)S(1)}, bf16[16,1024]{1,0:T(8,128)(2,1)S(1)}, u32[]{:S(2)}, u32[]{:S(2)}) collective-permute-start(bf16[16,1024]{1,0:T(8,128)(2,1)S(1)} %get-tuple-element.75), channel_id=1, source_target_pairs={{0,2},{1,3},{2,4},{3,5},{4,6},{5,7},{6,8},{7,9},{8,10},{9,11},{10,... | collective-permute-start | bytes 98312 | tf_op jit(solution)/shard_map/ppermute | solution.py:14
  413.7 18.8 %collective-permute-start.52 = (bf16[16,1024]{1,0:T(8,128)(2,1)S(1)}, bf16[16,1024]{1,0:T(8,128)(2,1)S(1)}, u32[]{:S(2)}, u32[]{:S(2)}) collective-permute-start(bf16[16,1024]{1,0:T(8,128)(2,1)S(1)} %get-tuple-element.73), channel_id=1, source_target_pairs={{0,1},{1,2},{2,3},{3,4},{4,5},{5,6},{6,7},{7,8},{8,9},{9,10},{10,1... | collective-permute-start | bytes 98312 | tf_op jit(solution)/shard_map/ppermute | solution.py:14
  416.3 16.2 %collective-permute-start.53 = (bf16[16,1024]{1,0:T(8,128)(2,1)S(1)}, bf16[16,1024]{1,0:T(8,128)(2,1)S(1)}, u32[]{:S(2)}, u32[]{:S(2)}) collective-permute-start(bf16[16,1024]{1,0:T(8,128)(2,1)S(1)} %get-tuple-element.72), channel_id=1, source_target_pairs={{1,0},{2,1},{3,2},{4,3},{5,4},{6,5},{7,6},{8,7},{9,8},{10,9},{11,1... | collective-permute-start | bytes 98312 | tf_op jit(solution)/shard_map/ppermute | solution.py:14
  423.3 9.2 %collective-permute-start.54 = (bf16[16,1024]{1,0:T(8,128)(2,1)S(1)}, bf16[16,1024]{1,0:T(8,128)(2,1)S(1)}, u32[]{:S(2)}, u32[]{:S(2)}) collective-permute-start(bf16[16,1024]{1,0:T(8,128)(2,1)S(1)} %get-tuple-element.71), channel_id=1, source_target_pairs={{0,2},{1,3},{2,4},{3,5},{4,6},{5,7},{6,8},{7,9},{8,10},{9,11},{10,... | collective-permute-start | bytes 98312 | tf_op jit(solution)/shard_map/ppermute | solution.py:14
  438.3 19.1 %collective-permute-start.56 = (bf16[16,1024]{1,0:T(8,128)(2,1)S(1)}, bf16[16,1024]{1,0:T(8,128)(2,1)S(1)}, u32[]{:S(2)}, u32[]{:S(2)}) collective-permute-start(bf16[16,1024]{1,0:T(8,128)(2,1)S(1)} %get-tuple-element.69), channel_id=1, source_target_pairs={{0,1},{1,2},{2,3},{3,4},{4,5},{5,6},{6,7},{7,8},{8,9},{9,10},{10,1... | collective-permute-start | bytes 98312 | tf_op jit(solution)/shard_map/ppermute | solution.py:14
  441.1 16.4 %collective-permute-start.57 = (bf16[16,1024]{1,0:T(8,128)(2,1)S(1)}, bf16[16,1024]{1,0:T(8,128)(2,1)S(1)}, u32[]{:S(2)}, u32[]{:S(2)}) collective-permute-start(bf16[16,1024]{1,0:T(8,128)(2,1)S(1)} %get-tuple-element.68), channel_id=1, source_target_pairs={{1,0},{2,1},{3,2},{4,3},{5,4},{6,5},{7,6},{8,7},{9,8},{10,9},{11,1... | collective-permute-start | bytes 98312 | tf_op jit(solution)/shard_map/ppermute | solution.py:14
  448.0 9.4 %collective-permute-start.58 = (bf16[16,1024]{1,0:T(8,128)(2,1)S(1)}, bf16[16,1024]{1,0:T(8,128)(2,1)S(1)}, u32[]{:S(2)}, u32[]{:S(2)}) collective-permute-start(bf16[16,1024]{1,0:T(8,128)(2,1)S(1)} %get-tuple-element.67), channel_id=1, source_target_pairs={{0,2},{1,3},{2,4},{3,5},{4,6},{5,7},{6,8},{7,9},{8,10},{9,11},{10,... | collective-permute-start | bytes 98312 | tf_op jit(solution)/shard_map/ppermute | solution.py:14
  463.1 18.8 %collective-permute-start.60 = (bf16[16,1024]{1,0:T(8,128)(2,1)S(1)}, bf16[16,1024]{1,0:T(8,128)(2,1)S(1)}, u32[]{:S(2)}, u32[]{:S(2)}) collective-permute-start(bf16[16,1024]{1,0:T(8,128)(2,1)S(1)} %get-tuple-element.65), channel_id=1, source_target_pairs={{0,1},{1,2},{2,3},{3,4},{4,5},{5,6},{6,7},{7,8},{8,9},{9,10},{10,1... | collective-permute-start | bytes 98312 | tf_op jit(solution)/shard_map/ppermute | solution.py:14
  465.7 16.2 %collective-permute-start.61 = (bf16[16,1024]{1,0:T(8,128)(2,1)S(1)}, bf16[16,1024]{1,0:T(8,128)(2,1)S(1)}, u32[]{:S(2)}, u32[]{:S(2)}) collective-permute-start(bf16[16,1024]{1,0:T(8,128)(2,1)S(1)} %get-tuple-element.64), channel_id=1, source_target_pairs={{1,0},{2,1},{3,2},{4,3},{5,4},{6,5},{7,6},{8,7},{9,8},{10,9},{11,1... | collective-permute-start | bytes 98312 | tf_op jit(solution)/shard_map/ppermute | solution.py:14
  472.7 9.2 %collective-permute-start.62 = (bf16[16,1024]{1,0:T(8,128)(2,1)S(1)}, bf16[16,1024]{1,0:T(8,128)(2,1)S(1)}, u32[]{:S(2)}, u32[]{:S(2)}) collective-permute-start(bf16[16,1024]{1,0:T(8,128)(2,1)S(1)} %get-tuple-element.63), channel_id=1, source_target_pairs={{0,2},{1,3},{2,4},{3,5},{4,6},{5,7},{6,8},{7,9},{8,10},{9,11},{10,... | collective-permute-start | bytes 98312 | tf_op jit(solution)/shard_map/ppermute | solution.py:14
  497.8 18.8 %collective-permute-start.65 = (bf16[16,1024]{1,0:T(8,128)(2,1)S(1)}, bf16[16,1024]{1,0:T(8,128)(2,1)S(1)}, u32[]{:S(2)}, u32[]{:S(2)}) collective-permute-start(bf16[16,1024]{1,0:T(8,128)(2,1)S(1)} %get-tuple-element.61), channel_id=1, source_target_pairs={{0,1},{1,2},{2,3},{3,4},{4,5},{5,6},{6,7},{7,8},{8,9},{9,10},{10,1... | collective-permute-start | bytes 98312 | tf_op jit(solution)/shard_map/ppermute | solution.py:14
  500.5 16.2 %collective-permute-start.66 = (bf16[16,1024]{1,0:T(8,128)(2,1)S(1)}, bf16[16,1024]{1,0:T(8,128)(2,1)S(1)}, u32[]{:S(2)}, u32[]{:S(2)}) collective-permute-start(bf16[16,1024]{1,0:T(8,128)(2,1)S(1)} %get-tuple-element.60), channel_id=1, source_target_pairs={{1,0},{2,1},{3,2},{4,3},{5,4},{6,5},{7,6},{8,7},{9,8},{10,9},{11,1... | collective-permute-start | bytes 98312 | tf_op jit(solution)/shard_map/ppermute | solution.py:14
  507.4 9.2 %collective-permute-start.67 = (bf16[16,1024]{1,0:T(8,128)(2,1)S(1)}, bf16[16,1024]{1,0:T(8,128)(2,1)S(1)}, u32[]{:S(2)}, u32[]{:S(2)}) collective-permute-start(bf16[16,1024]{1,0:T(8,128)(2,1)S(1)} %get-tuple-element.59), channel_id=1, source_target_pairs={{0,2},{1,3},{2,4},{3,5},{4,6},{5,7},{6,8},{7,9},{8,10},{9,11},{10,... | collective-permute-start | bytes 98312 | tf_op jit(solution)/shard_map/ppermute | solution.py:14
  522.5 18.8 %collective-permute-start.69 = (bf16[16,1024]{1,0:T(8,128)(2,1)S(1)}, bf16[16,1024]{1,0:T(8,128)(2,1)S(1)}, u32[]{:S(2)}, u32[]{:S(2)}) collective-permute-start(bf16[16,1024]{1,0:T(8,128)(2,1)S(1)} %get-tuple-element.57), channel_id=1, source_target_pairs={{0,1},{1,2},{2,3},{3,4},{4,5},{5,6},{6,7},{7,8},{8,9},{9,10},{10,1... | collective-permute-start | bytes 98312 | tf_op jit(solution)/shard_map/ppermute | solution.py:14
  525.1 16.2 %collective-permute-start.70 = (bf16[16,1024]{1,0:T(8,128)(2,1)S(1)}, bf16[16,1024]{1,0:T(8,128)(2,1)S(1)}, u32[]{:S(2)}, u32[]{:S(2)}) collective-permute-start(bf16[16,1024]{1,0:T(8,128)(2,1)S(1)} %get-tuple-element.56), channel_id=1, source_target_pairs={{1,0},{2,1},{3,2},{4,3},{5,4},{6,5},{7,6},{8,7},{9,8},{10,9},{11,1... | collective-permute-start | bytes 98312 | tf_op jit(solution)/shard_map/ppermute | solution.py:14
  532.1 9.2 %collective-permute-start.71 = (bf16[16,1024]{1,0:T(8,128)(2,1)S(1)}, bf16[16,1024]{1,0:T(8,128)(2,1)S(1)}, u32[]{:S(2)}, u32[]{:S(2)}) collective-permute-start(bf16[16,1024]{1,0:T(8,128)(2,1)S(1)} %get-tuple-element.55), channel_id=1, source_target_pairs={{0,2},{1,3},{2,4},{3,5},{4,6},{5,7},{6,8},{7,9},{8,10},{9,11},{10,... | collective-permute-start | bytes 98312 | tf_op jit(solution)/shard_map/ppermute | solution.py:14
  547.1 18.8 %collective-permute-start.73 = (bf16[16,1024]{1,0:T(8,128)(2,1)S(1)}, bf16[16,1024]{1,0:T(8,128)(2,1)S(1)}, u32[]{:S(2)}, u32[]{:S(2)}) collective-permute-start(bf16[16,1024]{1,0:T(8,128)(2,1)S(1)} %get-tuple-element.53), channel_id=1, source_target_pairs={{0,1},{1,2},{2,3},{3,4},{4,5},{5,6},{6,7},{7,8},{8,9},{9,10},{10,1... | collective-permute-start | bytes 98312 | tf_op jit(solution)/shard_map/ppermute | solution.py:14
  549.8 16.2 %collective-permute-start.74 = (bf16[16,1024]{1,0:T(8,128)(2,1)S(1)}, bf16[16,1024]{1,0:T(8,128)(2,1)S(1)}, u32[]{:S(2)}, u32[]{:S(2)}) collective-permute-start(bf16[16,1024]{1,0:T(8,128)(2,1)S(1)} %get-tuple-element.52), channel_id=1, source_target_pairs={{1,0},{2,1},{3,2},{4,3},{5,4},{6,5},{7,6},{8,7},{9,8},{10,9},{11,1... | collective-permute-start | bytes 98312 | tf_op jit(solution)/shard_map/ppermute | solution.py:14
  556.8 9.2 %collective-permute-start.75 = (bf16[16,1024]{1,0:T(8,128)(2,1)S(1)}, bf16[16,1024]{1,0:T(8,128)(2,1)S(1)}, u32[]{:S(2)}, u32[]{:S(2)}) collective-permute-start(bf16[16,1024]{1,0:T(8,128)(2,1)S(1)} %get-tuple-element.51), channel_id=1, source_target_pairs={{0,2},{1,3},{2,4},{3,5},{4,6},{5,7},{6,8},{7,9},{8,10},{9,11},{10,... | collective-permute-start | bytes 98312 | tf_op jit(solution)/shard_map/ppermute | solution.py:14
  581.9 18.8 %collective-permute-start.78 = (bf16[16,1024]{1,0:T(8,128)(2,1)S(1)}, bf16[16,1024]{1,0:T(8,128)(2,1)S(1)}, u32[]{:S(2)}, u32[]{:S(2)}) collective-permute-start(bf16[16,1024]{1,0:T(8,128)(2,1)S(1)} %get-tuple-element.49), channel_id=1, source_target_pairs={{0,1},{1,2},{2,3},{3,4},{4,5},{5,6},{6,7},{7,8},{8,9},{9,10},{10,1... | collective-permute-start | bytes 98312 | tf_op jit(solution)/shard_map/ppermute | solution.py:14
  584.6 16.2 %collective-permute-start.79 = (bf16[16,1024]{1,0:T(8,128)(2,1)S(1)}, bf16[16,1024]{1,0:T(8,128)(2,1)S(1)}, u32[]{:S(2)}, u32[]{:S(2)}) collective-permute-start(bf16[16,1024]{1,0:T(8,128)(2,1)S(1)} %get-tuple-element.48), channel_id=1, source_target_pairs={{1,0},{2,1},{3,2},{4,3},{5,4},{6,5},{7,6},{8,7},{9,8},{10,9},{11,1... | collective-permute-start | bytes 98312 | tf_op jit(solution)/shard_map/ppermute | solution.py:14
  591.5 9.2 %collective-permute-start.80 = (bf16[16,1024]{1,0:T(8,128)(2,1)S(1)}, bf16[16,1024]{1,0:T(8,128)(2,1)S(1)}, u32[]{:S(2)}, u32[]{:S(2)}) collective-permute-start(bf16[16,1024]{1,0:T(8,128)(2,1)S(1)} %get-tuple-element.47), channel_id=1, source_target_pairs={{0,2},{1,3},{2,4},{3,5},{4,6},{5,7},{6,8},{7,9},{8,10},{9,11},{10,... | collective-permute-start | bytes 98312 | tf_op jit(solution)/shard_map/ppermute | solution.py:14
  606.6 18.8 %collective-permute-start.82 = (bf16[16,1024]{1,0:T(8,128)(2,1)S(1)}, bf16[16,1024]{1,0:T(8,128)(2,1)S(1)}, u32[]{:S(2)}, u32[]{:S(2)}) collective-permute-start(bf16[16,1024]{1,0:T(8,128)(2,1)S(1)} %get-tuple-element.45), channel_id=1, source_target_pairs={{0,1},{1,2},{2,3},{3,4},{4,5},{5,6},{6,7},{7,8},{8,9},{9,10},{10,1... | collective-permute-start | bytes 98312 | tf_op jit(solution)/shard_map/ppermute | solution.py:14
  609.2 16.2 %collective-permute-start.83 = (bf16[16,1024]{1,0:T(8,128)(2,1)S(1)}, bf16[16,1024]{1,0:T(8,128)(2,1)S(1)}, u32[]{:S(2)}, u32[]{:S(2)}) collective-permute-start(bf16[16,1024]{1,0:T(8,128)(2,1)S(1)} %get-tuple-element.44), channel_id=1, source_target_pairs={{1,0},{2,1},{3,2},{4,3},{5,4},{6,5},{7,6},{8,7},{9,8},{10,9},{11,1... | collective-permute-start | bytes 98312 | tf_op jit(solution)/shard_map/ppermute | solution.py:14
  616.2 9.2 %collective-permute-start.84 = (bf16[16,1024]{1,0:T(8,128)(2,1)S(1)}, bf16[16,1024]{1,0:T(8,128)(2,1)S(1)}, u32[]{:S(2)}, u32[]{:S(2)}) collective-permute-start(bf16[16,1024]{1,0:T(8,128)(2,1)S(1)} %get-tuple-element.43), channel_id=1, source_target_pairs={{0,2},{1,3},{2,4},{3,5},{4,6},{5,7},{6,8},{7,9},{8,10},{9,11},{10,... | collective-permute-start | bytes 98312 | tf_op jit(solution)/shard_map/ppermute | solution.py:14
  631.2 18.8 %collective-permute-start.86 = (bf16[16,1024]{1,0:T(8,128)(2,1)S(1)}, bf16[16,1024]{1,0:T(8,128)(2,1)S(1)}, u32[]{:S(2)}, u32[]{:S(2)}) collective-permute-start(bf16[16,1024]{1,0:T(8,128)(2,1)S(1)} %get-tuple-element.41), channel_id=1, source_target_pairs={{0,1},{1,2},{2,3},{3,4},{4,5},{5,6},{6,7},{7,8},{8,9},{9,10},{10,1... | collective-permute-start | bytes 98312 | tf_op jit(solution)/shard_map/ppermute | solution.py:14
  633.9 16.2 %collective-permute-start.87 = (bf16[16,1024]{1,0:T(8,128)(2,1)S(1)}, bf16[16,1024]{1,0:T(8,128)(2,1)S(1)}, u32[]{:S(2)}, u32[]{:S(2)}) collective-permute-start(bf16[16,1024]{1,0:T(8,128)(2,1)S(1)} %get-tuple-element.40), channel_id=1, source_target_pairs={{1,0},{2,1},{3,2},{4,3},{5,4},{6,5},{7,6},{8,7},{9,8},{10,9},{11,1... | collective-permute-start | bytes 98312 | tf_op jit(solution)/shard_map/ppermute | solution.py:14
  (33 other events, 383.1 us)
Sparse Core Ops, SparseCore 0:
  10.6 89.0 all-gather.1
where the time goes:
time: 666 us; the launch traced here: 662 us
  starting transfers between devices  403 us (61%)
  waiting for transfers between devices  111 us (17%)
  matrix products  70.6 us (11%)
  local copies, waits for them, and re-layouts  37.9 us (6%)
  between operations  23.7 us (4%)
  other arithmetic  15.4 us (2%)
    ppermute x90, starting transfers between devices, shifted(): lax.ppermute(value, axis, [(source, source + steps) for source in range(i...  403 us
    dot_general x21, matrix products, propagate(): jnp.dot(support.astype(jnp.bfloat16), weight, preferred_element_type=jnp....  60.8 us
    ppermute x90, waiting for transfers between devices, shifted(): lax.ppermute(value, axis, [(source, source + steps) for source in range(i...  58.7 us
    all_gather x1, waiting for transfers between devices, shards(): lax.all_gather(lax.dynamic_slice_in_dim(weights, weight_base, slot_count,...  52.8 us
    gather x21, local copies, waits for them, and re-layouts, propagate(): arrived.append(jnp.take(layer_table, past_rows, axis=0))  14.9 us
    gather x21, local copies, waits for them, and re-layouts, propagate(): picked = jnp.take(current, send_rows.reshape(-1), axis=0)  14.8 us
  transfers between devices with their start and end apart: 91, of which 27 were waited for; matrix products, arithmetic and copies ran while one was open for 3% of the time, Pallas kernels for 0%

commit v1 on v0

v1 whole, which is shorter than its diff:
```python
import jax
import jax.numpy as jnp
from jax import lax
from jax.sharding import PartitionSpec as P

ALPHA = 0.1
LAMBDA = 1.5
BF = jnp.bfloat16
F32 = jnp.float32


def dot(a, b):
    return jnp.dot(a, b, preferred_element_type=F32)


def dot_t(a, b):
    return lax.dot_general(a, b, (((0,), (0,)), ((), ())), preferred_element_type=F32)


def one_hot(ids, width):
    return (ids[:, None] == lax.broadcasted_iota(jnp.int32, (ids.shape[0], width), 1)).astype(BF)


def shards(features, weights, history, own_adj, side_adj, hist_adj, send_ids, hist_ids):
    segment_pos = lax.axis_index("segment")
    segment_count = lax.axis_size("segment")
    graph_count = lax.axis_size("graph")
    core = lax.axis_index("graph") % 2
    layers, wrows, width = weights.shape
    half = width // 2
    rows = own_adj.shape[2]
    edge = send_ids.shape[2]
    hsel = hist_ids.shape[1]
    kept = layers // segment_count

    def partner(value):
        return lax.ppermute(value, "graph", [(p, p ^ 1) for p in range(graph_count)])

    def chip_shift(value, step):
        low, high = max(0, -step), min(graph_count, graph_count - step)
        return lax.ppermute(value, "graph", [(p, p + step) for p in range(low, high)])

    def pick_batch(value):
        return lax.dynamic_index_in_dim(value, segment_pos, 0, keepdims=False)

    def mine_half(value):
        return jnp.where(core == 0, value[..., :half], value[..., half:])

    def other_half(value):
        return jnp.where(core == 0, value[..., half:], value[..., :half])

    def by_part(mine, theirs):
        return jnp.where(core == 0, mine, theirs), jnp.where(core == 0, theirs, mine)

    w_swapped = partner(other_half(weights))
    w_low, w_high = by_part(mine_half(weights), w_swapped)
    w_chip = jnp.concatenate([w_low, w_high], axis=1)
    groups = [[p for p in range(graph_count) if p % 2 == c] for c in range(2)]

    initial = lax.dynamic_slice_in_dim(features, segment_pos * rows, rows, 0)
    own = pick_batch(own_adj)
    side = pick_batch(side_adj).reshape(4 * edge, rows)
    hist = pick_batch(hist_adj)
    sids = pick_batch(send_ids).reshape(-1)
    hids = pick_batch(hist_ids)
    x0, x1 = by_part(mine_half(initial), partner(other_half(initial)))
    h0, h1 = by_part(mine_half(history), partner(other_half(history)))
    tables = jnp.concatenate([own, side, hist], axis=0)
    t0, t1 = by_part(tables, partner(tables))
    ids = jnp.concatenate([sids, hids])
    i0, i1 = by_part(ids, partner(ids))

    def split(t, i):
        own = t[:rows]
        side = [t[rows + k * edge : rows + (k + 1) * edge] for k in range(4)]
        hist = t[rows + 4 * edge :]
        send = [one_hot(i[k * edge : (k + 1) * edge], rows) for k in range(4)]
        look = one_hot(i[4 * edge :], history.shape[1])
        return own, side, hist, send, look

    own0, side0, hist0, send0, look0 = split(t0, i0)
    own1, side1, hist1, send1, look1 = split(t1, i1)
    q10 = dot_t(side1[0], send0[0]).astype(BF)
    q01 = dot_t(side0[1], send1[1]).astype(BF)
    near = jnp.concatenate(
        [jnp.concatenate([own0, q01], axis=1), jnp.concatenate([q10, own1], axis=1)], axis=0
    )
    zs = jnp.zeros_like(side0[0])
    far_t = jnp.concatenate(
        [
            jnp.concatenate([side0[0], side0[2], zs, side0[3], zs, zs], axis=0),
            jnp.concatenate([zs, zs, side1[2], zs, side1[1], side1[3]], axis=0),
        ],
        axis=1,
    )
    zp = jnp.zeros_like(send0[0])
    picker = jnp.concatenate(
        [
            jnp.concatenate([zp, send1[0]], axis=1),
            jnp.concatenate([send0[2], zp], axis=1),
            jnp.concatenate([zp, send1[2]], axis=1),
            jnp.concatenate([send0[3], zp], axis=1),
            jnp.concatenate([send0[1], zp], axis=1),
            jnp.concatenate([zp, send1[3]], axis=1),
        ],
        axis=0,
    )
    start = jnp.concatenate([x0, x1], axis=0)
    start32 = ALPHA * start.astype(F32)

    def past(layer):
        g0 = dot(look0, h0[layer]).astype(BF)
        g1 = dot(look1, h1[layer]).astype(BF)
        return jnp.concatenate([dot_t(hist0, g0), dot_t(hist1, g1)], axis=0)

    weight_parts = []
    for layer in range(0, layers, 2):
        shard = w_chip[layer : layer + 2].reshape(2, 2 * wrows, half)
        full = lax.all_gather(shard, "graph", axis=1, tiled=True, axis_index_groups=groups)
        weight_parts += [full[0], full[1]]

    current = start
    own_rows = []
    for layer in range(layers):
        strength = jnp.log(jnp.float32(LAMBDA / (layer + 1.0)) + 1.0)
        picked = dot(picker, current).astype(BF)
        before = chip_shift(picked[: 3 * edge], 2)
        after = chip_shift(picked[3 * edge :], -2)
        local = dot(near, current) + past(layer)
        arrived = jnp.concatenate([before, after], axis=0)
        support = (1.0 - ALPHA) * (local + dot_t(far_t, arrived)) + start32
        mine = support.astype(BF)
        theirs = partner(mine)
        left, right = by_part(mine, theirs)
        weight = weight_parts[layer]
        mixing = dot(left, weight[:half]) + dot(right, weight[half:])
        current = jax.nn.relu((1.0 - strength) * support + strength * mixing).astype(BF)
        own_rows.append(current)
    stacked = jnp.stack(own_rows).reshape(layers, 2, rows, half)
    to_keep = jnp.where(core == 0, stacked[:, 0], stacked[:, 1])
    to_send = jnp.where(core == 0, stacked[:, 1], stacked[:, 0])
    left, right = by_part(to_keep, partner(to_send))
    whole = jnp.concatenate([left, right], axis=2).reshape(segment_count, kept, rows, width)
    exchanged = lax.all_to_all(whole, "segment", 0, 0)
    return exchanged.transpose(1, 0, 2, 3).reshape(kept, segment_count * rows, width)


def solution(mesh):
    in_specs = (
        P("graph", None),
        P(None, "graph", None),
        P(None, "graph", None),
        P(None, "graph", None),
        P(None, None, "graph", None),
        P(None, "graph", None),
        P(None, None, "graph"),
        P(None, "graph"),
    )
    out_specs = P("segment", "graph", None)
    return jax.shard_map(shards, mesh=mesh, in_specs=in_specs, out_specs=out_specs, check_vma=False)
```

time: 666 us -> 414 us (0.62)
  the two profiles are of different devices: /device:TPU:34 before, /device:TPU:16 now
where the time goes in v1:
time: 414 us; the launch traced here: 412 us
  waiting for transfers between devices  203 us (49%)
  starting transfers between devices  97.6 us (24%)
  matrix products  50.2 us (12%)
  blocking collectives  30.7 us (7%)
  between operations  14.6 us (4%)
  other arithmetic  8.27 us (2%)
  local copies, waits for them, and re-layouts  6.97 us (2%)
    all_gather x4, waiting for transfers between devices, shards(): lax.all_gather(shard, 'graph', axis=1, tiled=True, axis_index_groups=groups)  186 us
    ppermute x16, starting transfers between devices, chip_shift(): lax.ppermute(value, 'graph', [(p, p + step) for p in range(low, high)])  69.6 us
    all_to_all x1, blocking collectives, shards(): exchanged = lax.all_to_all(whole, 'segment', 0, 0)  30.7 us
    ppermute x14, starting transfers between devices, partner(): lax.ppermute(value, 'graph', [(p, p ^ 1) for p in range(graph_count)])  27.9 us
    dot_general x26, matrix products, dot_t(): lax.dot_general(a, b, (((0,), (0,)), ((), ())), preferred_element_type=F32)  26.1 us
    dot_general x32, matrix products, dot(): return jnp.dot(a, b, preferred_element_type=F32)  24.1 us
    ppermute x16, waiting for transfers between devices, chip_shift(): lax.ppermute(value, 'graph', [(p, p + step) for p in range(low, high)])  11.8 us
  transfers between devices with their start and end apart: 34, of which 19 were waited for; matrix products, arithmetic and copies ran while one was open for 14% of the time, Pallas kernels for 0%

profile of v1, /device:TPU:16, one launch (start us, length us, event | category | flops | bytes accessed | tf_op | source)
XLA Modules:
  0.0 411.7 jit_solution(8164150229853594689)
XLA Ops:
  7.5 1.9 collective-permute-start.7
  14.2 2.1 collective-permute-start.3
  18.3 2.3 collective-permute-start
  22.2 2.1 collective-permute-start.1
  25.2 2.3 collective-permute-start.2
  31.1 4.3 %collective-permute-start.4 = (bf16[48,512]{1,0:T(8,128)(2,1)S(1)}, bf16[48,512]{1,0:T(8,128)(2,1)S(1)}, u32[]{:S(2)}, u32[]{:S(2)}) collective-permute-start(bf16[48,512]{1,0:T(8,128)(2,1)S(1)} %get-tuple-element.33), channel_id=1, source_target_pairs={{0,2},{1,3},{2,4},{3,5},{4,6},{5,7},{6,8},{7,9},{8,10},{9,11},{10,... | collective-permute-start | bytes 147464 | tf_op jit(solution)/shard_map/ppermute | solution.py:41
  35.4 8.5 %collective-permute-start.5 = (bf16[48,512]{1,0:T(8,128)(2,1)S(1)}, bf16[48,512]{1,0:T(8,128)(2,1)S(1)}, u32[]{:S(2)}, u32[]{:S(2)}) collective-permute-start(bf16[48,512]{1,0:T(8,128)(2,1)S(1)} %get-tuple-element.34), channel_id=1, source_target_pairs={{2,0},{3,1},{4,2},{5,3},{6,4},{7,5},{8,6},{9,7},{10,8},{11,9},{12,... | collective-permute-start | bytes 147464 | tf_op jit(solution)/shard_map/ppermute | solution.py:41
  44.0 1.6 collective-permute-done.5
  51.3 1.9 collective-permute-start.6
  55.3 45.0 %all-gather.5.cloned.1.call-done = bf16[2,1024,512]{2,1,0:T(8,128)(2,1)} async-done(((bf16[2,16,512]{2,1,0:T(8,128)(2,1)}), bf16[2,1024,512]{2,1,0:T(8,128)(2,1)}) %all-gather.5.cloned.1.call-update) | async-done | bytes 2097168 | tf_op jit(solution)/shard_map/all_gather | solution.py:119
  100.3 1.3 fusion.50
  101.7 1.4 maximum_convert_fusion.7
  103.3 2.6 collective-permute-start.8
  105.9 5.4 %collective-permute-start.9 = (bf16[48,512]{1,0:T(8,128)(2,1)S(1)}, bf16[48,512]{1,0:T(8,128)(2,1)S(1)}, u32[]{:S(2)}, u32[]{:S(2)}) collective-permute-start(bf16[48,512]{1,0:T(8,128)(2,1)S(1)} %get-tuple-element.32), channel_id=1, source_target_pairs={{2,0},{3,1},{4,2},{5,3},{6,4},{7,5},{8,6},{9,7},{10,8},{11,9},{12,... | collective-permute-start | bytes 147464 | tf_op jit(solution)/shard_map/ppermute | solution.py:41
  111.6 1.5 collective-permute-done.9
  113.3 1.9 collective-permute-start.10
  116.3 1.9 fusion.33
  118.9 1.3 fusion.49
  120.3 1.4 maximum_convert_fusion.6
  121.9 2.0 collective-permute-start.11
  123.9 6.3 %collective-permute-start.12 = (bf16[48,512]{1,0:T(8,128)(2,1)S(1)}, bf16[48,512]{1,0:T(8,128)(2,1)S(1)}, u32[]{:S(2)}, u32[]{:S(2)}) collective-permute-start(bf16[48,512]{1,0:T(8,128)(2,1)S(1)} %get-tuple-element.30), channel_id=1, source_target_pairs={{2,0},{3,1},{4,2},{5,3},{6,4},{7,5},{8,6},{9,7},{10,8},{11,9},{12,... | collective-permute-start | bytes 147464 | tf_op jit(solution)/shard_map/ppermute | solution.py:41
  132.2 1.9 collective-permute-start.13
  135.3 1.9 fusion.35
  137.2 46.5 %all-gather.7.cloned.1.call-done = bf16[2,1024,512]{2,1,0:T(8,128)(2,1)} async-done(((bf16[2,16,512]{2,1,0:T(8,128)(2,1)}), bf16[2,1024,512]{2,1,0:T(8,128)(2,1)}) %all-gather.7.cloned.1.call-update) | async-done | bytes 2097168 | tf_op jit(solution)/shard_map/all_gather | solution.py:119
  183.7 1.3 fusion.48
  185.1 1.4 maximum_convert_fusion.5
  186.7 2.5 collective-permute-start.14
  189.3 5.4 %collective-permute-start.15 = (bf16[48,512]{1,0:T(8,128)(2,1)S(1)}, bf16[48,512]{1,0:T(8,128)(2,1)S(1)}, u32[]{:S(2)}, u32[]{:S(2)}) collective-permute-start(bf16[48,512]{1,0:T(8,128)(2,1)S(1)} %get-tuple-element.28), channel_id=1, source_target_pairs={{2,0},{3,1},{4,2},{5,3},{6,4},{7,5},{8,6},{9,7},{10,8},{11,9},{12,... | collective-permute-start | bytes 147464 | tf_op jit(solution)/shard_map/ppermute | solution.py:41
  194.9 1.5 collective-permute-done.15
  196.7 1.9 collective-permute-start.16
  198.6 1.9 fusion.36
  200.6 2.0 fusion.37
  202.5 1.4 fusion.47
  204.0 1.4 maximum_convert_fusion.4
  205.6 2.0 collective-permute-start.17
  207.6 6.3 %collective-permute-start.18 = (bf16[48,512]{1,0:T(8,128)(2,1)S(1)}, bf16[48,512]{1,0:T(8,128)(2,1)S(1)}, u32[]{:S(2)}, u32[]{:S(2)}) collective-permute-start(bf16[48,512]{1,0:T(8,128)(2,1)S(1)} %get-tuple-element.26), channel_id=1, source_target_pairs={{2,0},{3,1},{4,2},{5,3},{6,4},{7,5},{8,6},{9,7},{10,8},{11,9},{12,... | collective-permute-start | bytes 147464 | tf_op jit(solution)/shard_map/ppermute | solution.py:41
  215.9 1.9 collective-permute-start.19
  217.9 1.9 fusion.38
  219.8 1.9 fusion.39
  221.7 45.4 %all-gather.9.cloned.1.call-done = bf16[2,1024,512]{2,1,0:T(8,128)(2,1)} async-done(((bf16[2,16,512]{2,1,0:T(8,128)(2,1)}), bf16[2,1024,512]{2,1,0:T(8,128)(2,1)}) %all-gather.9.cloned.1.call-update) | async-done | bytes 2097168 | tf_op jit(solution)/shard_map/all_gather | solution.py:119
  267.1 1.4 fusion.46
  268.6 1.4 maximum_convert_fusion.3
  270.3 2.5 collective-permute-start.20
  272.8 5.4 %collective-permute-start.21 = (bf16[48,512]{1,0:T(8,128)(2,1)S(1)}, bf16[48,512]{1,0:T(8,128)(2,1)S(1)}, u32[]{:S(2)}, u32[]{:S(2)}) collective-permute-start(bf16[48,512]{1,0:T(8,128)(2,1)S(1)} %get-tuple-element.24), channel_id=1, source_target_pairs={{2,0},{3,1},{4,2},{5,3},{6,4},{7,5},{8,6},{9,7},{10,8},{11,9},{12,... | collective-permute-start | bytes 147464 | tf_op jit(solution)/shard_map/ppermute | solution.py:41
  278.5 1.4 collective-permute-done.21
  281.1 1.9 collective-permute-start.22
  283.0 1.9 fusion.40
  285.0 1.5 fusion.45
  286.5 1.5 maximum_convert_fusion.2
  288.3 2.0 collective-permute-start.23
  290.3 6.4 %collective-permute-start.24 = (bf16[48,512]{1,0:T(8,128)(2,1)S(1)}, bf16[48,512]{1,0:T(8,128)(2,1)S(1)}, u32[]{:S(2)}, u32[]{:S(2)}) collective-permute-start(bf16[48,512]{1,0:T(8,128)(2,1)S(1)} %get-tuple-element.22), channel_id=1, source_target_pairs={{2,0},{3,1},{4,2},{5,3},{6,4},{7,5},{8,6},{9,7},{10,8},{11,9},{12,... | collective-permute-start | bytes 147464 | tf_op jit(solution)/shard_map/ppermute | solution.py:41
  299.6 1.9 collective-permute-start.25
  301.7 48.7 %all-gather.11.cloned.1.call-done = bf16[2,1024,512]{2,1,0:T(8,128)(2,1)} async-done(((bf16[2,16,512]{2,1,0:T(8,128)(2,1)}), bf16[2,1024,512]{2,1,0:T(8,128)(2,1)}) %all-gather.11.cloned.1.call-update) | async-done | bytes 2097168 | tf_op jit(solution)/shard_map/all_gather | solution.py:119
  350.4 1.4 fusion.44
  351.8 1.7 maximum_convert_fusion.1
  353.7 2.6 collective-permute-start.26
  356.3 5.4 %collective-permute-start.27 = (bf16[48,512]{1,0:T(8,128)(2,1)S(1)}, bf16[48,512]{1,0:T(8,128)(2,1)S(1)}, u32[]{:S(2)}, u32[]{:S(2)}) collective-permute-start(bf16[48,512]{1,0:T(8,128)(2,1)S(1)} %get-tuple-element.20), channel_id=1, source_target_pairs={{2,0},{3,1},{4,2},{5,3},{6,4},{7,5},{8,6},{9,7},{10,8},{11,9},{12,... | collective-permute-start | bytes 147464 | tf_op jit(solution)/shard_map/ppermute | solution.py:41
  362.0 1.4 collective-permute-done.27
  363.7 1.9 collective-permute-start.28
  365.7 1.4 collective-permute-done.28
  367.9 2.0 collective-permute-start.29
  370.0 2.5 collective-permute-done.29
  373.0 30.7 %all_to_all.5 = bf16[4,2,128,1024]{3,2,1,0:T(8,128)(2,1)S(1)} all-to-all(bf16[4,2,128,1024]{3,2,1,0:T(8,128)(2,1)S(1)} %bitcast.195), channel_id=1, replica_groups=mesh['segment'=4,'graph'=128] {'segment'}, dimensions={0} | all-to-all | bytes 4194304 | tf_op jit(solution)/shard_map/all_to_all | solution.py:144
  403.7 1.5 copy.63
  (255 shorter events, 37.0 us)
Async XLA Ops:
  6.5 93.8 %all-gather.5.cloned.1.call-start = ((), (), s32[]{:S(2)}) async-start(), calls=%async_computation.1 | async-start | bytes 2129920 | tf_op jit(solution)/shard_map/all_gather | solution.py:119
  7.5 3.1 collective-permute-start.7
  12.2 171.5 %all-gather.7.cloned.1.call-start = ((), (), s32[]{:S(2)}) async-start(), calls=%async_computation.2 | async-start | bytes 2129920 | tf_op jit(solution)/shard_map/all_gather | solution.py:119
  12.9 254.2 %all-gather.9.cloned.1.call-start = ((), (), s32[]{:S(2)}) async-start(), calls=%async_computation.3 | async-start | bytes 2129920 | tf_op jit(solution)/shard_map/all_gather | solution.py:119
  14.2 31.6 %collective-permute-start.3 = (bf16[8,64,512]{2,1,0:T(8,128)(2,1)S(1)}, bf16[8,64,512]{2,1,0:T(8,128)(2,1)}, u32[]{:S(2)}, u32[]{:S(2)}) collective-permute-start(bf16[8,64,512]{2,1,0:T(8,128)(2,1)S(1)} %broadcast_select_fusion.4), channel_id=1, source_target_pairs={{0,1},{1,0},{2,3},{3,2},{4,5},{5,4},{6,7},{7,6},{8,9},{9,8},{10,11... | collective-permute-start | bytes 1572872 | tf_op jit(solution)/shard_map/ppermute | solution.py:37
  16.5 29.4 %copy-start.5 = (bf16[8,64,1024]{2,1,0:T(8,128)(2,1)S(1)}, bf16[8,64,1024]{2,1,0:T(8,128)(2,1)}, u32[]{:S(2)}) copy-start(bf16[8,64,1024]{2,1,0:T(8,128)(2,1)} %param.10) | copy-start | bytes 3145732
  18.3 10.1 %collective-permute-start = (bf16[256,128]{0,1:T(8,128)(2,1)S(1)}, bf16[256,128]{0,1:T(8,128)(2,1)S(1)}, u32[]{:S(2)}, u32[]{:S(2)}) collective-permute-start(bf16[256,128]{0,1:T(8,128)(2,1)S(1)} %pad_maximum_fusion.2), channel_id=1, source_target_pairs={{0,1},{1,0},{2,3},{3,2},{4,5},{5,4},{6,7},{7,6},{8,9},{9,8},{10,11... | collective-permute-start | bytes 196616 | tf_op jit(solution)/shard_map/ppermute | solution.py:37
  22.2 5.4 %collective-permute-start.1 = (s32[128]{0:T(128)S(1)}, s32[128]{0:T(128)S(1)}, u32[]{:S(2)}, u32[]{:S(2)}) collective-permute-start(s32[128]{0:T(128)S(1)} %pad_add_fusion), channel_id=1, source_target_pairs={{0,1},{1,0},{2,3},{3,2},{4,5},{5,4},{6,7},{7,6},{8,9},{9,8},{10,11... | collective-permute-start | bytes 1544 | tf_op jit(solution)/shard_map/ppermute | solution.py:37
  25.2 4.6 %collective-permute-start.2 = (bf16[128,512]{1,0:T(8,128)(2,1)S(1)}, bf16[128,512]{1,0:T(8,128)(2,1)S(1)}, u32[]{:S(2)}, u32[]{:S(2)}) collective-permute-start(bf16[128,512]{1,0:T(8,128)(2,1)S(1)} %broadcast_select_fusion.8), channel_id=1, source_target_pairs={{0,1},{1,0},{2,3},{3,2},{4,5},{5,4},{6,7},{7,6},{8,9},{9,8},{10,11... | collective-permute-start | bytes 393224 | tf_op jit(solution)/shard_map/ppermute | solution.py:37
  28.0 322.4 %all-gather.11.cloned.1.call-start = ((), (), s32[]{:S(2)}) async-start(), calls=%async_computation.4 | async-start | bytes 2129920 | tf_op jit(solution)/shard_map/all_gather | solution.py:119
  28.4 15.4 %copy-start.34 = (pred[96,256]{1,0:T(8,128)(4,1)}, pred[96,256]{1,0:T(8,128)(4,1)S(1)}, u32[]{:S(2)}) copy-start(pred[96,256]{1,0:T(8,128)(4,1)S(1)} %constant_dynamic-update-slice_fusion.10) | copy-start | bytes 73732
  29.4 248.8 %copy-start.6 = (bf16[128,128]{0,1:T(8,128)(2,1)}, bf16[128,128]{0,1:T(8,128)(2,1)S(1)}, u32[]{:S(2)}) copy-start(bf16[128,128]{0,1:T(8,128)(2,1)S(1)} %convolution_convert_fusion.24) | copy-start | bytes 98308
  29.7 248.5 %copy-start.9 = (bf16[128,128]{0,1:T(8,128)(2,1)}, bf16[128,128]{0,1:T(8,128)(2,1)S(1)}, u32[]{:S(2)}) copy-start(bf16[128,128]{0,1:T(8,128)(2,1)S(1)} %convolution_convert_fusion.25) | copy-start | bytes 98308
  29.8 16.0 %copy-start.28 = (bf16[96,128]{1,0:T(8,128)(2,1)}, bf16[96,128]{1,0:T(8,128)(2,1)S(1)}, u32[]{:S(2)}) copy-start(bf16[96,128]{1,0:T(8,128)(2,1)S(1)} %constant_dynamic-update-slice_fusion) | copy-start | bytes 73732
  31.1 12.9 %collective-permute-start.4 = (bf16[48,512]{1,0:T(8,128)(2,1)S(1)}, bf16[48,512]{1,0:T(8,128)(2,1)S(1)}, u32[]{:S(2)}, u32[]{:S(2)}) collective-permute-start(bf16[48,512]{1,0:T(8,128)(2,1)S(1)} %get-tuple-element.33), channel_id=1, source_target_pairs={{0,2},{1,3},{2,4},{3,5},{4,6},{5,7},{6,8},{7,9},{8,10},{9,11},{10,... | collective-permute-start | bytes 147464 | tf_op jit(solution)/shard_map/ppermute | solution.py:41
  35.4 10.2 %collective-permute-start.5 = (bf16[48,512]{1,0:T(8,128)(2,1)S(1)}, bf16[48,512]{1,0:T(8,128)(2,1)S(1)}, u32[]{:S(2)}, u32[]{:S(2)}) collective-permute-start(bf16[48,512]{1,0:T(8,128)(2,1)S(1)} %get-tuple-element.34), channel_id=1, source_target_pairs={{2,0},{3,1},{4,2},{5,3},{6,4},{7,5},{8,6},{9,7},{10,8},{11,9},{12,... | collective-permute-start | bytes 147464 | tf_op jit(solution)/shard_map/ppermute | solution.py:41
  43.9 234.4 %copy-start.12 = (bf16[128,128]{0,1:T(8,128)(2,1)}, bf16[128,128]{0,1:T(8,128)(2,1)S(1)}, u32[]{:S(2)}) copy-start(bf16[128,128]{0,1:T(8,128)(2,1)S(1)} %slice.424) | copy-start | bytes 98308
  43.9 234.4 %copy-start.15 = (bf16[128,128]{0,1:T(8,128)(2,1)}, bf16[128,128]{0,1:T(8,128)(2,1)S(1)}, u32[]{:S(2)}) copy-start(bf16[128,128]{0,1:T(8,128)(2,1)S(1)} %slice.427) | copy-start | bytes 98308
  47.0 87.1 %copy-start.20 = (bf16[8,64,512]{2,1,0:T(8,128)(2,1)}, bf16[8,64,512]{2,1,0:T(8,128)(2,1)S(1)}, u32[]{:S(2)}) copy-start(bf16[8,64,512]{2,1,0:T(8,128)(2,1)S(1)} %get-tuple-element.8) | copy-start | bytes 1572868
  51.3 4.1 collective-permute-start.6
  54.2 48.9 %copy-start.35 = (pred[96,256]{1,0:T(8,128)(4,1)S(1)}, pred[96,256]{1,0:T(8,128)(4,1)}, u32[]{:S(2)}) copy-start(pred[96,256]{1,0:T(8,128)(4,1)} %copy-done.34) | copy-start | bytes 73732
  55.3 46.3 %copy-start.54 = (bf16[256,512]{1,0:T(8,128)(2,1)}, bf16[256,512]{1,0:T(8,128)(2,1)S(1)}, u32[]{:S(2)}) copy-start(bf16[256,512]{1,0:T(8,128)(2,1)S(1)} %collective-permute-done.6) | copy-start | bytes 786436
  103.3 8.2 %collective-permute-start.8 = (bf16[48,512]{1,0:T(8,128)(2,1)S(1)}, bf16[48,512]{1,0:T(8,128)(2,1)S(1)}, u32[]{:S(2)}, u32[]{:S(2)}) collective-permute-start(bf16[48,512]{1,0:T(8,128)(2,1)S(1)} %get-tuple-element.31), channel_id=1, source_target_pairs={{0,2},{1,3},{2,4},{3,5},{4,6},{5,7},{6,8},{7,9},{8,10},{9,11},{10,... | collective-permute-start | bytes 147464 | tf_op jit(solution)/shard_map/ppermute | solution.py:41
  105.9 7.1 %collective-permute-start.9 = (bf16[48,512]{1,0:T(8,128)(2,1)S(1)}, bf16[48,512]{1,0:T(8,128)(2,1)S(1)}, u32[]{:S(2)}, u32[]{:S(2)}) collective-permute-start(bf16[48,512]{1,0:T(8,128)(2,1)S(1)} %get-tuple-element.32), channel_id=1, source_target_pairs={{2,0},{3,1},{4,2},{5,3},{6,4},{7,5},{8,6},{9,7},{10,8},{11,9},{12,... | collective-permute-start | bytes 147464 | tf_op jit(solution)/shard_map/ppermute | solution.py:41
  113.3 4.9 %collective-permute-start.10 = (bf16[256,512]{1,0:T(8,128)(2,1)S(1)}, bf16[256,512]{1,0:T(8,128)(2,1)S(1)}, u32[]{:S(2)}, u32[]{:S(2)}) collective-permute-start(bf16[256,512]{1,0:T(8,128)(2,1)S(1)} %get-tuple-element.53), channel_id=1, source_target_pairs={{0,1},{1,0},{2,3},{3,2},{4,5},{5,4},{6,7},{7,6},{8,9},{9,8},{10,11... | collective-permute-start | bytes 786440 | tf_op jit(solution)/shard_map/ppermute | solution.py:37
  120.3 11.7 %copy-start.45 = (f32[128,512]{1,0:T(8,128)S(1)}, f32[128,512]{1,0:T(8,128)}, u32[]{:S(2)}) copy-start(f32[128,512]{1,0:T(8,128)} %fusion.29) | copy-start | bytes 786436
  120.3 11.7 %copy-start.48 = (f32[128,512]{1,0:T(8,128)S(1)}, f32[128,512]{1,0:T(8,128)}, u32[]{:S(2)}) copy-start(f32[128,512]{1,0:T(8,128)} %fusion.30) | copy-start | bytes 786436
  121.9 8.8 %collective-permute-start.11 = (bf16[48,512]{1,0:T(8,128)(2,1)S(1)}, bf16[48,512]{1,0:T(8,128)(2,1)S(1)}, u32[]{:S(2)}, u32[]{:S(2)}) collective-permute-start(bf16[48,512]{1,0:T(8,128)(2,1)S(1)} %get-tuple-element.29), channel_id=1, source_target_pairs={{0,2},{1,3},{2,4},{3,5},{4,6},{5,7},{6,8},{7,9},{8,10},{9,11},{10,... | collective-permute-start | bytes 147464 | tf_op jit(solution)/shard_map/ppermute | solution.py:41
  123.9 8.0 %collective-permute-start.12 = (bf16[48,512]{1,0:T(8,128)(2,1)S(1)}, bf16[48,512]{1,0:T(8,128)(2,1)S(1)}, u32[]{:S(2)}, u32[]{:S(2)}) collective-permute-start(bf16[48,512]{1,0:T(8,128)(2,1)S(1)} %get-tuple-element.30), channel_id=1, source_target_pairs={{2,0},{3,1},{4,2},{5,3},{6,4},{7,5},{8,6},{9,7},{10,8},{11,9},{12,... | collective-permute-start | bytes 147464 | tf_op jit(solution)/shard_map/ppermute | solution.py:41
  132.2 51.5 %collective-permute-start.13 = (bf16[256,512]{1,0:T(8,128)(2,1)S(1)}, bf16[256,512]{1,0:T(8,128)(2,1)S(1)}, u32[]{:S(2)}, u32[]{:S(2)}) collective-permute-start(bf16[256,512]{1,0:T(8,128)(2,1)S(1)} %get-tuple-element.55), channel_id=1, source_target_pairs={{0,1},{1,0},{2,3},{3,2},{4,5},{5,4},{6,7},{7,6},{8,9},{9,8},{10,11... | collective-permute-start | bytes 786440 | tf_op jit(solution)/shard_map/ppermute | solution.py:37
  186.7 8.2 %collective-permute-start.14 = (bf16[48,512]{1,0:T(8,128)(2,1)S(1)}, bf16[48,512]{1,0:T(8,128)(2,1)S(1)}, u32[]{:S(2)}, u32[]{:S(2)}) collective-permute-start(bf16[48,512]{1,0:T(8,128)(2,1)S(1)} %get-tuple-element.27), channel_id=1, source_target_pairs={{0,2},{1,3},{2,4},{3,5},{4,6},{5,7},{6,8},{7,9},{8,10},{9,11},{10,... | collective-permute-start | bytes 147464 | tf_op jit(solution)/shard_map/ppermute | solution.py:41
  189.3 7.1 %collective-permute-start.15 = (bf16[48,512]{1,0:T(8,128)(2,1)S(1)}, bf16[48,512]{1,0:T(8,128)(2,1)S(1)}, u32[]{:S(2)}, u32[]{:S(2)}) collective-permute-start(bf16[48,512]{1,0:T(8,128)(2,1)S(1)} %get-tuple-element.28), channel_id=1, source_target_pairs={{2,0},{3,1},{4,2},{5,3},{6,4},{7,5},{8,6},{9,7},{10,8},{11,9},{12,... | collective-permute-start | bytes 147464 | tf_op jit(solution)/shard_map/ppermute | solution.py:41
  196.7 5.8 %collective-permute-start.16 = (bf16[256,512]{1,0:T(8,128)(2,1)S(1)}, bf16[256,512]{1,0:T(8,128)(2,1)S(1)}, u32[]{:S(2)}, u32[]{:S(2)}) collective-permute-start(bf16[256,512]{1,0:T(8,128)(2,1)S(1)} %get-tuple-element.57), channel_id=1, source_target_pairs={{0,1},{1,0},{2,3},{3,2},{4,5},{5,4},{6,7},{7,6},{8,9},{9,8},{10,11... | collective-permute-start | bytes 786440 | tf_op jit(solution)/shard_map/ppermute | solution.py:37
  203.9 11.7 %copy-start.43 = (f32[128,512]{1,0:T(8,128)S(1)}, f32[128,512]{1,0:T(8,128)}, u32[]{:S(2)}) copy-start(f32[128,512]{1,0:T(8,128)} %fusion.33) | copy-start | bytes 786436
  204.0 11.7 %copy-start.50 = (f32[128,512]{1,0:T(8,128)S(1)}, f32[128,512]{1,0:T(8,128)}, u32[]{:S(2)}) copy-start(f32[128,512]{1,0:T(8,128)} %fusion.34) | copy-start | bytes 786436
  205.4 16.3 %copy-start.1 = (bf16[256,512]{1,0:T(8,128)(2,1)}, bf16[256,512]{1,0:T(8,128)(2,1)S(1)}, u32[]{:S(2)}) copy-start(bf16[256,512]{1,0:T(8,128)(2,1)S(1)} %maximum_convert_fusion.4) | copy-start | bytes 786436
  205.6 8.9 %collective-permute-start.17 = (bf16[48,512]{1,0:T(8,128)(2,1)S(1)}, bf16[48,512]{1,0:T(8,128)(2,1)S(1)}, u32[]{:S(2)}, u32[]{:S(2)}) collective-permute-start(bf16[48,512]{1,0:T(8,128)(2,1)S(1)} %get-tuple-element.25), channel_id=1, source_target_pairs={{0,2},{1,3},{2,4},{3,5},{4,6},{5,7},{6,8},{7,9},{8,10},{9,11},{10,... | collective-permute-start | bytes 147464 | tf_op jit(solution)/shard_map/ppermute | solution.py:41
  207.6 8.0 %collective-permute-start.18 = (bf16[48,512]{1,0:T(8,128)(2,1)S(1)}, bf16[48,512]{1,0:T(8,128)(2,1)S(1)}, u32[]{:S(2)}, u32[]{:S(2)}) collective-permute-start(bf16[48,512]{1,0:T(8,128)(2,1)S(1)} %get-tuple-element.26), channel_id=1, source_target_pairs={{2,0},{3,1},{4,2},{5,3},{6,4},{7,5},{8,6},{9,7},{10,8},{11,9},{12,... | collective-permute-start | bytes 147464 | tf_op jit(solution)/shard_map/ppermute | solution.py:41
  215.9 51.2 %collective-permute-start.19 = (bf16[256,512]{1,0:T(8,128)(2,1)S(1)}, bf16[256,512]{1,0:T(8,128)(2,1)S(1)}, u32[]{:S(2)}, u32[]{:S(2)}) collective-permute-start(bf16[256,512]{1,0:T(8,128)(2,1)S(1)} %get-tuple-element.59), channel_id=1, source_target_pairs={{0,1},{1,0},{2,3},{3,2},{4,5},{5,4},{6,7},{7,6},{8,9},{9,8},{10,11... | collective-permute-start | bytes 786440 | tf_op jit(solution)/shard_map/ppermute | solution.py:37
  270.3 8.3 %collective-permute-start.20 = (bf16[48,512]{1,0:T(8,128)(2,1)S(1)}, bf16[48,512]{1,0:T(8,128)(2,1)S(1)}, u32[]{:S(2)}, u32[]{:S(2)}) collective-permute-start(bf16[48,512]{1,0:T(8,128)(2,1)S(1)} %get-tuple-element.23), channel_id=1, source_target_pairs={{0,2},{1,3},{2,4},{3,5},{4,6},{5,7},{6,8},{7,9},{8,10},{9,11},{10,... | collective-permute-start | bytes 147464 | tf_op jit(solution)/shard_map/ppermute | solution.py:41
  272.8 7.1 %collective-permute-start.21 = (bf16[48,512]{1,0:T(8,128)(2,1)S(1)}, bf16[48,512]{1,0:T(8,128)(2,1)S(1)}, u32[]{:S(2)}, u32[]{:S(2)}) collective-permute-start(bf16[48,512]{1,0:T(8,128)(2,1)S(1)} %get-tuple-element.24), channel_id=1, source_target_pairs={{2,0},{3,1},{4,2},{5,3},{6,4},{7,5},{8,6},{9,7},{10,8},{11,9},{12,... | collective-permute-start | bytes 147464 | tf_op jit(solution)/shard_map/ppermute | solution.py:41
  281.1 3.9 collective-permute-start.22
  285.0 11.8 %copy-start.7 = (bf16[128,128]{0,1:T(8,128)(2,1)S(1)}, bf16[128,128]{0,1:T(8,128)(2,1)}, u32[]{:S(2)}) copy-start(bf16[128,128]{0,1:T(8,128)(2,1)} %copy-done.6) | copy-start | bytes 98308
  285.0 11.8 %copy-start.10 = (bf16[128,128]{0,1:T(8,128)(2,1)S(1)}, bf16[128,128]{0,1:T(8,128)(2,1)}, u32[]{:S(2)}) copy-start(bf16[128,128]{0,1:T(8,128)(2,1)} %copy-done.9) | copy-start | bytes 98308
  285.0 11.8 %copy-start.13 = (bf16[128,128]{0,1:T(8,128)(2,1)S(1)}, bf16[128,128]{0,1:T(8,128)(2,1)}, u32[]{:S(2)}) copy-start(bf16[128,128]{0,1:T(8,128)(2,1)} %copy-done.12) | copy-start | bytes 98308
  285.0 11.8 %copy-start.16 = (bf16[128,128]{0,1:T(8,128)(2,1)S(1)}, bf16[128,128]{0,1:T(8,128)(2,1)}, u32[]{:S(2)}) copy-start(bf16[128,128]{0,1:T(8,128)(2,1)} %copy-done.15) | copy-start | bytes 98308
  286.5 12.0 %copy-start.26 = (bf16[96,128]{1,0:T(8,128)(2,1)S(1)}, bf16[96,128]{1,0:T(8,128)(2,1)}, u32[]{:S(2)}) copy-start(bf16[96,128]{1,0:T(8,128)(2,1)} %copy-done.22) | copy-start | bytes 73732
  286.5 12.0 %copy-start.32 = (bf16[96,128]{1,0:T(8,128)(2,1)S(1)}, bf16[96,128]{1,0:T(8,128)(2,1)}, u32[]{:S(2)}) copy-start(bf16[96,128]{1,0:T(8,128)(2,1)} %copy-done.28) | copy-start | bytes 73732
  286.5 12.0 %copy-start.40 = (f32[128,512]{1,0:T(8,128)S(1)}, f32[128,512]{1,0:T(8,128)}, u32[]{:S(2)}) copy-start(f32[128,512]{1,0:T(8,128)} %fusion.37) | copy-start | bytes 786436
  286.5 11.9 %copy-start.46 = (f32[128,512]{1,0:T(8,128)S(1)}, f32[128,512]{1,0:T(8,128)}, u32[]{:S(2)}) copy-start(f32[128,512]{1,0:T(8,128)} %fusion.38) | copy-start | bytes 786436
  288.1 13.5 %copy-start.3 = (bf16[256,512]{1,0:T(8,128)(2,1)}, bf16[256,512]{1,0:T(8,128)(2,1)S(1)}, u32[]{:S(2)}) copy-start(bf16[256,512]{1,0:T(8,128)(2,1)S(1)} %maximum_convert_fusion.2) | copy-start | bytes 786436
  288.3 8.9 %collective-permute-start.23 = (bf16[48,512]{1,0:T(8,128)(2,1)S(1)}, bf16[48,512]{1,0:T(8,128)(2,1)S(1)}, u32[]{:S(2)}, u32[]{:S(2)}) collective-permute-start(bf16[48,512]{1,0:T(8,128)(2,1)S(1)} %get-tuple-element.21), channel_id=1, source_target_pairs={{0,2},{1,3},{2,4},{3,5},{4,6},{5,7},{6,8},{7,9},{8,10},{9,11},{10,... | collective-permute-start | bytes 147464 | tf_op jit(solution)/shard_map/ppermute | solution.py:41
  290.3 8.2 %collective-permute-start.24 = (bf16[48,512]{1,0:T(8,128)(2,1)S(1)}, bf16[48,512]{1,0:T(8,128)(2,1)S(1)}, u32[]{:S(2)}, u32[]{:S(2)}) collective-permute-start(bf16[48,512]{1,0:T(8,128)(2,1)S(1)} %get-tuple-element.22), channel_id=1, source_target_pairs={{2,0},{3,1},{4,2},{5,3},{6,4},{7,5},{8,6},{9,7},{10,8},{11,9},{12,... | collective-permute-start | bytes 147464 | tf_op jit(solution)/shard_map/ppermute | solution.py:41
  299.6 50.7 %collective-permute-start.25 = (bf16[256,512]{1,0:T(8,128)(2,1)}, bf16[256,512]{1,0:T(8,128)(2,1)}, u32[]{:S(2)}, u32[]{:S(2)}) collective-permute-start(bf16[256,512]{1,0:T(8,128)(2,1)} %get-tuple-element.63), channel_id=1, source_target_pairs={{0,1},{1,0},{2,3},{3,2},{4,5},{5,4},{6,7},{7,6},{8,9},{9,8},{10,11... | collective-permute-start | bytes 786440 | tf_op jit(solution)/shard_map/ppermute | solution.py:37
  301.6 51.9 %copy-start.38 = (pred[96,256]{1,0:T(8,128)(4,1)S(1)}, pred[96,256]{1,0:T(8,128)(4,1)}, u32[]{:S(2)}) copy-start(pred[96,256]{1,0:T(8,128)(4,1)} %copy-done.34) | copy-start | bytes 73732
  301.6 60.0 %copy-start.8 = (bf16[128,128]{0,1:T(8,128)(2,1)S(1)}, bf16[128,128]{0,1:T(8,128)(2,1)}, u32[]{:S(2)}) copy-start(bf16[128,128]{0,1:T(8,128)(2,1)} %copy-done.6) | copy-start | bytes 98308
  301.7 60.0 %copy-start.11 = (bf16[128,128]{0,1:T(8,128)(2,1)S(1)}, bf16[128,128]{0,1:T(8,128)(2,1)}, u32[]{:S(2)}) copy-start(bf16[128,128]{0,1:T(8,128)(2,1)} %copy-done.9) | copy-start | bytes 98308
  301.7 60.0 %copy-start.14 = (bf16[128,128]{0,1:T(8,128)(2,1)S(1)}, bf16[128,128]{0,1:T(8,128)(2,1)}, u32[]{:S(2)}) copy-start(bf16[128,128]{0,1:T(8,128)(2,1)} %copy-done.12) | copy-start | bytes 98308
  301.7 60.0 %copy-start.17 = (bf16[128,128]{0,1:T(8,128)(2,1)S(1)}, bf16[128,128]{0,1:T(8,128)(2,1)}, u32[]{:S(2)}) copy-start(bf16[128,128]{0,1:T(8,128)(2,1)} %copy-done.15) | copy-start | bytes 98308
  353.5 12.2 %copy-start.4 = (bf16[256,512]{1,0:T(8,128)(2,1)S(1)}, bf16[256,512]{1,0:T(8,128)(2,1)}, u32[]{:S(2)}) copy-start(bf16[256,512]{1,0:T(8,128)(2,1)} %copy-done.3) | copy-start | bytes 786436
  353.7 8.3 %collective-permute-start.26 = (bf16[48,512]{1,0:T(8,128)(2,1)S(1)}, bf16[48,512]{1,0:T(8,128)(2,1)S(1)}, u32[]{:S(2)}, u32[]{:S(2)}) collective-permute-start(bf16[48,512]{1,0:T(8,128)(2,1)S(1)} %get-tuple-element.19), channel_id=1, source_target_pairs={{0,2},{1,3},{2,4},{3,5},{4,6},{5,7},{6,8},{7,9},{8,10},{9,11},{10,... | collective-permute-start | bytes 147464 | tf_op jit(solution)/shard_map/ppermute | solution.py:41
  356.3 7.1 %collective-permute-start.27 = (bf16[48,512]{1,0:T(8,128)(2,1)S(1)}, bf16[48,512]{1,0:T(8,128)(2,1)S(1)}, u32[]{:S(2)}, u32[]{:S(2)}) collective-permute-start(bf16[48,512]{1,0:T(8,128)(2,1)S(1)} %get-tuple-element.20), channel_id=1, source_target_pairs={{2,0},{3,1},{4,2},{5,3},{6,4},{7,5},{8,6},{9,7},{10,8},{11,9},{12,... | collective-permute-start | bytes 147464 | tf_op jit(solution)/shard_map/ppermute | solution.py:41
  363.7 3.4 collective-permute-start.28
  367.9 4.6 %collective-permute-start.29 = (bf16[8,128,512]{2,1,0:T(8,128)(2,1)S(1)}, bf16[8,128,512]{2,1,0:T(8,128)(2,1)S(1)}, u32[]{:S(2)}, u32[]{:S(2)}) collective-permute-start(bf16[8,128,512]{2,1,0:T(8,128)(2,1)S(1)} %fusion.41), channel_id=1, source_target_pairs={{0,1},{1,0},{2,3},{3,2},{4,5},{5,4},{6,7},{7,6},{8,9},{9,8},{10,11... | collective-permute-start | bytes 3145736 | tf_op jit(solution)/shard_map/ppermute | solution.py:37
  (27 other events, 231.6 us)
Sparse Core Ops, SparseCore 0:
  12.3 87.9 all-gather.4
  103.4 80.2 all-gather.6
  186.8 80.3 all-gather.8
  270.0 80.2 all-gather.10

commit v2 on v1

v2 whole, which is shorter than its diff:
```python
import jax
import jax.numpy as jnp
from jax import lax
from jax.sharding import PartitionSpec as P

ALPHA = 0.1
LAMBDA = 1.5
BF = jnp.bfloat16
F32 = jnp.float32


def dot(a, b):
    return jnp.dot(a, b, preferred_element_type=F32)


def dot_t(a, b):
    return lax.dot_general(a, b, (((0,), (0,)), ((), ())), preferred_element_type=F32)


def one_hot(ids, width):
    return (ids[:, None] == lax.broadcasted_iota(jnp.int32, (ids.shape[0], width), 1)).astype(BF)


def shards(features, weights, history, own_adj, side_adj, hist_adj, send_ids, hist_ids):
    segment_pos = lax.axis_index("segment")
    segment_count = lax.axis_size("segment")
    graph_count = lax.axis_size("graph")
    core = lax.axis_index("graph") % 2
    chip_odd = (lax.axis_index("graph") // 2) % 2
    layers, _, width = weights.shape
    rows = own_adj.shape[2]
    edge = send_ids.shape[2]
    kept = layers // segment_count
    resident = lax.all_gather(weights, "graph", axis=1, tiled=True)

    def partner(value):
        return lax.ppermute(value, "graph", [(p, p ^ 1) for p in range(graph_count)])

    def exchange(value, first):
        pairs = []
        for p in range(first, graph_count - first - 2, 4):
            for c in range(2):
                pairs += [(p + c, p + c + 2), (p + c + 2, p + c)]
        return lax.ppermute(value, "graph", pairs)

    def pick_batch(value):
        return lax.dynamic_index_in_dim(value, segment_pos, 0, keepdims=False)

    def by_part(mine, theirs):
        return jnp.where(core == 0, mine, theirs), jnp.where(core == 0, theirs, mine)

    initial = lax.dynamic_slice_in_dim(features, segment_pos * rows, rows, 0)
    own = pick_batch(own_adj)
    side = pick_batch(side_adj).reshape(4 * edge, rows)
    hist = pick_batch(hist_adj)
    sids = pick_batch(send_ids).reshape(-1)
    hids = pick_batch(hist_ids)
    tables = jnp.concatenate([own, side, hist], axis=0)
    ids = jnp.concatenate([sids, hids])
    i0, i1 = by_part(ids, partner(ids))
    t0, t1 = by_part(tables, partner(tables))
    x0, x1 = by_part(initial, partner(initial))

    looked = jax.vmap(lambda t: dot(one_hot(hids, t.shape[0]), t).astype(BF))(history)
    g0, g1 = by_part(looked, partner(looked))

    def split(t, i):
        own = t[:rows]
        side = [t[rows + k * edge : rows + (k + 1) * edge] for k in range(4)]
        hist = t[rows + 4 * edge :]
        send = [one_hot(i[k * edge : (k + 1) * edge], rows) for k in range(4)]
        return own, side, hist, send

    own0, side0, hist0, send0 = split(t0, i0)
    own1, side1, hist1, send1 = split(t1, i1)
    q10 = dot_t(side1[0], send0[0]).astype(BF)
    q01 = dot_t(side0[1], send1[1]).astype(BF)
    near = jnp.concatenate(
        [jnp.concatenate([own0, q01], axis=1), jnp.concatenate([q10, own1], axis=1)], axis=0
    )
    zs = jnp.zeros_like(side0[0])
    from_before = jnp.concatenate(
        [
            jnp.concatenate([side0[0], side0[2], zs], axis=0),
            jnp.concatenate([zs, zs, side1[2]], axis=0),
        ],
        axis=1,
    )
    from_after = jnp.concatenate(
        [
            jnp.concatenate([side0[3], zs, zs], axis=0),
            jnp.concatenate([zs, side1[1], side1[3]], axis=0),
        ],
        axis=1,
    )
    to_after = jnp.concatenate(
        [
            jnp.concatenate([zs, send1[0]], axis=1),
            jnp.concatenate([send0[2], zs], axis=1),
            jnp.concatenate([zs, send1[2]], axis=1),
        ],
        axis=0,
    )
    to_before = jnp.concatenate(
        [
            jnp.concatenate([send0[3], zs], axis=1),
            jnp.concatenate([send0[1], zs], axis=1),
            jnp.concatenate([zs, send1[3]], axis=1),
        ],
        axis=0,
    )
    far_a = jnp.where(chip_odd == 0, from_after, from_before)
    far_b = jnp.where(chip_odd == 0, from_before, from_after)
    pick_a = jnp.where(chip_odd == 0, to_after, to_before)
    pick_b = jnp.where(chip_odd == 0, to_before, to_after)
    zh = jnp.zeros_like(hist0)
    hist_t = jnp.concatenate(
        [jnp.concatenate([hist0, zh], axis=1), jnp.concatenate([zh, hist1], axis=1)], axis=0
    )
    looked = jnp.concatenate([g0, g1], axis=1)
    start = jnp.concatenate([x0, x1], axis=0)

    current = start
    own_rows = []
    for layer in range(layers):
        strength = jnp.log(jnp.float32(LAMBDA / (layer + 1.0)) + 1.0)
        got_a = exchange(dot(pick_a, current).astype(BF), 0)
        got_b = exchange(dot(pick_b, current).astype(BF), 2)
        local = dot(near, current) + dot_t(hist_t, looked[layer])
        total = local + dot_t(far_a, got_a) + dot_t(far_b, got_b)
        support = (1.0 - ALPHA) * total + ALPHA * start.astype(F32)
        mixing = dot(support.astype(BF), resident[layer])
        current = jax.nn.relu((1.0 - strength) * support + strength * mixing).astype(BF)
        own_rows.append(lax.dynamic_slice_in_dim(current, core * rows, rows, 0))
    whole = jnp.stack(own_rows).reshape(segment_count, kept, rows, width)
    exchanged = lax.all_to_all(whole, "segment", 0, 0)
    return exchanged.transpose(1, 0, 2, 3).reshape(kept, segment_count * rows, width)


def solution(mesh):
    in_specs = (
        P("graph", None),
        P(None, "graph", None),
        P(None, "graph", None),
        P(None, "graph", None),
        P(None, None, "graph", None),
        P(None, "graph", None),
        P(None, None, "graph"),
        P(None, "graph"),
    )
    out_specs = P("segment", "graph", None)
    return jax.shard_map(shards, mesh=mesh, in_specs=in_specs, out_specs=out_specs, check_vma=False)
```

time: 414 us -> 254 us (0.61)
  the two profiles are of different devices: /device:TPU:16 before, /device:TPU:32 now
where the time goes in v2:
time: 254 us; the launch traced here: 253 us
  waiting for transfers between devices  104 us (41%)
  starting transfers between devices  66.9 us (26%)
  matrix products  35.9 us (14%)
  blocking collectives  21.4 us (8%)
  between operations  14.1 us (6%)
  local copies, waits for them, and re-layouts  7.57 us (3%)
  other arithmetic  3.38 us (1%)
    all_gather x1, waiting for transfers between devices, shards(): resident = lax.all_gather(weights, 'graph', axis=1, tiled=True)  68.9 us
    ppermute x16, starting transfers between devices, exchange(): return lax.ppermute(value, 'graph', pairs)  58.2 us
    ppermute x16, waiting for transfers between devices, exchange(): return lax.ppermute(value, 'graph', pairs)  34 us
    dot_general x33, matrix products, dot(): return jnp.dot(a, b, preferred_element_type=F32)  27.5 us
    all_to_all x1, blocking collectives, shards(): exchanged = lax.all_to_all(whole, 'segment', 0, 0)  21.4 us
    ppermute x4, starting transfers between devices, partner(): lax.ppermute(value, 'graph', [(p, p ^ 1) for p in range(graph_count)])  8.64 us
    dot_general x26, matrix products, dot_t(): lax.dot_general(a, b, (((0,), (0,)), ((), ())), preferred_element_type=F32)  8.4 us
  transfers between devices with their start and end apart: 21, of which 17 were waited for; matrix products, arithmetic and copies ran while one was open for 7% of the time, Pallas kernels for 0%

profile of v2, /device:TPU:32, one launch (start us, length us, event | category | flops | bytes accessed | tf_op | source)
XLA Modules:
  0.0 252.8 jit_solution(157648303293373457)
XLA Ops:
  6.5 0.7 all-gather.2.cloned.1.call-update
  7.3 0.7 constant_dynamic-slice_fusion.2
  8.0 0.7 fusion.95
  8.8 1.9 collective-permute-start.1
  10.7 1.0 constant_dynamic-slice_fusion
  11.7 2.4 collective-permute-start.2
  14.1 0.7 constant_dynamic-slice_fusion.3
  15.0 0.7 constant_dynamic-slice_fusion.4
  15.8 0.8 constant_dynamic-slice_fusion.5
  16.8 1.9 collective-permute-start
  18.7 0.5 fusion.8
  19.2 2.4 collective-permute-start.3
  23.7 1.1 broadcast_select_fusion.3
  25.1 10.8 %collective-permute-start.5 = (bf16[48,1024]{1,0:T(8,128)(2,1)S(1)}, bf16[48,1024]{1,0:T(8,128)(2,1)S(1)}, u32[]{:S(2)}, u32[]{:S(2)}) collective-permute-start(bf16[48,1024]{1,0:T(8,128)(2,1)S(1)} %convolution_convert_fusion.15), channel_id=1, source_target_pairs={{2,4},{4,2},{3,5},{5,3},{6,8},{8,6},{7,9},{9,7},{10,12},{12,10},{1... | collective-permute-start | bytes 294920 | tf_op jit(solution)/shard_map/ppermute | solution.py:44
  36.1 1.9 collective-permute-start.4
  38.1 1.0 collective-permute-done.5
  39.4 3.6 %collective-permute-done.4 = bf16[48,1024]{1,0:T(8,128)(2,1)S(1)} collective-permute-done((bf16[48,1024]{1,0:T(8,128)(2,1)S(1)}, bf16[48,1024]{1,0:T(8,128)(2,1)S(1)}, u32[]{:S(2)}, u32[]{:S(2)}) %collective-permute-start.4) | collective-permute-done | bytes 98336 | tf_op jit(solution)/shard_map/ppermute | solution.py:44
  43.3 1.4 broadcast_select_fusion
  45.0 1.4 fusion.19
  46.5 68.9 %all-gather.2.cloned.1.call-done = bf16[8,1024,1024]{2,1,0:T(8,128)(2,1)} async-done(((bf16[8,8,1024]{2,1,0:T(8,128)(2,1)}), bf16[8,1024,1024]{2,1,0:T(8,128)(2,1)}) %all-gather.2.cloned.1.call-update) | async-done | bytes 16777232 | tf_op jit(solution)/shard_map/all_gather | solution.py:34
  115.3 3.1 %maximum_convert_fusion.6 = bf16[256,1024]{1,0:T(8,128)(2,1)S(1)} fusion(f32[256,1024]{1,0:T(8,128)} %fusion.19, bf16[8,1024,1024]{2,1,0:T(8,128)(2,1)} %all-gather.2.cloned.1.call-done), kind=kOutput, calls=%fused_computation.103 | convolution fusion | flops 538443776 | bytes 4718592 | tf_op jit(solution)/shard_map/dot_general | solution.py:13
  119.2 4.4 %collective-permute-start.7 = (bf16[48,1024]{1,0:T(8,128)(2,1)S(1)}, bf16[48,1024]{1,0:T(8,128)(2,1)S(1)}, u32[]{:S(2)}, u32[]{:S(2)}) collective-permute-start(bf16[48,1024]{1,0:T(8,128)(2,1)S(1)} %convolution_convert_fusion.13), channel_id=1, source_target_pairs={{2,4},{4,2},{3,5},{5,3},{6,8},{8,6},{7,9},{9,7},{10,12},{12,10},{1... | collective-permute-start | bytes 294920 | tf_op jit(solution)/shard_map/ppermute | solution.py:44
  123.9 1.9 collective-permute-start.6
  125.8 3.5 %collective-permute-done.7 = bf16[48,1024]{1,0:T(8,128)(2,1)S(1)} collective-permute-done((bf16[48,1024]{1,0:T(8,128)(2,1)S(1)}, bf16[48,1024]{1,0:T(8,128)(2,1)S(1)}, u32[]{:S(2)}, u32[]{:S(2)}) %collective-permute-start.7) | collective-permute-done | bytes 98336 | tf_op jit(solution)/shard_map/ppermute | solution.py:44
  129.7 0.7 collective-permute-done.6
  130.4 0.4 fusion.21
  130.8 2.4 maximum_convert_fusion.5
  134.0 4.8 %collective-permute-start.9 = (bf16[48,1024]{1,0:T(8,128)(2,1)S(1)}, bf16[48,1024]{1,0:T(8,128)(2,1)S(1)}, u32[]{:S(2)}, u32[]{:S(2)}) collective-permute-start(bf16[48,1024]{1,0:T(8,128)(2,1)S(1)} %convolution_convert_fusion.11), channel_id=1, source_target_pairs={{2,4},{4,2},{3,5},{5,3},{6,8},{8,6},{7,9},{9,7},{10,12},{12,10},{1... | collective-permute-start | bytes 294920 | tf_op jit(solution)/shard_map/ppermute | solution.py:44
  139.1 1.9 collective-permute-start.8
  141.1 2.7 %collective-permute-done.9 = bf16[48,1024]{1,0:T(8,128)(2,1)S(1)} collective-permute-done((bf16[48,1024]{1,0:T(8,128)(2,1)S(1)}, bf16[48,1024]{1,0:T(8,128)(2,1)S(1)}, u32[]{:S(2)}, u32[]{:S(2)}) %collective-permute-start.9) | collective-permute-done | bytes 98336 | tf_op jit(solution)/shard_map/ppermute | solution.py:44
  144.1 1.5 collective-permute-done.8
  145.6 0.4 fusion.23
  146.0 2.4 maximum_convert_fusion.4
  149.2 4.3 %collective-permute-start.11 = (bf16[48,1024]{1,0:T(8,128)(2,1)S(1)}, bf16[48,1024]{1,0:T(8,128)(2,1)S(1)}, u32[]{:S(2)}, u32[]{:S(2)}) collective-permute-start(bf16[48,1024]{1,0:T(8,128)(2,1)S(1)} %convolution_convert_fusion.9), channel_id=1, source_target_pairs={{2,4},{4,2},{3,5},{5,3},{6,8},{8,6},{7,9},{9,7},{10,12},{12,10},{1... | collective-permute-start | bytes 294920 | tf_op jit(solution)/shard_map/ppermute | solution.py:44
  153.8 1.9 collective-permute-start.10
  155.8 3.2 %collective-permute-done.11 = bf16[48,1024]{1,0:T(8,128)(2,1)S(1)} collective-permute-done((bf16[48,1024]{1,0:T(8,128)(2,1)S(1)}, bf16[48,1024]{1,0:T(8,128)(2,1)S(1)}, u32[]{:S(2)}, u32[]{:S(2)}) %collective-permute-start.11) | collective-permute-done | bytes 98336 | tf_op jit(solution)/shard_map/ppermute | solution.py:44
  159.3 1.0 collective-permute-done.10
  160.4 0.4 fusion.25
  160.7 2.4 maximum_convert_fusion.3
  163.9 4.8 %collective-permute-start.13 = (bf16[48,1024]{1,0:T(8,128)(2,1)S(1)}, bf16[48,1024]{1,0:T(8,128)(2,1)S(1)}, u32[]{:S(2)}, u32[]{:S(2)}) collective-permute-start(bf16[48,1024]{1,0:T(8,128)(2,1)S(1)} %convolution_convert_fusion.7), channel_id=1, source_target_pairs={{2,4},{4,2},{3,5},{5,3},{6,8},{8,6},{7,9},{9,7},{10,12},{12,10},{1... | collective-permute-start | bytes 294920 | tf_op jit(solution)/shard_map/ppermute | solution.py:44
  169.1 1.9 collective-permute-start.12
  171.0 2.7 %collective-permute-done.13 = bf16[48,1024]{1,0:T(8,128)(2,1)S(1)} collective-permute-done((bf16[48,1024]{1,0:T(8,128)(2,1)S(1)}, bf16[48,1024]{1,0:T(8,128)(2,1)S(1)}, u32[]{:S(2)}, u32[]{:S(2)}) %collective-permute-start.13) | collective-permute-done | bytes 98336 | tf_op jit(solution)/shard_map/ppermute | solution.py:44
  174.1 1.5 collective-permute-done.12
  175.6 0.4 fusion.27
  175.9 2.4 maximum_convert_fusion.2
  179.1 4.3 %collective-permute-start.15 = (bf16[48,1024]{1,0:T(8,128)(2,1)S(1)}, bf16[48,1024]{1,0:T(8,128)(2,1)S(1)}, u32[]{:S(2)}, u32[]{:S(2)}) collective-permute-start(bf16[48,1024]{1,0:T(8,128)(2,1)S(1)} %convolution_convert_fusion.5), channel_id=1, source_target_pairs={{2,4},{4,2},{3,5},{5,3},{6,8},{8,6},{7,9},{9,7},{10,12},{12,10},{1... | collective-permute-start | bytes 294920 | tf_op jit(solution)/shard_map/ppermute | solution.py:44
  183.8 2.1 collective-permute-start.14
  185.9 3.0 %collective-permute-done.15 = bf16[48,1024]{1,0:T(8,128)(2,1)S(1)} collective-permute-done((bf16[48,1024]{1,0:T(8,128)(2,1)S(1)}, bf16[48,1024]{1,0:T(8,128)(2,1)S(1)}, u32[]{:S(2)}, u32[]{:S(2)}) %collective-permute-start.15) | collective-permute-done | bytes 98336 | tf_op jit(solution)/shard_map/ppermute | solution.py:44
  189.3 1.0 collective-permute-done.14
  190.7 2.4 maximum_convert_fusion.1
  193.8 4.8 %collective-permute-start.17 = (bf16[48,1024]{1,0:T(8,128)(2,1)S(1)}, bf16[48,1024]{1,0:T(8,128)(2,1)S(1)}, u32[]{:S(2)}, u32[]{:S(2)}) collective-permute-start(bf16[48,1024]{1,0:T(8,128)(2,1)S(1)} %convolution_convert_fusion.3), channel_id=1, source_target_pairs={{2,4},{4,2},{3,5},{5,3},{6,8},{8,6},{7,9},{9,7},{10,12},{12,10},{1... | collective-permute-start | bytes 294920 | tf_op jit(solution)/shard_map/ppermute | solution.py:44
  199.0 1.9 collective-permute-start.16
  201.0 2.7 %collective-permute-done.17 = bf16[48,1024]{1,0:T(8,128)(2,1)S(1)} collective-permute-done((bf16[48,1024]{1,0:T(8,128)(2,1)S(1)}, bf16[48,1024]{1,0:T(8,128)(2,1)S(1)}, u32[]{:S(2)}, u32[]{:S(2)}) %collective-permute-start.17) | collective-permute-done | bytes 98336 | tf_op jit(solution)/shard_map/ppermute | solution.py:44
  204.0 1.5 collective-permute-done.16
  205.5 0.4 fusion.31
  205.9 2.4 maximum_convert_fusion
  209.1 4.3 %collective-permute-start.19 = (bf16[48,1024]{1,0:T(8,128)(2,1)S(1)}, bf16[48,1024]{1,0:T(8,128)(2,1)S(1)}, u32[]{:S(2)}, u32[]{:S(2)}) collective-permute-start(bf16[48,1024]{1,0:T(8,128)(2,1)S(1)} %convolution_convert_fusion.1), channel_id=1, source_target_pairs={{2,4},{4,2},{3,5},{5,3},{6,8},{8,6},{7,9},{9,7},{10,12},{12,10},{1... | collective-permute-start | bytes 294920 | tf_op jit(solution)/shard_map/ppermute | solution.py:44
  213.7 1.9 collective-permute-start.18
  215.7 3.2 %collective-permute-done.19 = bf16[48,1024]{1,0:T(8,128)(2,1)S(1)} collective-permute-done((bf16[48,1024]{1,0:T(8,128)(2,1)S(1)}, bf16[48,1024]{1,0:T(8,128)(2,1)S(1)}, u32[]{:S(2)}, u32[]{:S(2)}) %collective-permute-start.19) | collective-permute-done | bytes 98336 | tf_op jit(solution)/shard_map/ppermute | solution.py:44
  219.2 1.0 collective-permute-done.18
  220.2 0.4 fusion.33
  220.6 2.3 fusion
  223.0 21.4 %all_to_all.5 = bf16[4,2,128,1024]{3,2,1,0:T(8,128)(2,1)S(1)} all-to-all(bf16[4,2,128,1024]{3,2,1,0:T(8,128)(2,1)S(1)} %bitcast.146), channel_id=1, replica_groups=mesh['segment'=4,'graph'=128] {'segment'}, dimensions={0} | all-to-all | bytes 4194304 | tf_op jit(solution)/shard_map/all_to_all | solution.py:136
  244.4 1.5 copy.28
  (91 shorter events, 14.2 us)
Async XLA Ops:
  6.5 12.2 %copy-start = (bf16[8,64,1024]{2,1,0:T(8,128)(2,1)S(1)}, bf16[8,64,1024]{2,1,0:T(8,128)(2,1)}, u32[]{:S(2)}) copy-start(bf16[8,64,1024]{2,1,0:T(8,128)(2,1)} %param.10) | copy-start | bytes 3145732
  6.5 108.8 %all-gather.2.cloned.1.call-start = ((), (), s32[]{:S(2)}) async-start(), calls=%async_computation.1 | async-start | bytes 16908288 | tf_op jit(solution)/shard_map/all_gather | solution.py:34
  8.8 12.9 %collective-permute-start.1 = (s32[128]{0:T(128)S(1)}, s32[128]{0:T(128)S(1)}, u32[]{:S(2)}, u32[]{:S(2)}) collective-permute-start(s32[128]{0:T(128)S(1)} %pad_add_fusion.4), channel_id=1, source_target_pairs={{0,1},{1,0},{2,3},{3,2},{4,5},{5,4},{6,7},{7,6},{8,9},{9,8},{10,11... | collective-permute-start | bytes 1544 | tf_op jit(solution)/shard_map/ppermute | solution.py:37
  11.7 12.1 %collective-permute-start.2 = (bf16[128,1024]{1,0:T(8,128)(2,1)S(1)}, bf16[128,1024]{1,0:T(8,128)(2,1)S(1)}, u32[]{:S(2)}, u32[]{:S(2)}) collective-permute-start(bf16[128,1024]{1,0:T(8,128)(2,1)S(1)} %constant_dynamic-slice_fusion), channel_id=1, source_target_pairs={{0,1},{1,0},{2,3},{3,2},{4,5},{5,4},{6,7},{7,6},{8,9},{9,8},{10,11... | collective-permute-start | bytes 786440 | tf_op jit(solution)/shard_map/ppermute | solution.py:37
  16.8 5.5 %collective-permute-start = (bf16[256,128]{0,1:T(8,128)(2,1)S(1)}, bf16[256,128]{0,1:T(8,128)(2,1)S(1)}, u32[]{:S(2)}, u32[]{:S(2)}) collective-permute-start(bf16[256,128]{0,1:T(8,128)(2,1)S(1)} %pad_maximum_fusion.2), channel_id=1, source_target_pairs={{0,1},{1,0},{2,3},{3,2},{4,5},{5,4},{6,7},{7,6},{8,9},{9,8},{10,11... | collective-permute-start | bytes 196616 | tf_op jit(solution)/shard_map/ppermute | solution.py:37
  19.2 16.9 %copy-start.2 = (bf16[8,64,1024]{2,1,0:T(8,128)(2,1)}, bf16[8,64,1024]{2,1,0:T(8,128)(2,1)S(1)}, u32[]{:S(2)}) copy-start(bf16[8,64,1024]{2,1,0:T(8,128)(2,1)S(1)} %fusion.8) | copy-start | bytes 3145732
  19.2 24.1 %collective-permute-start.3 = (bf16[8,64,1024]{2,1,0:T(8,128)(2,1)S(1)}, bf16[8,64,1024]{2,1,0:T(8,128)(2,1)}, u32[]{:S(2)}, u32[]{:S(2)}) collective-permute-start(bf16[8,64,1024]{2,1,0:T(8,128)(2,1)S(1)} %fusion.8), channel_id=1, source_target_pairs={{0,1},{1,0},{2,3},{3,2},{4,5},{5,4},{6,7},{7,6},{8,9},{9,8},{10,11... | collective-permute-start | bytes 3145736 | tf_op jit(solution)/shard_map/ppermute | solution.py:37
  25.1 14.0 %collective-permute-start.5 = (bf16[48,1024]{1,0:T(8,128)(2,1)S(1)}, bf16[48,1024]{1,0:T(8,128)(2,1)S(1)}, u32[]{:S(2)}, u32[]{:S(2)}) collective-permute-start(bf16[48,1024]{1,0:T(8,128)(2,1)S(1)} %convolution_convert_fusion.15), channel_id=1, source_target_pairs={{2,4},{4,2},{3,5},{5,3},{6,8},{8,6},{7,9},{9,7},{10,12},{12,10},{1... | collective-permute-start | bytes 294920 | tf_op jit(solution)/shard_map/ppermute | solution.py:44
  36.1 6.9 %collective-permute-start.4 = (bf16[48,1024]{1,0:T(8,128)(2,1)S(1)}, bf16[48,1024]{1,0:T(8,128)(2,1)S(1)}, u32[]{:S(2)}, u32[]{:S(2)}) collective-permute-start(bf16[48,1024]{1,0:T(8,128)(2,1)S(1)} %convolution_convert_fusion.16), channel_id=1, source_target_pairs={{0,2},{2,0},{1,3},{3,1},{4,6},{6,4},{5,7},{7,5},{8,10},{10,8},{9,1... | collective-permute-start | bytes 294920 | tf_op jit(solution)/shard_map/ppermute | solution.py:44
  38.1 5.3 %copy-start.3 = (bf16[8,64,1024]{2,1,0:T(8,128)(2,1)S(1)}, bf16[8,64,1024]{2,1,0:T(8,128)(2,1)}, u32[]{:S(2)}) copy-start(bf16[8,64,1024]{2,1,0:T(8,128)(2,1)} %copy-done.2) | copy-start | bytes 3145732
  119.2 10.2 %collective-permute-start.7 = (bf16[48,1024]{1,0:T(8,128)(2,1)S(1)}, bf16[48,1024]{1,0:T(8,128)(2,1)S(1)}, u32[]{:S(2)}, u32[]{:S(2)}) collective-permute-start(bf16[48,1024]{1,0:T(8,128)(2,1)S(1)} %convolution_convert_fusion.13), channel_id=1, source_target_pairs={{2,4},{4,2},{3,5},{5,3},{6,8},{8,6},{7,9},{9,7},{10,12},{12,10},{1... | collective-permute-start | bytes 294920 | tf_op jit(solution)/shard_map/ppermute | solution.py:44
  123.9 6.5 %collective-permute-start.6 = (bf16[48,1024]{1,0:T(8,128)(2,1)S(1)}, bf16[48,1024]{1,0:T(8,128)(2,1)S(1)}, u32[]{:S(2)}, u32[]{:S(2)}) collective-permute-start(bf16[48,1024]{1,0:T(8,128)(2,1)S(1)} %convolution_convert_fusion.14), channel_id=1, source_target_pairs={{0,2},{2,0},{1,3},{3,1},{4,6},{6,4},{5,7},{7,5},{8,10},{10,8},{9,1... | collective-permute-start | bytes 294920 | tf_op jit(solution)/shard_map/ppermute | solution.py:44
  134.0 9.8 %collective-permute-start.9 = (bf16[48,1024]{1,0:T(8,128)(2,1)S(1)}, bf16[48,1024]{1,0:T(8,128)(2,1)S(1)}, u32[]{:S(2)}, u32[]{:S(2)}) collective-permute-start(bf16[48,1024]{1,0:T(8,128)(2,1)S(1)} %convolution_convert_fusion.11), channel_id=1, source_target_pairs={{2,4},{4,2},{3,5},{5,3},{6,8},{8,6},{7,9},{9,7},{10,12},{12,10},{1... | collective-permute-start | bytes 294920 | tf_op jit(solution)/shard_map/ppermute | solution.py:44
  139.1 6.5 %collective-permute-start.8 = (bf16[48,1024]{1,0:T(8,128)(2,1)S(1)}, bf16[48,1024]{1,0:T(8,128)(2,1)S(1)}, u32[]{:S(2)}, u32[]{:S(2)}) collective-permute-start(bf16[48,1024]{1,0:T(8,128)(2,1)S(1)} %convolution_convert_fusion.12), channel_id=1, source_target_pairs={{0,2},{2,0},{1,3},{3,1},{4,6},{6,4},{5,7},{7,5},{8,10},{10,8},{9,1... | collective-permute-start | bytes 294920 | tf_op jit(solution)/shard_map/ppermute | solution.py:44
  149.2 9.8 %collective-permute-start.11 = (bf16[48,1024]{1,0:T(8,128)(2,1)S(1)}, bf16[48,1024]{1,0:T(8,128)(2,1)S(1)}, u32[]{:S(2)}, u32[]{:S(2)}) collective-permute-start(bf16[48,1024]{1,0:T(8,128)(2,1)S(1)} %convolution_convert_fusion.9), channel_id=1, source_target_pairs={{2,4},{4,2},{3,5},{5,3},{6,8},{8,6},{7,9},{9,7},{10,12},{12,10},{1... | collective-permute-start | bytes 294920 | tf_op jit(solution)/shard_map/ppermute | solution.py:44
  153.8 6.5 %collective-permute-start.10 = (bf16[48,1024]{1,0:T(8,128)(2,1)S(1)}, bf16[48,1024]{1,0:T(8,128)(2,1)S(1)}, u32[]{:S(2)}, u32[]{:S(2)}) collective-permute-start(bf16[48,1024]{1,0:T(8,128)(2,1)S(1)} %convolution_convert_fusion.10), channel_id=1, source_target_pairs={{0,2},{2,0},{1,3},{3,1},{4,6},{6,4},{5,7},{7,5},{8,10},{10,8},{9,1... | collective-permute-start | bytes 294920 | tf_op jit(solution)/shard_map/ppermute | solution.py:44
  163.9 9.8 %collective-permute-start.13 = (bf16[48,1024]{1,0:T(8,128)(2,1)S(1)}, bf16[48,1024]{1,0:T(8,128)(2,1)S(1)}, u32[]{:S(2)}, u32[]{:S(2)}) collective-permute-start(bf16[48,1024]{1,0:T(8,128)(2,1)S(1)} %convolution_convert_fusion.7), channel_id=1, source_target_pairs={{2,4},{4,2},{3,5},{5,3},{6,8},{8,6},{7,9},{9,7},{10,12},{12,10},{1... | collective-permute-start | bytes 294920 | tf_op jit(solution)/shard_map/ppermute | solution.py:44
  169.1 6.5 %collective-permute-start.12 = (bf16[48,1024]{1,0:T(8,128)(2,1)S(1)}, bf16[48,1024]{1,0:T(8,128)(2,1)S(1)}, u32[]{:S(2)}, u32[]{:S(2)}) collective-permute-start(bf16[48,1024]{1,0:T(8,128)(2,1)S(1)} %convolution_convert_fusion.8), channel_id=1, source_target_pairs={{0,2},{2,0},{1,3},{3,1},{4,6},{6,4},{5,7},{7,5},{8,10},{10,8},{9,1... | collective-permute-start | bytes 294920 | tf_op jit(solution)/shard_map/ppermute | solution.py:44
  179.1 9.8 %collective-permute-start.15 = (bf16[48,1024]{1,0:T(8,128)(2,1)S(1)}, bf16[48,1024]{1,0:T(8,128)(2,1)S(1)}, u32[]{:S(2)}, u32[]{:S(2)}) collective-permute-start(bf16[48,1024]{1,0:T(8,128)(2,1)S(1)} %convolution_convert_fusion.5), channel_id=1, source_target_pairs={{2,4},{4,2},{3,5},{5,3},{6,8},{8,6},{7,9},{9,7},{10,12},{12,10},{1... | collective-permute-start | bytes 294920 | tf_op jit(solution)/shard_map/ppermute | solution.py:44
  183.8 6.5 %collective-permute-start.14 = (bf16[48,1024]{1,0:T(8,128)(2,1)S(1)}, bf16[48,1024]{1,0:T(8,128)(2,1)S(1)}, u32[]{:S(2)}, u32[]{:S(2)}) collective-permute-start(bf16[48,1024]{1,0:T(8,128)(2,1)S(1)} %convolution_convert_fusion.6), channel_id=1, source_target_pairs={{0,2},{2,0},{1,3},{3,1},{4,6},{6,4},{5,7},{7,5},{8,10},{10,8},{9,1... | collective-permute-start | bytes 294920 | tf_op jit(solution)/shard_map/ppermute | solution.py:44
  193.8 9.8 %collective-permute-start.17 = (bf16[48,1024]{1,0:T(8,128)(2,1)S(1)}, bf16[48,1024]{1,0:T(8,128)(2,1)S(1)}, u32[]{:S(2)}, u32[]{:S(2)}) collective-permute-start(bf16[48,1024]{1,0:T(8,128)(2,1)S(1)} %convolution_convert_fusion.3), channel_id=1, source_target_pairs={{2,4},{4,2},{3,5},{5,3},{6,8},{8,6},{7,9},{9,7},{10,12},{12,10},{1... | collective-permute-start | bytes 294920 | tf_op jit(solution)/shard_map/ppermute | solution.py:44
  199.0 6.5 %collective-permute-start.16 = (bf16[48,1024]{1,0:T(8,128)(2,1)S(1)}, bf16[48,1024]{1,0:T(8,128)(2,1)S(1)}, u32[]{:S(2)}, u32[]{:S(2)}) collective-permute-start(bf16[48,1024]{1,0:T(8,128)(2,1)S(1)} %convolution_convert_fusion.4), channel_id=1, source_target_pairs={{0,2},{2,0},{1,3},{3,1},{4,6},{6,4},{5,7},{7,5},{8,10},{10,8},{9,1... | collective-permute-start | bytes 294920 | tf_op jit(solution)/shard_map/ppermute | solution.py:44
  209.1 9.8 %collective-permute-start.19 = (bf16[48,1024]{1,0:T(8,128)(2,1)S(1)}, bf16[48,1024]{1,0:T(8,128)(2,1)S(1)}, u32[]{:S(2)}, u32[]{:S(2)}) collective-permute-start(bf16[48,1024]{1,0:T(8,128)(2,1)S(1)} %convolution_convert_fusion.1), channel_id=1, source_target_pairs={{2,4},{4,2},{3,5},{5,3},{6,8},{8,6},{7,9},{9,7},{10,12},{12,10},{1... | collective-permute-start | bytes 294920 | tf_op jit(solution)/shard_map/ppermute | solution.py:44
  213.7 6.5 %collective-permute-start.18 = (bf16[48,1024]{1,0:T(8,128)(2,1)S(1)}, bf16[48,1024]{1,0:T(8,128)(2,1)S(1)}, u32[]{:S(2)}, u32[]{:S(2)}) collective-permute-start(bf16[48,1024]{1,0:T(8,128)(2,1)S(1)} %convolution_convert_fusion.2), channel_id=1, source_target_pairs={{0,2},{2,0},{1,3},{3,1},{4,6},{6,4},{5,7},{7,5},{8,10},{10,8},{9,1... | collective-permute-start | bytes 294920 | tf_op jit(solution)/shard_map/ppermute | solution.py:44
  244.4 1.5 copy-start.1
Sparse Core Ops, SparseCore 0:
  10.6 104.6 all-gather.1

commit v3 on v2

--- a/solution.py
+++ b/solution.py
@@ -1,6 +1,8 @@
 import jax
 import jax.numpy as jnp
 from jax import lax
+from jax.experimental import pallas as pl
+from jax.experimental.pallas import tpu as pltpu
 from jax.sharding import PartitionSpec as P
 
 ALPHA = 0.1
@@ -19,6 +21,103 @@
 
 def one_hot(ids, width):
     return (ids[:, None] == lax.broadcasted_iota(jnp.int32, (ids.shape[0], width), 1)).astype(BF)
+
+
+VM = pl.BlockSpec(memory_space=pltpu.VMEM)
+HB = pl.BlockSpec(memory_space=pltpu.HBM)
+
+
+def in_vmem(*values):
+    return [pltpu.with_memory_space_constraint(v, pltpu.VMEM) for v in values]
+
+
+def finish_body(layer, strip, prefetched, *refs):
+    if prefetched:
+        local, got_a, got_b, far, picks, start, weight, new, out_a, out_b, total, rounded = refs
+    else:
+        local, got_a, got_b, far, picks, start, stored = refs[:7]
+        new, out_a, out_b, total, rounded, weight, sem = refs[7:]
+        copy = pltpu.make_async_copy(stored.at[layer], weight, sem)
+        copy.start()
+    width = start.shape[1]
+    edges = got_a.shape[0]
+    strength = jnp.log(jnp.float32(LAMBDA / (layer + 1.0)) + 1.0)
+    for low in range(0, width, strip):
+        cols = slice(low, low + strip)
+        got = jnp.concatenate([got_a[:, cols], got_b[:, cols]], axis=0)
+        summed = local[:, cols] + dot(far[...], got)
+        support = (1.0 - ALPHA) * summed + ALPHA * start[:, cols].astype(F32)
+        total[:, cols] = support
+        rounded[:, cols] = support.astype(BF)
+    if not prefetched:
+        copy.wait()
+    for low in range(0, width, strip):
+        cols = slice(low, low + strip)
+        mixing = dot(rounded[...], weight[:, cols])
+        fresh = jax.nn.relu((1.0 - strength) * total[:, cols] + strength * mixing).astype(BF)
+        new[:, cols] = fresh
+        sent = dot(picks[...], fresh).astype(BF)
+        out_a[:, cols] = sent[:edges]
+        out_b[:, cols] = sent[edges:]
+
+
+def finish(layer, local, got_a, got_b, far, picks, start, weight, prefetched):
+    rows, width = start.shape
+    edges = got_a.shape[0]
+    ins = in_vmem(local, got_a, got_b, far, picks, start)
+    scratch = [pltpu.VMEM((rows, width), F32), pltpu.VMEM((rows, width), BF)]
+    if prefetched:
+        ins += in_vmem(weight)
+    else:
+        ins.append(pltpu.with_memory_space_constraint(weight, pltpu.HBM))
+        scratch += [pltpu.VMEM(weight.shape[1:], BF), pltpu.SemaphoreType.DMA]
+    return pl.pallas_call(
+        lambda *refs: finish_body(layer, min(256, width), prefetched, *refs),
+        out_shape=(
+            pltpu.VMEM((rows, width), BF),
+            pltpu.VMEM((edges, width), BF),
+            pltpu.VMEM((edges, width), BF),
+        ),
+        in_specs=[VM] * 6 + [VM if prefetched else HB],
+        out_specs=(VM, VM, VM),
+        scratch_shapes=scratch,
+        compiler_params=pltpu.CompilerParams(vmem_limit_bytes=10 << 20),
+        name="finish",
+    )(*ins)
+
+
+def begin_body(layer, strip, *refs):
+    if layer is None:
+        current, near, hist, looked, local = refs
+    else:
+        current, near, hist, looked, stored, local, weight, sem = refs
+        copy = pltpu.make_async_copy(stored.at[layer], weight, sem)
+        copy.start()
+    for low in range(0, current.shape[1], strip):
+        cols = slice(low, low + strip)
+        local[:, cols] = dot(near[...], current[:, cols]) + dot(hist[...], looked[:, cols])
+    if layer is not None:
+        copy.wait()
+
+
+def begin(layer, current, near, hist, looked, stored):
+    rows, width = current.shape
+    ins = in_vmem(current, near, hist, looked)
+    outs = [pltpu.VMEM((rows, width), F32)]
+    scratch = []
+    if layer is not None:
+        ins.append(pltpu.with_memory_space_constraint(stored, pltpu.HBM))
+        outs.append(pltpu.VMEM(stored.shape[1:], BF))
+        scratch.append(pltpu.SemaphoreType.DMA)
+    return pl.pallas_call(
+        lambda *refs: begin_body(layer, min(256, width), *refs),
+        out_shape=tuple(outs),
+        in_specs=[VM] * 4 + [HB] * (layer is not None),
+        out_specs=(VM,) * len(outs),
+        scratch_shapes=scratch,
+        compiler_params=pltpu.CompilerParams(vmem_limit_bytes=4 << 20),
+        name="begin",
+    )(*ins)
 
 
 def shards(features, weights, history, own_adj, side_adj, hist_adj, send_ids, hist_ids):
@@ -120,21 +219,26 @@
     looked = jnp.concatenate([g0, g1], axis=1)
     start = jnp.concatenate([x0, x1], axis=0)
 
+    far = jnp.concatenate([far_a, far_b], axis=0).T
+    picks = jnp.concatenate([pick_a, pick_b], axis=0)
+    hist_n = hist_t.T
     current = start
+    sent = dot(picks, current).astype(BF)
+    send_a, send_b = sent[: 3 * edge], sent[3 * edge :]
+    (local,) = begin(None, current, near, hist_n, looked[0], None)
+    weight = resident
     own_rows = []
     for layer in range(layers):
-        strength = jnp.log(jnp.float32(LAMBDA / (layer + 1.0)) + 1.0)
-        got_a = exchange(dot(pick_a, current).astype(BF), 0)
-        got_b = exchange(dot(pick_b, current).astype(BF), 2)
-        local = dot(near, current) + dot_t(hist_t, looked[layer])
-        total = local + dot_t(far_a, got_a) + dot_t(far_b, got_b)
-        support = (1.0 - ALPHA) * total + ALPHA * start.astype(F32)
-        mixing = dot(support.astype(BF), resident[layer])
-        current = jax.nn.relu((1.0 - strength) * support + strength * mixing).astype(BF)
+        got_a = exchange(send_a, 0)
+        got_b = exchange(send_b, 2)
+        current, send_a, send_b = finish(
+            layer, local, got_a, got_b, far, picks, start, weight, layer > 0
+        )
+        if layer + 1 < layers:
+            local, weight = begin(layer + 1, current, near, hist_n, looked[layer + 1], resident)
         own_rows.append(lax.dynamic_slice_in_dim(current, core * rows, rows, 0))
-    whole = jnp.stack(own_rows).reshape(segment_count, kept, rows, width)
-    exchanged = lax.all_to_all(whole, "segment", 0, 0)
-    return exchanged.transpose(1, 0, 2, 3).reshape(kept, segment_count * rows, width)
+    whole = jnp.stack(own_rows)
+    return lax.all_to_all(whole, "segment", 0, 1, tiled=True)
 
 
 def solution(mesh):

time: 254 us -> 250 us (0.984)
  matrix products: 35.9 us -> 1.09 us
  Pallas kernels: 0 us -> 31.3 us
  waiting for transfers between devices: 104 us -> 93.5 us
  starting transfers between devices: 66.9 us -> 73.1 us
    pallas_call x0 -> x16, Pallas kernels: none -> 31.3 us  [the longest x8 18 us: finish(): pl.pallas_call(lambda *refs: finish_body(layer, min(256, width), prefetch...]
    dot_general x33 -> x2, matrix products: 27.5 us -> 0.7 us  [dot(): return jnp.dot(a, b, preferred_element_type=F32)]
    ppermute x16, waiting for transfers between devices: 34 us -> 18.6 us  [exchange(): return lax.ppermute(value, 'graph', pairs)]
    dot_general x26 -> x2, matrix products: 8.4 us -> 0.39 us  [dot_t(): lax.dot_general(a, b, (((0,), (0,)), ((), ())), preferred_element_type=F32)]
    ppermute x16, starting transfers between devices: 58.2 us -> 64.4 us  [exchange(): return lax.ppermute(value, 'graph', pairs)]
    all_gather x1, waiting for transfers between devices: 68.9 us -> 74.2 us  [shards(): resident = lax.all_gather(weights, 'graph', axis=1, tiled=True)]
  transfers between devices with their start and end apart: 21 -> 21, of which waited for: 17 -> 9; matrix products, arithmetic and copies ran while one was open for 7% -> 4% of each run, Pallas kernels for 0% -> 5%
where the time goes in v3:
time: 250 us; the launch traced here: 248 us
  waiting for transfers between devices  93.5 us (37%)
  starting transfers between devices  73.1 us (29%)
  Pallas kernels  31.3 us (13%)
  blocking collectives  23 us (9%)
  between operations  14.1 us (6%)
  local copies, waits for them, and re-layouts  8.22 us (3%)
  other arithmetic  4.24 us (2%)
    all_gather x1, waiting for transfers between devices, shards(): resident = lax.all_gather(weights, 'graph', axis=1, tiled=True)  74.2 us
    ppermute x16, starting transfers between devices, exchange(): return lax.ppermute(value, 'graph', pairs)  64.4 us
    all_to_all x1, blocking collectives, shards(): return lax.all_to_all(whole, 'segment', 0, 1, tiled=True)  23 us
    ppermute x16, waiting for transfers between devices, exchange(): return lax.ppermute(value, 'graph', pairs)  18.6 us
    pallas_call x8, Pallas kernels, finish(): pl.pallas_call(lambda *refs: finish_body(layer, min(256, width), prefetch...  18 us
    pallas_call x8, Pallas kernels, begin(): pl.pallas_call(lambda *refs: begin_body(layer, min(256, width), *refs), o...  13.3 us
    ppermute x4, starting transfers between devices, partner(): lax.ppermute(value, 'graph', [(p, p ^ 1) for p in range(graph_count)])  8.64 us
  transfers between devices with their start and end apart: 21, of which 9 were waited for; matrix products, arithmetic and copies ran while one was open for 4% of the time, Pallas kernels for 5%

profile of v3, /device:TPU:32, one launch (start us, length us, event | category | flops | bytes accessed | tf_op | source)
XLA Modules:
  0.0 248.5 jit_solution(7518454092843238576)
XLA Ops:
  6.5 0.7 all-gather.2.cloned.1.call-update
  7.3 0.7 constant_dynamic-slice_fusion.2
  8.0 0.7 dynamic-slice_bitcast_fusion.1
  8.7 0.8 dynamic-slice_bitcast_fusion
  9.5 1.9 collective-permute-start.1
  11.4 0.7 fusion.33
  12.1 0.5 fusion
  12.6 2.4 collective-permute-start.3
  15.0 0.7 constant_dynamic-slice_fusion.1
  15.8 1.9 collective-permute-start.2
  17.8 1.0 constant_dynamic-slice_fusion.3
  18.7 2.4 collective-permute-start
  22.0 0.1 copy.48.refs_3_
  22.3 0.2 convolution_convert_fusion.2
  22.4 0.2 convolution_convert_fusion.3
  22.7 1.1 broadcast_select_fusion.3
  23.8 0.2 convolution_convert_fusion.1
  24.0 4.3 %collective-permute-start.4 = (bf16[48,1024]{1,0:T(8,128)(2,1)S(1)}, bf16[48,1024]{1,0:T(8,128)(2,1)S(1)}, u32[]{:S(2)}, u32[]{:S(2)}) collective-permute-start(bf16[48,1024]{1,0:T(8,128)(2,1)S(1)} %get-tuple-element.90), channel_id=1, source_target_pairs={{0,2},{2,0},{1,3},{3,1},{4,6},{6,4},{5,7},{7,5},{8,10},{10,8},{9,1... | collective-permute-start | bytes 294920 | tf_op jit(solution)/shard_map/ppermute | solution.py:143
  28.3 9.0 %collective-permute-start.5 = (bf16[48,1024]{1,0:T(8,128)(2,1)S(1)}, bf16[48,1024]{1,0:T(8,128)(2,1)S(1)}, u32[]{:S(2)}, u32[]{:S(2)}) collective-permute-start(bf16[48,1024]{1,0:T(8,128)(2,1)S(1)} %get-tuple-element.89), channel_id=1, source_target_pairs={{2,4},{4,2},{3,5},{5,3},{6,8},{8,6},{7,9},{9,7},{10,12},{12,10},{1... | collective-permute-start | bytes 294920 | tf_op jit(solution)/shard_map/ppermute | solution.py:143
  37.4 1.4 broadcast_select_fusion.1
  38.8 1.1 fusion.8
  39.8 0.4 begin.8.refs_0_
  40.2 0.3 collective-permute-done.5.refs_2_
  40.6 0.6 copy-done.6
  41.2 74.2 %all-gather.2.cloned.1.call-done.refs_6_.refs_4_ = bf16[8,1024,1024]{2,1,0:T(8,128)(2,1)} async-done(((bf16[8,8,1024]{2,1,0:T(8,128)(2,1)}), bf16[8,1024,1024]{2,1,0:T(8,128)(2,1)}) %all-gather.2.cloned.1.call-update) | async-done | bytes 16777232 | tf_op jit(solution)/shard_map/all_gather | solution.py:133
  115.4 0.9 copy-done.7
  116.2 3.5 %finish.8 = (bf16[256,1024]{1,0:T(8,128)(2,1)S(1)}, bf16[48,1024]{1,0:T(8,128)(2,1)S(1)}, bf16[48,1024]{1,0:T(8,128)(2,1)S(1)}) custom-call(f32[256,1024]{1,0:T(8,128)S(1)} %begin.8.refs_0_, bf16[48,1024]{1,0:T(8,128)(2,1)S(1)} %collective-permute-done.4.refs_1_, bf16[48,1024]{1,0:T(8,128)(2,1)S(1)} %copy-done.7, bf16[256,96]{1,0:T(8,128)(2,1)S(1)} %copy.48.refs_3_, ...), custom_call_target="tpu_custom_call" | custom-call | tf_op jit(solution)/shard_map/finish/pallas_call | solution.py:74
  119.7 1.9 collective-permute-start.6
  121.7 5.6 %collective-permute-start.7 = (bf16[48,1024]{1,0:T(8,128)(2,1)S(1)}, bf16[48,1024]{1,0:T(8,128)(2,1)S(1)}, u32[]{:S(2)}, u32[]{:S(2)}) collective-permute-start(bf16[48,1024]{1,0:T(8,128)(2,1)S(1)} %get-tuple-element.44), channel_id=1, source_target_pairs={{2,4},{4,2},{3,5},{5,3},{6,8},{8,6},{7,9},{9,7},{10,12},{12,10},{1... | collective-permute-start | bytes 294920 | tf_op jit(solution)/shard_map/ppermute | solution.py:143
  127.3 1.8 begin.9
  129.2 2.6 %collective-permute-done.7.refs_2_ = bf16[48,1024]{1,0:T(8,128)(2,1)S(1)} collective-permute-done((bf16[48,1024]{1,0:T(8,128)(2,1)S(1)}, bf16[48,1024]{1,0:T(8,128)(2,1)S(1)}, u32[]{:S(2)}, u32[]{:S(2)}) %collective-permute-start.7) | collective-permute-done | bytes 98336 | tf_op jit(solution)/shard_map/ppermute | solution.py:143
  131.8 2.0 finish.9
  133.8 1.9 collective-permute-start.8
  135.7 5.3 %collective-permute-start.9 = (bf16[48,1024]{1,0:T(8,128)(2,1)S(1)}, bf16[48,1024]{1,0:T(8,128)(2,1)S(1)}, u32[]{:S(2)}, u32[]{:S(2)}) collective-permute-start(bf16[48,1024]{1,0:T(8,128)(2,1)S(1)} %get-tuple-element.49), channel_id=1, source_target_pairs={{2,4},{4,2},{3,5},{5,3},{6,8},{8,6},{7,9},{9,7},{10,12},{12,10},{1... | collective-permute-start | bytes 294920 | tf_op jit(solution)/shard_map/ppermute | solution.py:143
  141.1 1.8 begin.10
  143.0 2.6 %collective-permute-done.9.refs_2_ = bf16[48,1024]{1,0:T(8,128)(2,1)S(1)} collective-permute-done((bf16[48,1024]{1,0:T(8,128)(2,1)S(1)}, bf16[48,1024]{1,0:T(8,128)(2,1)S(1)}, u32[]{:S(2)}, u32[]{:S(2)}) %collective-permute-start.9) | collective-permute-done | bytes 98336 | tf_op jit(solution)/shard_map/ppermute | solution.py:143
  145.6 2.0 finish.10
  147.6 1.9 collective-permute-start.10
  149.5 5.3 %collective-permute-start.11 = (bf16[48,1024]{1,0:T(8,128)(2,1)S(1)}, bf16[48,1024]{1,0:T(8,128)(2,1)S(1)}, u32[]{:S(2)}, u32[]{:S(2)}) collective-permute-start(bf16[48,1024]{1,0:T(8,128)(2,1)S(1)} %get-tuple-element.54), channel_id=1, source_target_pairs={{2,4},{4,2},{3,5},{5,3},{6,8},{8,6},{7,9},{9,7},{10,12},{12,10},{1... | collective-permute-start | bytes 294920 | tf_op jit(solution)/shard_map/ppermute | solution.py:143
  154.8 1.8 begin.11
  156.7 2.6 %collective-permute-done.11.refs_2_ = bf16[48,1024]{1,0:T(8,128)(2,1)S(1)} collective-permute-done((bf16[48,1024]{1,0:T(8,128)(2,1)S(1)}, bf16[48,1024]{1,0:T(8,128)(2,1)S(1)}, u32[]{:S(2)}, u32[]{:S(2)}) %collective-permute-start.11) | collective-permute-done | bytes 98336 | tf_op jit(solution)/shard_map/ppermute | solution.py:143
  159.3 2.0 finish.11
  161.3 1.9 collective-permute-start.12
  163.2 5.3 %collective-permute-start.13 = (bf16[48,1024]{1,0:T(8,128)(2,1)S(1)}, bf16[48,1024]{1,0:T(8,128)(2,1)S(1)}, u32[]{:S(2)}, u32[]{:S(2)}) collective-permute-start(bf16[48,1024]{1,0:T(8,128)(2,1)S(1)} %get-tuple-element.59), channel_id=1, source_target_pairs={{2,4},{4,2},{3,5},{5,3},{6,8},{8,6},{7,9},{9,7},{10,12},{12,10},{1... | collective-permute-start | bytes 294920 | tf_op jit(solution)/shard_map/ppermute | solution.py:143
  168.6 1.8 begin.12
  170.5 2.6 %collective-permute-done.13.refs_2_ = bf16[48,1024]{1,0:T(8,128)(2,1)S(1)} collective-permute-done((bf16[48,1024]{1,0:T(8,128)(2,1)S(1)}, bf16[48,1024]{1,0:T(8,128)(2,1)S(1)}, u32[]{:S(2)}, u32[]{:S(2)}) %collective-permute-start.13) | collective-permute-done | bytes 98336 | tf_op jit(solution)/shard_map/ppermute | solution.py:143
  173.1 2.0 finish.12
  175.0 1.9 collective-permute-start.14
  177.0 5.3 %collective-permute-start.15 = (bf16[48,1024]{1,0:T(8,128)(2,1)S(1)}, bf16[48,1024]{1,0:T(8,128)(2,1)S(1)}, u32[]{:S(2)}, u32[]{:S(2)}) collective-permute-start(bf16[48,1024]{1,0:T(8,128)(2,1)S(1)} %get-tuple-element.64), channel_id=1, source_target_pairs={{2,4},{4,2},{3,5},{5,3},{6,8},{8,6},{7,9},{9,7},{10,12},{12,10},{1... | collective-permute-start | bytes 294920 | tf_op jit(solution)/shard_map/ppermute | solution.py:143
  182.3 1.8 begin.13
  184.2 2.6 %collective-permute-done.15.refs_2_ = bf16[48,1024]{1,0:T(8,128)(2,1)S(1)} collective-permute-done((bf16[48,1024]{1,0:T(8,128)(2,1)S(1)}, bf16[48,1024]{1,0:T(8,128)(2,1)S(1)}, u32[]{:S(2)}, u32[]{:S(2)}) %collective-permute-start.15) | collective-permute-done | bytes 98336 | tf_op jit(solution)/shard_map/ppermute | solution.py:143
  186.8 2.0 finish.13
  188.8 1.9 collective-permute-start.16
  190.7 5.5 %collective-permute-start.17 = (bf16[48,1024]{1,0:T(8,128)(2,1)S(1)}, bf16[48,1024]{1,0:T(8,128)(2,1)S(1)}, u32[]{:S(2)}, u32[]{:S(2)}) collective-permute-start(bf16[48,1024]{1,0:T(8,128)(2,1)S(1)} %get-tuple-element.69), channel_id=1, source_target_pairs={{2,4},{4,2},{3,5},{5,3},{6,8},{8,6},{7,9},{9,7},{10,12},{12,10},{1... | collective-permute-start | bytes 294920 | tf_op jit(solution)/shard_map/ppermute | solution.py:143
  196.2 1.8 begin.14
  198.1 2.6 %collective-permute-done.17.refs_2_ = bf16[48,1024]{1,0:T(8,128)(2,1)S(1)} collective-permute-done((bf16[48,1024]{1,0:T(8,128)(2,1)S(1)}, bf16[48,1024]{1,0:T(8,128)(2,1)S(1)}, u32[]{:S(2)}, u32[]{:S(2)}) %collective-permute-start.17) | collective-permute-done | bytes 98336 | tf_op jit(solution)/shard_map/ppermute | solution.py:143
  200.7 2.0 finish.14
  202.7 1.9 collective-permute-start.18
  204.6 5.3 %collective-permute-start.19 = (bf16[48,1024]{1,0:T(8,128)(2,1)S(1)}, bf16[48,1024]{1,0:T(8,128)(2,1)S(1)}, u32[]{:S(2)}, u32[]{:S(2)}) collective-permute-start(bf16[48,1024]{1,0:T(8,128)(2,1)S(1)} %get-tuple-element.74), channel_id=1, source_target_pairs={{2,4},{4,2},{3,5},{5,3},{6,8},{8,6},{7,9},{9,7},{10,12},{12,10},{1... | collective-permute-start | bytes 294920 | tf_op jit(solution)/shard_map/ppermute | solution.py:143
  210.0 1.8 begin.15
  211.9 2.6 %collective-permute-done.19.refs_2_ = bf16[48,1024]{1,0:T(8,128)(2,1)S(1)} collective-permute-done((bf16[48,1024]{1,0:T(8,128)(2,1)S(1)}, bf16[48,1024]{1,0:T(8,128)(2,1)S(1)}, u32[]{:S(2)}, u32[]{:S(2)}) %collective-permute-start.19) | collective-permute-done | bytes 98336 | tf_op jit(solution)/shard_map/ppermute | solution.py:143
  214.5 2.6 %finish.15 = (bf16[256,1024]{1,0:T(8,128)(2,1)S(1)}, bf16[48,1024]{1,0:T(8,128)(2,1)}, bf16[48,1024]{1,0:T(8,128)(2,1)}) custom-call(f32[256,1024]{1,0:T(8,128)S(1)} %get-tuple-element.72.refs_0_, bf16[48,1024]{1,0:T(8,128)(2,1)S(1)} %collective-permute-done.18.refs_1_, bf16[48,1024]{1,0:T(8,128)(2,1)S(1)} %collective-permute-done.19.refs_2_, ...), custom_call_target="tpu_custom_call" | custom-call | tf_op jit(solution)/shard_map/finish/pallas_call | solution.py:74
  217.1 23.0 %all_to_all.18 = bf16[8,128,1024]{2,1,0:T(8,128)(2,1)S(1)} all-to-all(bf16[8,128,1024]{2,1,0:T(8,128)(2,1)S(1)} %bitcast_dynamic-update-slice_fusion), channel_id=1, replica_groups=mesh['segment'=4,'graph'=128] {'segment'}, dimensions={0} | all-to-all | bytes 4194304 | tf_op jit(solution)/shard_map/all_to_all | solution.py:241
  240.2 1.5 copy.63
  (62 shorter events, 1.3 us)
Async XLA Ops:
  6.5 5.6 %copy-start = (bf16[8,64,1024]{2,1,0:T(8,128)(2,1)S(1)}, bf16[8,64,1024]{2,1,0:T(8,128)(2,1)}, u32[]{:S(2)}) copy-start(bf16[8,64,1024]{2,1,0:T(8,128)(2,1)} %param.10) | copy-start | bytes 3145732
  6.5 108.8 %all-gather.2.cloned.1.call-start = ((), (), s32[]{:S(2)}) async-start(), calls=%async_computation.1 | async-start | bytes 16908288 | tf_op jit(solution)/shard_map/all_gather | solution.py:133
  9.5 12.4 %collective-permute-start.1 = (bf16[256,128]{1,0:T(8,128)(2,1)S(1)}, bf16[256,128]{1,0:T(8,128)(2,1)S(1)}, u32[]{:S(2)}, u32[]{:S(2)}) collective-permute-start(bf16[256,128]{1,0:T(8,128)(2,1)S(1)} %pad_maximum_fusion.2), channel_id=1, source_target_pairs={{0,1},{1,0},{2,3},{3,2},{4,5},{5,4},{6,7},{7,6},{8,9},{9,8},{10,11... | collective-permute-start | bytes 196616 | tf_op jit(solution)/shard_map/ppermute | solution.py:136
  12.6 24.8 %collective-permute-start.3 = (bf16[8,64,1024]{2,1,0:T(8,128)(2,1)S(1)}, bf16[8,64,1024]{2,1,0:T(8,128)(2,1)}, u32[]{:S(2)}, u32[]{:S(2)}) collective-permute-start(bf16[8,64,1024]{2,1,0:T(8,128)(2,1)S(1)} %fusion), channel_id=1, source_target_pairs={{0,1},{1,0},{2,3},{3,2},{4,5},{5,4},{6,7},{7,6},{8,9},{9,8},{10,11... | collective-permute-start | bytes 3145736 | tf_op jit(solution)/shard_map/ppermute | solution.py:136
  15.8 5.4 %collective-permute-start.2 = (s32[128]{0:T(128)S(1)}, s32[128]{0:T(128)S(1)}, u32[]{:S(2)}, u32[]{:S(2)}) collective-permute-start(s32[128]{0:T(128)S(1)} %pad_add_fusion.4), channel_id=1, source_target_pairs={{0,1},{1,0},{2,3},{3,2},{4,5},{5,4},{6,7},{7,6},{8,9},{9,8},{10,11... | collective-permute-start | bytes 1544 | tf_op jit(solution)/shard_map/ppermute | solution.py:136
  18.7 3.9 %collective-permute-start = (bf16[128,1024]{1,0:T(8,128)(2,1)S(1)}, bf16[128,1024]{1,0:T(8,128)(2,1)S(1)}, u32[]{:S(2)}, u32[]{:S(2)}) collective-permute-start(bf16[128,1024]{1,0:T(8,128)(2,1)S(1)} %constant_dynamic-slice_fusion.3), channel_id=1, source_target_pairs={{0,1},{1,0},{2,3},{3,2},{4,5},{5,4},{6,7},{7,6},{8,9},{9,8},{10,11... | collective-permute-start | bytes 786440 | tf_op jit(solution)/shard_map/ppermute | solution.py:136
  24.0 16.2 %collective-permute-start.4 = (bf16[48,1024]{1,0:T(8,128)(2,1)S(1)}, bf16[48,1024]{1,0:T(8,128)(2,1)S(1)}, u32[]{:S(2)}, u32[]{:S(2)}) collective-permute-start(bf16[48,1024]{1,0:T(8,128)(2,1)S(1)} %get-tuple-element.90), channel_id=1, source_target_pairs={{0,2},{2,0},{1,3},{3,1},{4,6},{6,4},{5,7},{7,5},{8,10},{10,8},{9,1... | collective-permute-start | bytes 294920 | tf_op jit(solution)/shard_map/ppermute | solution.py:143
  28.3 12.3 %collective-permute-start.5 = (bf16[48,1024]{1,0:T(8,128)(2,1)S(1)}, bf16[48,1024]{1,0:T(8,128)(2,1)S(1)}, u32[]{:S(2)}, u32[]{:S(2)}) collective-permute-start(bf16[48,1024]{1,0:T(8,128)(2,1)S(1)} %get-tuple-element.89), channel_id=1, source_target_pairs={{2,4},{4,2},{3,5},{5,3},{6,8},{8,6},{7,9},{9,7},{10,12},{12,10},{1... | collective-permute-start | bytes 294920 | tf_op jit(solution)/shard_map/ppermute | solution.py:143
  40.6 0.6 copy-start.6
  115.4 0.9 copy-start.7
  116.2 11.1 %copy-start.5 = (bf16[128,1024]{1,0:T(8,128)(2,1)S(1)}, bf16[128,1024]{1,0:T(8,128)(2,1)}, u32[]{:S(2)}) copy-start(bf16[128,1024]{1,0:T(8,128)(2,1)} %get-tuple-element.79.refs_3_) | copy-start | bytes 786436
  119.7 9.5 %collective-permute-start.6 = (bf16[48,1024]{1,0:T(8,128)(2,1)S(1)}, bf16[48,1024]{1,0:T(8,128)(2,1)S(1)}, u32[]{:S(2)}, u32[]{:S(2)}) collective-permute-start(bf16[48,1024]{1,0:T(8,128)(2,1)S(1)} %get-tuple-element.43), channel_id=1, source_target_pairs={{0,2},{2,0},{1,3},{3,1},{4,6},{6,4},{5,7},{7,5},{8,10},{10,8},{9,1... | collective-permute-start | bytes 294920 | tf_op jit(solution)/shard_map/ppermute | solution.py:143
  121.7 10.2 %collective-permute-start.7 = (bf16[48,1024]{1,0:T(8,128)(2,1)S(1)}, bf16[48,1024]{1,0:T(8,128)(2,1)S(1)}, u32[]{:S(2)}, u32[]{:S(2)}) collective-permute-start(bf16[48,1024]{1,0:T(8,128)(2,1)S(1)} %get-tuple-element.44), channel_id=1, source_target_pairs={{2,4},{4,2},{3,5},{5,3},{6,8},{8,6},{7,9},{9,7},{10,12},{12,10},{1... | collective-permute-start | bytes 294920 | tf_op jit(solution)/shard_map/ppermute | solution.py:143
  131.8 9.2 %copy-start.4 = (bf16[128,1024]{1,0:T(8,128)(2,1)S(1)}, bf16[128,1024]{1,0:T(8,128)(2,1)}, u32[]{:S(2)}) copy-start(bf16[128,1024]{1,0:T(8,128)(2,1)} %get-tuple-element.80.refs_3_) | copy-start | bytes 786436
  133.8 9.1 %collective-permute-start.8 = (bf16[48,1024]{1,0:T(8,128)(2,1)S(1)}, bf16[48,1024]{1,0:T(8,128)(2,1)S(1)}, u32[]{:S(2)}, u32[]{:S(2)}) collective-permute-start(bf16[48,1024]{1,0:T(8,128)(2,1)S(1)} %get-tuple-element.48), channel_id=1, source_target_pairs={{0,2},{2,0},{1,3},{3,1},{4,6},{6,4},{5,7},{7,5},{8,10},{10,8},{9,1... | collective-permute-start | bytes 294920 | tf_op jit(solution)/shard_map/ppermute | solution.py:143
  135.7 9.8 %collective-permute-start.9 = (bf16[48,1024]{1,0:T(8,128)(2,1)S(1)}, bf16[48,1024]{1,0:T(8,128)(2,1)S(1)}, u32[]{:S(2)}, u32[]{:S(2)}) collective-permute-start(bf16[48,1024]{1,0:T(8,128)(2,1)S(1)} %get-tuple-element.49), channel_id=1, source_target_pairs={{2,4},{4,2},{3,5},{5,3},{6,8},{8,6},{7,9},{9,7},{10,12},{12,10},{1... | collective-permute-start | bytes 294920 | tf_op jit(solution)/shard_map/ppermute | solution.py:143
  145.6 9.2 %copy-start.3 = (bf16[128,1024]{1,0:T(8,128)(2,1)S(1)}, bf16[128,1024]{1,0:T(8,128)(2,1)}, u32[]{:S(2)}) copy-start(bf16[128,1024]{1,0:T(8,128)(2,1)} %get-tuple-element.81.refs_3_) | copy-start | bytes 786436
  147.6 9.1 %collective-permute-start.10 = (bf16[48,1024]{1,0:T(8,128)(2,1)S(1)}, bf16[48,1024]{1,0:T(8,128)(2,1)S(1)}, u32[]{:S(2)}, u32[]{:S(2)}) collective-permute-start(bf16[48,1024]{1,0:T(8,128)(2,1)S(1)} %get-tuple-element.53), channel_id=1, source_target_pairs={{0,2},{2,0},{1,3},{3,1},{4,6},{6,4},{5,7},{7,5},{8,10},{10,8},{9,1... | collective-permute-start | bytes 294920 | tf_op jit(solution)/shard_map/ppermute | solution.py:143
  149.5 9.8 %collective-permute-start.11 = (bf16[48,1024]{1,0:T(8,128)(2,1)S(1)}, bf16[48,1024]{1,0:T(8,128)(2,1)S(1)}, u32[]{:S(2)}, u32[]{:S(2)}) collective-permute-start(bf16[48,1024]{1,0:T(8,128)(2,1)S(1)} %get-tuple-element.54), channel_id=1, source_target_pairs={{2,4},{4,2},{3,5},{5,3},{6,8},{8,6},{7,9},{9,7},{10,12},{12,10},{1... | collective-permute-start | bytes 294920 | tf_op jit(solution)/shard_map/ppermute | solution.py:143
  159.3 9.2 %copy-start.2 = (bf16[128,1024]{1,0:T(8,128)(2,1)S(1)}, bf16[128,1024]{1,0:T(8,128)(2,1)}, u32[]{:S(2)}) copy-start(bf16[128,1024]{1,0:T(8,128)(2,1)} %get-tuple-element.82.refs_3_) | copy-start | bytes 786436
  161.3 9.1 %collective-permute-start.12 = (bf16[48,1024]{1,0:T(8,128)(2,1)S(1)}, bf16[48,1024]{1,0:T(8,128)(2,1)S(1)}, u32[]{:S(2)}, u32[]{:S(2)}) collective-permute-start(bf16[48,1024]{1,0:T(8,128)(2,1)S(1)} %get-tuple-element.58), channel_id=1, source_target_pairs={{0,2},{2,0},{1,3},{3,1},{4,6},{6,4},{5,7},{7,5},{8,10},{10,8},{9,1... | collective-permute-start | bytes 294920 | tf_op jit(solution)/shard_map/ppermute | solution.py:143
  163.2 9.8 %collective-permute-start.13 = (bf16[48,1024]{1,0:T(8,128)(2,1)S(1)}, bf16[48,1024]{1,0:T(8,128)(2,1)S(1)}, u32[]{:S(2)}, u32[]{:S(2)}) collective-permute-start(bf16[48,1024]{1,0:T(8,128)(2,1)S(1)} %get-tuple-element.59), channel_id=1, source_target_pairs={{2,4},{4,2},{3,5},{5,3},{6,8},{8,6},{7,9},{9,7},{10,12},{12,10},{1... | collective-permute-start | bytes 294920 | tf_op jit(solution)/shard_map/ppermute | solution.py:143
  173.1 9.2 %copy-start.1 = (bf16[128,1024]{1,0:T(8,128)(2,1)S(1)}, bf16[128,1024]{1,0:T(8,128)(2,1)}, u32[]{:S(2)}) copy-start(bf16[128,1024]{1,0:T(8,128)(2,1)} %get-tuple-element.83.refs_3_) | copy-start | bytes 786436
  175.0 9.1 %collective-permute-start.14 = (bf16[48,1024]{1,0:T(8,128)(2,1)S(1)}, bf16[48,1024]{1,0:T(8,128)(2,1)S(1)}, u32[]{:S(2)}, u32[]{:S(2)}) collective-permute-start(bf16[48,1024]{1,0:T(8,128)(2,1)S(1)} %get-tuple-element.63), channel_id=1, source_target_pairs={{0,2},{2,0},{1,3},{3,1},{4,6},{6,4},{5,7},{7,5},{8,10},{10,8},{9,1... | collective-permute-start | bytes 294920 | tf_op jit(solution)/shard_map/ppermute | solution.py:143
  177.0 9.8 %collective-permute-start.15 = (bf16[48,1024]{1,0:T(8,128)(2,1)S(1)}, bf16[48,1024]{1,0:T(8,128)(2,1)S(1)}, u32[]{:S(2)}, u32[]{:S(2)}) collective-permute-start(bf16[48,1024]{1,0:T(8,128)(2,1)S(1)} %get-tuple-element.64), channel_id=1, source_target_pairs={{2,4},{4,2},{3,5},{5,3},{6,8},{8,6},{7,9},{9,7},{10,12},{12,10},{1... | collective-permute-start | bytes 294920 | tf_op jit(solution)/shard_map/ppermute | solution.py:143
  188.8 9.3 %collective-permute-start.16 = (bf16[48,1024]{1,0:T(8,128)(2,1)S(1)}, bf16[48,1024]{1,0:T(8,128)(2,1)S(1)}, u32[]{:S(2)}, u32[]{:S(2)}) collective-permute-start(bf16[48,1024]{1,0:T(8,128)(2,1)S(1)} %get-tuple-element.68), channel_id=1, source_target_pairs={{0,2},{2,0},{1,3},{3,1},{4,6},{6,4},{5,7},{7,5},{8,10},{10,8},{9,1... | collective-permute-start | bytes 294920 | tf_op jit(solution)/shard_map/ppermute | solution.py:143
  190.7 10.0 %collective-permute-start.17 = (bf16[48,1024]{1,0:T(8,128)(2,1)S(1)}, bf16[48,1024]{1,0:T(8,128)(2,1)S(1)}, u32[]{:S(2)}, u32[]{:S(2)}) collective-permute-start(bf16[48,1024]{1,0:T(8,128)(2,1)S(1)} %get-tuple-element.69), channel_id=1, source_target_pairs={{2,4},{4,2},{3,5},{5,3},{6,8},{8,6},{7,9},{9,7},{10,12},{12,10},{1... | collective-permute-start | bytes 294920 | tf_op jit(solution)/shard_map/ppermute | solution.py:143
  202.7 9.1 %collective-permute-start.18 = (bf16[48,1024]{1,0:T(8,128)(2,1)S(1)}, bf16[48,1024]{1,0:T(8,128)(2,1)S(1)}, u32[]{:S(2)}, u32[]{:S(2)}) collective-permute-start(bf16[48,1024]{1,0:T(8,128)(2,1)S(1)} %get-tuple-element.73), channel_id=1, source_target_pairs={{0,2},{2,0},{1,3},{3,1},{4,6},{6,4},{5,7},{7,5},{8,10},{10,8},{9,1... | collective-permute-start | bytes 294920 | tf_op jit(solution)/shard_map/ppermute | solution.py:143
  204.6 9.8 %collective-permute-start.19 = (bf16[48,1024]{1,0:T(8,128)(2,1)S(1)}, bf16[48,1024]{1,0:T(8,128)(2,1)S(1)}, u32[]{:S(2)}, u32[]{:S(2)}) collective-permute-start(bf16[48,1024]{1,0:T(8,128)(2,1)S(1)} %get-tuple-element.74), channel_id=1, source_target_pairs={{2,4},{4,2},{3,5},{5,3},{6,8},{8,6},{7,9},{9,7},{10,12},{12,10},{1... | collective-permute-start | bytes 294920 | tf_op jit(solution)/shard_map/ppermute | solution.py:143
Sparse Core Ops, SparseCore 0:
  10.6 104.7 all-gather.1

commit v4 on v3

--- a/solution.py
+++ b/solution.py
@@ -25,34 +25,112 @@
 
 VM = pl.BlockSpec(memory_space=pltpu.VMEM)
 HB = pl.BlockSpec(memory_space=pltpu.HBM)
+SM = pl.BlockSpec(memory_space=pltpu.SMEM)
+EARLY = 2
 
 
 def in_vmem(*values):
     return [pltpu.with_memory_space_constraint(v, pltpu.VMEM) for v in values]
 
 
-def finish_body(layer, strip, prefetched, *refs):
-    if prefetched:
-        local, got_a, got_b, far, picks, start, weight, new, out_a, out_b, total, rounded = refs
-    else:
-        local, got_a, got_b, far, picks, start, stored = refs[:7]
-        new, out_a, out_b, total, rounded, weight, sem = refs[7:]
-        copy = pltpu.make_async_copy(stored.at[layer], weight, sem)
-        copy.start()
-    width = start.shape[1]
-    edges = got_a.shape[0]
-    strength = jnp.log(jnp.float32(LAMBDA / (layer + 1.0)) + 1.0)
-    for low in range(0, width, strip):
+def add_up(strip, local, got_a, got_b, far, start, total, rounded):
+    for low in range(0, start.shape[1], strip):
         cols = slice(low, low + strip)
         got = jnp.concatenate([got_a[:, cols], got_b[:, cols]], axis=0)
         summed = local[:, cols] + dot(far[...], got)
         support = (1.0 - ALPHA) * summed + ALPHA * start[:, cols].astype(F32)
         total[:, cols] = support
         rounded[:, cols] = support.astype(BF)
-    if not prefetched:
-        copy.wait()
+
+
+def half_body(layer, strip, core, local, got_a, got_b, far, start, early, out, total, rounded):
+    strength = jnp.log(jnp.float32(LAMBDA / (layer + 1.0)) + 1.0)
+    add_up(strip, local, got_a, got_b, far, start, total, rounded)
+    parts, _, wide = early.shape
+    piece = wide // EARLY
+    half = parts * piece
+    low_half = core[0] == 0
+    for part in range(parts):
+        low = part * piece
+        mixing = dot(rounded[...], early[part, :, layer * piece : (layer + 1) * piece])
+        support = jnp.where(
+            low_half, total[:, low : low + piece], total[:, half + low : half + low + piece]
+        )
+        fresh = jax.nn.relu((1.0 - strength) * support + strength * mixing)
+        out[:, low : low + piece] = fresh.astype(BF)
+
+
+def half_finish(layer, core, local, got_a, got_b, far, start, early):
+    rows, width = start.shape
+    return pl.pallas_call(
+        lambda *refs: half_body(layer, min(256, width), *refs),
+        out_shape=pltpu.VMEM((rows, width // 2), BF),
+        in_specs=[SM] + [VM] * 6,
+        out_specs=VM,
+        scratch_shapes=[pltpu.VMEM((rows, width), F32), pltpu.VMEM((rows, width), BF)],
+        compiler_params=pltpu.CompilerParams(vmem_limit_bytes=10 << 20),
+        name="half_finish",
+    )(core, *in_vmem(local, got_a, got_b, far, start, early))
+
+
+def join_body(core, mine, theirs, picks, new, out_a, out_b):
+    half = mine.shape[1]
+    edges = out_a.shape[0]
+
+    @pl.when(core[0] == 0)
+    def _():
+        new[:, :half] = mine[...]
+        new[:, half:] = theirs[...]
+
+    @pl.when(core[0] != 0)
+    def _():
+        new[:, :half] = theirs[...]
+        new[:, half:] = mine[...]
+
+    sent = dot(picks[...], new[...]).astype(BF)
+    out_a[...] = sent[:edges]
+    out_b[...] = sent[edges:]
+
+
+def join(core, mine, theirs, picks):
+    rows, half = mine.shape
+    edges = picks.shape[0] // 2
+    return pl.pallas_call(
+        join_body,
+        out_shape=(
+            pltpu.VMEM((rows, 2 * half), BF),
+            pltpu.VMEM((edges, 2 * half), BF),
+            pltpu.VMEM((edges, 2 * half), BF),
+        ),
+        in_specs=[SM] + [VM] * 3,
+        out_specs=(VM, VM, VM),
+        compiler_params=pltpu.CompilerParams(vmem_limit_bytes=4 << 20),
+        name="join",
+    )(core, *in_vmem(mine, theirs, picks))
+
+
+def finish_body(layer, slot, strip, prefetched, *refs):
+    if prefetched:
+        local, got_a, got_b, far, picks, start, weight, new, out_a, out_b, total, rounded = refs
+    else:
+        local, got_a, got_b, far, picks, start, stored = refs[:7]
+        new, out_a, out_b, total, rounded, weight, sems = refs[7:]
+        copies = []
+        for low in range(0, start.shape[1], strip):
+            cols = slice(low, low + strip)
+            copy = pltpu.make_async_copy(
+                stored.at[slot, :, cols], weight.at[:, cols], sems.at[low // strip]
+            )
+            copy.start()
+            copies.append(copy)
+    width = start.shape[1]
+    edges = got_a.shape[0]
+    strength = jnp.log(jnp.float32(LAMBDA / (layer + 1.0)) + 1.0)
+    add_up(strip, local, got_a, got_b, far, start, total, rounded)
     for low in range(0, width, strip):
         cols = slice(low, low + strip)
+        if not prefetched:
+            copies[low // strip].wait()
         mixing = dot(rounded[...], weight[:, cols])
         fresh = jax.nn.relu((1.0 - strength) * total[:, cols] + strength * mixing).astype(BF)
         new[:, cols] = fresh
@@ -70,9 +148,10 @@
         ins += in_vmem(weight)
     else:
         ins.append(pltpu.with_memory_space_constraint(weight, pltpu.HBM))
-        scratch += [pltpu.VMEM(weight.shape[1:], BF), pltpu.SemaphoreType.DMA]
+        scratch += [pltpu.VMEM(weight.shape[1:], BF)]
+        scratch += [pltpu.SemaphoreType.DMA((width // min(256, width),))]
     return pl.pallas_call(
-        lambda *refs: finish_body(layer, min(256, width), prefetched, *refs),
+        lambda *refs: finish_body(layer, layer - EARLY, min(256, width), prefetched, *refs),
         out_shape=(
             pltpu.VMEM((rows, width), BF),
             pltpu.VMEM((edges, width), BF),
@@ -130,7 +209,18 @@
     rows = own_adj.shape[2]
     edge = send_ids.shape[2]
     kept = layers // segment_count
-    resident = lax.all_gather(weights, "graph", axis=1, tiled=True)
+    resident = lax.all_gather(weights[EARLY:], "graph", axis=1, tiled=True)
+
+    piece = width // (2 * segment_count)
+    wrows = weights.shape[1]
+    columns = weights[:EARLY].reshape(EARLY, wrows, 2, segment_count, piece)
+    quarter = lax.dynamic_index_in_dim(columns, segment_pos, 3, keepdims=False)
+    quarter = quarter.transpose(2, 1, 0, 3).reshape(1, 2, wrows, EARLY * piece)
+    spread = jnp.broadcast_to(quarter, (graph_count // 2, 2, wrows, EARLY * piece))
+    spread = spread.reshape(graph_count, wrows, EARLY * piece)
+    quarter = lax.all_to_all(spread, "graph", 0, 0, tiled=True).reshape(1, width, EARLY * piece)
+    spread = jnp.broadcast_to(quarter, (segment_count, width, EARLY * piece))
+    early = lax.all_to_all(spread, "segment", 0, 0, tiled=True)
 
     def partner(value):
         return lax.ppermute(value, "graph", [(p, p ^ 1) for p in range(graph_count)])
@@ -226,16 +316,23 @@
     sent = dot(picks, current).astype(BF)
     send_a, send_b = sent[: 3 * edge], sent[3 * edge :]
     (local,) = begin(None, current, near, hist_n, looked[0], None)
+    place = core.astype(jnp.int32).reshape(1)
     weight = resident
     own_rows = []
     for layer in range(layers):
+        got_b = exchange(send_b, 2)
         got_a = exchange(send_a, 0)
-        got_b = exchange(send_b, 2)
-        current, send_a, send_b = finish(
-            layer, local, got_a, got_b, far, picks, start, weight, layer > 0
-        )
+        if layer < EARLY:
+            mine = half_finish(layer, place, local, got_a, got_b, far, start, early)
+            current, send_a, send_b = join(place, mine, partner(mine), picks)
+        else:
+            current, send_a, send_b = finish(
+                layer, local, got_a, got_b, far, picks, start, weight, layer > EARLY
+            )
         if layer + 1 < layers:
-            local, weight = begin(layer + 1, current, near, hist_n, looked[layer + 1], resident)
+            brought = layer + 1 - EARLY if layer >= EARLY else None
+            out = begin(brought, current, near, hist_n, looked[layer + 1], resident)
+            local, weight = (out[0], resident) if brought is None else out
         own_rows.append(lax.dynamic_slice_in_dim(current, core * rows, rows, 0))
     whole = jnp.stack(own_rows)
     return lax.all_to_all(whole, "segment", 0, 1, tiled=True)

time: 250 us -> 237 us (0.948)
  waiting for transfers between devices: 93.5 us -> 56.3 us
  starting transfers between devices: 73.1 us -> 89.4 us
  local copies, waits for them, and re-layouts: 8.22 us -> 16.3 us
    all_gather x1, waiting for transfers between devices: 74.2 us -> 0.01 us  [shards(): resident = lax.all_gather(weights[EARLY:], 'graph', axis=1, tiled=True)]
    all_to_all x0 -> x2, waiting for transfers between devices: none -> 28.9 us  [the longest x1 16.8 us: shards(): lax.all_to_all(spread, 'graph', 0, 0, tiled=True)]
    all_to_all x0 -> x2, starting transfers between devices: none -> 21.8 us  [the longest x1 17.3 us: shards(): lax.all_to_all(spread, 'graph', 0, 0, tiled=True)]
    ppermute x16, starting transfers between devices: 64.4 us -> 55.1 us  [exchange(): return lax.ppermute(value, 'graph', pairs)]
    ppermute x16, waiting for transfers between devices: 18.6 us -> 25.2 us  [exchange(): return lax.ppermute(value, 'graph', pairs)]
    unnamed x23 -> x37, local copies, waits for them, and re-layouts: 1.74 us -> 5.85 us
    ppermute x4 -> x6, starting transfers between devices: 8.64 us -> 12.5 us  [partner(): lax.ppermute(value, 'graph', [(p, p ^ 1) for p in range(graph_count)])]
    pallas_call x8, Pallas kernels: 13.3 us -> 10.6 us  [begin(): pl.pallas_call(lambda *refs: begin_body(layer, min(256, width), *refs), o...]
  transfers between devices with their start and end apart: 21 -> 25, of which waited for: 9 -> 13; matrix products, arithmetic and copies ran while one was open for 4% -> 6% of each run, Pallas kernels for 5% -> 7%
where the time goes in v4:
time: 237 us; the launch traced here: 235 us
  starting transfers between devices  89.4 us (38%)
  waiting for transfers between devices  56.3 us (24%)
  Pallas kernels  30.1 us (13%)
  blocking collectives  23.4 us (10%)
  local copies, waits for them, and re-layouts  16.3 us (7%)
  between operations  14.2 us (6%)
  other arithmetic  4.65 us (2%)
    ppermute x16, starting transfers between devices, exchange(): return lax.ppermute(value, 'graph', pairs)  55.1 us
    ppermute x16, waiting for transfers between devices, exchange(): return lax.ppermute(value, 'graph', pairs)  25.2 us
    all_to_all x1, blocking collectives, shards(): return lax.all_to_all(whole, 'segment', 0, 1, tiled=True)  23.4 us
    all_to_all x1, starting transfers between devices, shards(): lax.all_to_all(spread, 'graph', 0, 0, tiled=True)  17.3 us
    all_to_all x1, waiting for transfers between devices, shards(): lax.all_to_all(spread, 'graph', 0, 0, tiled=True)  16.8 us
    pallas_call x6, Pallas kernels, finish(): pl.pallas_call(lambda *refs: finish_body(layer, layer - EARLY, min(256, w...  13.9 us
    ppermute x6, starting transfers between devices, partner(): lax.ppermute(value, 'graph', [(p, p ^ 1) for p in range(graph_count)])  12.5 us
    all_to_all x1, waiting for transfers between devices, shards(): early = lax.all_to_all(spread, 'segment', 0, 0, tiled=True)  12 us
  transfers between devices with their start and end apart: 25, of which 13 were waited for; matrix products, arithmetic and copies ran while one was open for 6% of the time, Pallas kernels for 7%

profile of v4, /device:TPU:32, one launch (start us, length us, event | category | flops | bytes accessed | tf_op | source)
XLA Modules:
  0.0 235.4 jit_solution(7941300998140827020)
XLA Ops:
  6.5 1.6 slice.122
  8.2 1.0 constant_dynamic-slice_fusion.4
  9.2 1.9 collective-permute-start
  12.5 0.8 dynamic-slice_bitcast_fusion
  13.3 2.4 %collective-permute-start.1 = (bf16[256,128]{1,0:T(8,128)(2,1)S(1)}, bf16[256,128]{1,0:T(8,128)(2,1)S(1)}, u32[]{:S(2)}, u32[]{:S(2)}) collective-permute-start(bf16[256,128]{1,0:T(8,128)(2,1)S(1)} %pad_maximum_fusion.2), channel_id=1, source_target_pairs={{0,1},{1,0},{2,3},{3,2},{4,5},{5,4},{6,7},{7,6},{8,9},{9,8},{10,11... | collective-permute-start | bytes 196616 | tf_op jit(solution)/shard_map/ppermute | solution.py:226
  17.3 1.9 collective-permute-start.2
  19.7 2.4 %collective-permute-start.3 = (bf16[8,64,1024]{2,1,0:T(8,128)(2,1)S(1)}, bf16[8,64,1024]{2,1,0:T(8,128)(2,1)}, u32[]{:S(2)}, u32[]{:S(2)}) collective-permute-start(bf16[8,64,1024]{2,1,0:T(8,128)(2,1)S(1)} %fusion), channel_id=1, source_target_pairs={{0,1},{1,0},{2,3},{3,2},{4,5},{5,4},{6,7},{7,6},{8,9},{9,8},{10,11... | collective-permute-start | bytes 3145736 | tf_op jit(solution)/shard_map/ppermute | solution.py:226
  22.1 0.8 broadcast_in_dim.12
  22.9 17.3 %all-to-all-start = ((bf16[128,8,256]{2,1,0:T(8,128)(2,1)}), bf16[128,8,256]{2,1,0:T(8,128)(2,1)S(1)}, u32[]{:S(2)}, u32[]{:S(2)}) async-start(bf16[128,8,256]{2,1,0:T(8,128)(2,1)} %bitcast.14), calls=%async_computation | async-start | bytes 1048576 | tf_op jit(solution)/shard_map/all_to_all | solution.py:221
  41.3 16.8 %all-to-all-done = bf16[128,8,256]{2,1,0:T(8,128)(2,1)S(1)} async-done(((bf16[128,8,256]{2,1,0:T(8,128)(2,1)}), bf16[128,8,256]{2,1,0:T(8,128)(2,1)S(1)}, u32[]{:S(2)}, u32[]{:S(2)}) %all-to-all-start) | async-done | bytes 524320 | tf_op jit(solution)/shard_map/all_to_all | solution.py:221
  58.1 1.5 broadcast_in_dim.14
  59.6 4.4 %all-to-all-start.1 = ((bf16[4,1024,256]{2,1,0:T(8,128)(2,1)}), bf16[4,1024,256]{2,1,0:T(8,128)(2,1)}, u32[]{:S(2)}, u32[]{:S(2)}) async-start(bf16[4,1024,256]{2,1,0:T(8,128)(2,1)} %broadcast_in_dim.14), calls=%async_computation.1 | async-start | bytes 4194304 | tf_op jit(solution)/shard_map/all_to_all | solution.py:223
  64.5 1.1 broadcast_select_fusion.3
  66.0 2.5 %collective-permute-start.4 = (bf16[48,1024]{1,0:T(8,128)(2,1)S(1)}, bf16[48,1024]{1,0:T(8,128)(2,1)S(1)}, u32[]{:S(2)}, u32[]{:S(2)}) collective-permute-start(bf16[48,1024]{1,0:T(8,128)(2,1)S(1)} %get-tuple-element.82), channel_id=1, source_target_pairs={{0,2},{2,0},{1,3},{3,1},{4,6},{6,4},{5,7},{7,5},{8,10},{10,8},{9,1... | collective-permute-start | bytes 294920 | tf_op jit(solution)/shard_map/ppermute | solution.py:233
  68.5 5.1 %collective-permute-start.5 = (bf16[48,1024]{1,0:T(8,128)(2,1)S(1)}, bf16[48,1024]{1,0:T(8,128)(2,1)S(1)}, u32[]{:S(2)}, u32[]{:S(2)}) collective-permute-start(bf16[48,1024]{1,0:T(8,128)(2,1)S(1)} %get-tuple-element.81), channel_id=1, source_target_pairs={{2,4},{4,2},{3,5},{5,3},{6,8},{8,6},{7,9},{9,7},{10,12},{12,10},{1... | collective-permute-start | bytes 294920 | tf_op jit(solution)/shard_map/ppermute | solution.py:233
  73.6 1.7 broadcast_select_fusion.1
  75.3 1.1 fusion.8
  76.8 1.9 collective-permute-done.5.refs_3_
  79.3 12.0 %all-to-all-done.1.refs_6_ = bf16[4,1024,256]{2,1,0:T(8,128)(2,1)} async-done(((bf16[4,1024,256]{2,1,0:T(8,128)(2,1)}), bf16[4,1024,256]{2,1,0:T(8,128)(2,1)}, u32[]{:S(2)}, u32[]{:S(2)}) %all-to-all-start.1) | async-done | bytes 2097184 | tf_op jit(solution)/shard_map/all_to_all | solution.py:223
  91.4 0.9 copy-done.9
  92.3 2.6 %half_finish.2.mine = bf16[256,512]{1,0:T(8,128)(2,1)S(1)} custom-call(s32[1]{0:T(128)} %bitcast.refs_0_.core, f32[256,1024]{1,0:T(8,128)S(1)} %begin.8.refs_1_, bf16[48,1024]{1,0:T(8,128)(2,1)S(1)} %collective-permute-done.4.refs_2_, bf16[48,1024]{1,0:T(8,128)(2,1)S(1)} %copy-done.9, bf16[256,96]{1,0:T(8,128)(2,1)S(1)} %copy.50.refs_4_.refs_3_, ...), custom_call_target="tpu_custom_call" | custom-call | tf_op jit(solution)/shard_map/half_finish/pallas_call | solution.py:65
  94.9 1.9 collective-permute-start.6
  96.8 1.5 collective-permute-done.6.theirs
  98.6 2.7 %collective-permute-start.7 = (bf16[48,1024]{1,0:T(8,128)(2,1)S(1)}, bf16[48,1024]{1,0:T(8,128)(2,1)S(1)}, u32[]{:S(2)}, u32[]{:S(2)}) collective-permute-start(bf16[48,1024]{1,0:T(8,128)(2,1)S(1)} %get-tuple-element.38), channel_id=1, source_target_pairs={{0,2},{2,0},{1,3},{3,1},{4,6},{6,4},{5,7},{7,5},{8,10},{10,8},{9,1... | collective-permute-start | bytes 294920 | tf_op jit(solution)/shard_map/ppermute | solution.py:233
  101.3 4.5 %collective-permute-start.8 = (bf16[48,1024]{1,0:T(8,128)(2,1)S(1)}, bf16[48,1024]{1,0:T(8,128)(2,1)S(1)}, u32[]{:S(2)}, u32[]{:S(2)}) collective-permute-start(bf16[48,1024]{1,0:T(8,128)(2,1)S(1)} %get-tuple-element.39), channel_id=1, source_target_pairs={{2,4},{4,2},{3,5},{5,3},{6,8},{8,6},{7,9},{9,7},{10,12},{12,10},{1... | collective-permute-start | bytes 294920 | tf_op jit(solution)/shard_map/ppermute | solution.py:233
  106.2 1.5 collective-permute-done.7.refs_2_
  107.7 3.4 %collective-permute-done.8.refs_3_ = bf16[48,1024]{1,0:T(8,128)(2,1)S(1)} collective-permute-done((bf16[48,1024]{1,0:T(8,128)(2,1)S(1)}, bf16[48,1024]{1,0:T(8,128)(2,1)S(1)}, u32[]{:S(2)}, u32[]{:S(2)}) %collective-permute-start.8) | collective-permute-done | bytes 98336 | tf_op jit(solution)/shard_map/ppermute | solution.py:233
  111.1 2.5 %half_finish.3.mine = bf16[256,512]{1,0:T(8,128)(2,1)S(1)} custom-call(s32[1]{0:T(128)} %bitcast.refs_0_.core, f32[256,1024]{1,0:T(8,128)S(1)} %begin.9.refs_1_, bf16[48,1024]{1,0:T(8,128)(2,1)S(1)} %collective-permute-done.7.refs_2_, bf16[48,1024]{1,0:T(8,128)(2,1)S(1)} %collective-permute-done.8.refs_3_, bf16[256,96]{1,0:T(8,128)(2,1)S(1)} %copy.50.refs_4_.refs_3_, ...), custom_call_target="tpu_custom_call" | custom-call | tf_op jit(solution)/shard_map/half_finish/pallas_call | solution.py:65
  113.6 1.9 collective-permute-start.9
  116.3 0.8 collective-permute-done.9.theirs
  117.3 1.9 collective-permute-start.10
  119.2 4.8 %collective-permute-start.11 = (bf16[48,1024]{1,0:T(8,128)(2,1)S(1)}, bf16[48,1024]{1,0:T(8,128)(2,1)S(1)}, u32[]{:S(2)}, u32[]{:S(2)}) collective-permute-start(bf16[48,1024]{1,0:T(8,128)(2,1)S(1)} %get-tuple-element.42), channel_id=1, source_target_pairs={{2,4},{4,2},{3,5},{5,3},{6,8},{8,6},{7,9},{9,7},{10,12},{12,10},{1... | collective-permute-start | bytes 294920 | tf_op jit(solution)/shard_map/ppermute | solution.py:233
  124.0 0.9 copy-done.4
  125.4 0.7 bitcast_dynamic-update-slice_fusion.6
  126.1 3.2 %collective-permute-done.11.refs_2_ = bf16[48,1024]{1,0:T(8,128)(2,1)S(1)} collective-permute-done((bf16[48,1024]{1,0:T(8,128)(2,1)S(1)}, bf16[48,1024]{1,0:T(8,128)(2,1)S(1)}, u32[]{:S(2)}, u32[]{:S(2)}) %collective-permute-start.11) | collective-permute-done | bytes 98336 | tf_op jit(solution)/shard_map/ppermute | solution.py:233
  129.9 0.9 copy-done.7
  130.8 3.4 %finish.6 = (bf16[256,1024]{1,0:T(8,128)(2,1)S(1)}, bf16[48,1024]{1,0:T(8,128)(2,1)S(1)}, bf16[48,1024]{1,0:T(8,128)(2,1)S(1)}) custom-call(f32[256,1024]{1,0:T(8,128)S(1)} %begin.10.refs_0_, bf16[48,1024]{1,0:T(8,128)(2,1)S(1)} %collective-permute-done.10.refs_1_, bf16[48,1024]{1,0:T(8,128)(2,1)S(1)} %copy-done.7, ...), custom_call_target="tpu_custom_call" | custom-call | tf_op jit(solution)/shard_map/finish/pallas_call | solution.py:153
  134.2 1.9 collective-permute-start.12
  136.1 4.8 %collective-permute-start.13 = (bf16[48,1024]{1,0:T(8,128)(2,1)S(1)}, bf16[48,1024]{1,0:T(8,128)(2,1)S(1)}, u32[]{:S(2)}, u32[]{:S(2)}) collective-permute-start(bf16[48,1024]{1,0:T(8,128)(2,1)S(1)} %get-tuple-element.46), channel_id=1, source_target_pairs={{2,4},{4,2},{3,5},{5,3},{6,8},{8,6},{7,9},{9,7},{10,12},{12,10},{1... | collective-permute-start | bytes 294920 | tf_op jit(solution)/shard_map/ppermute | solution.py:233
  140.9 2.0 begin.11
  143.2 2.8 %collective-permute-done.13.refs_2_ = bf16[48,1024]{1,0:T(8,128)(2,1)S(1)} collective-permute-done((bf16[48,1024]{1,0:T(8,128)(2,1)S(1)}, bf16[48,1024]{1,0:T(8,128)(2,1)S(1)}, u32[]{:S(2)}, u32[]{:S(2)}) %collective-permute-start.13) | collective-permute-done | bytes 98336 | tf_op jit(solution)/shard_map/ppermute | solution.py:233
  146.0 2.0 finish.7
  147.9 1.9 collective-permute-start.14
  149.9 4.9 %collective-permute-start.15 = (bf16[48,1024]{1,0:T(8,128)(2,1)S(1)}, bf16[48,1024]{1,0:T(8,128)(2,1)S(1)}, u32[]{:S(2)}, u32[]{:S(2)}) collective-permute-start(bf16[48,1024]{1,0:T(8,128)(2,1)S(1)} %get-tuple-element.51), channel_id=1, source_target_pairs={{2,4},{4,2},{3,5},{5,3},{6,8},{8,6},{7,9},{9,7},{10,12},{12,10},{1... | collective-permute-start | bytes 294920 | tf_op jit(solution)/shard_map/ppermute | solution.py:233
  154.8 1.8 begin.12
  156.7 3.0 %collective-permute-done.15.refs_2_ = bf16[48,1024]{1,0:T(8,128)(2,1)S(1)} collective-permute-done((bf16[48,1024]{1,0:T(8,128)(2,1)S(1)}, bf16[48,1024]{1,0:T(8,128)(2,1)S(1)}, u32[]{:S(2)}, u32[]{:S(2)}) %collective-permute-start.15) | collective-permute-done | bytes 98336 | tf_op jit(solution)/shard_map/ppermute | solution.py:233
  159.7 2.0 finish.8
  161.7 1.9 collective-permute-start.16
  163.6 4.8 %collective-permute-start.17 = (bf16[48,1024]{1,0:T(8,128)(2,1)S(1)}, bf16[48,1024]{1,0:T(8,128)(2,1)S(1)}, u32[]{:S(2)}, u32[]{:S(2)}) collective-permute-start(bf16[48,1024]{1,0:T(8,128)(2,1)S(1)} %get-tuple-element.56), channel_id=1, source_target_pairs={{2,4},{4,2},{3,5},{5,3},{6,8},{8,6},{7,9},{9,7},{10,12},{12,10},{1... | collective-permute-start | bytes 294920 | tf_op jit(solution)/shard_map/ppermute | solution.py:233
  168.4 1.8 begin.13
  170.3 3.2 %collective-permute-done.17.refs_2_ = bf16[48,1024]{1,0:T(8,128)(2,1)S(1)} collective-permute-done((bf16[48,1024]{1,0:T(8,128)(2,1)S(1)}, bf16[48,1024]{1,0:T(8,128)(2,1)S(1)}, u32[]{:S(2)}, u32[]{:S(2)}) %collective-permute-start.17) | collective-permute-done | bytes 98336 | tf_op jit(solution)/shard_map/ppermute | solution.py:233
  173.4 2.0 finish.9
  175.4 1.9 collective-permute-start.18
  177.4 4.8 %collective-permute-start.19 = (bf16[48,1024]{1,0:T(8,128)(2,1)S(1)}, bf16[48,1024]{1,0:T(8,128)(2,1)S(1)}, u32[]{:S(2)}, u32[]{:S(2)}) collective-permute-start(bf16[48,1024]{1,0:T(8,128)(2,1)S(1)} %get-tuple-element.61), channel_id=1, source_target_pairs={{2,4},{4,2},{3,5},{5,3},{6,8},{8,6},{7,9},{9,7},{10,12},{12,10},{1... | collective-permute-start | bytes 294920 | tf_op jit(solution)/shard_map/ppermute | solution.py:233
  182.1 1.8 begin.14
  184.0 3.2 %collective-permute-done.19.refs_2_ = bf16[48,1024]{1,0:T(8,128)(2,1)S(1)} collective-permute-done((bf16[48,1024]{1,0:T(8,128)(2,1)S(1)}, bf16[48,1024]{1,0:T(8,128)(2,1)S(1)}, u32[]{:S(2)}, u32[]{:S(2)}) %collective-permute-start.19) | collective-permute-done | bytes 98336 | tf_op jit(solution)/shard_map/ppermute | solution.py:233
  187.2 2.0 finish.10
  189.2 1.9 collective-permute-start.20
  191.1 4.8 %collective-permute-start.21 = (bf16[48,1024]{1,0:T(8,128)(2,1)S(1)}, bf16[48,1024]{1,0:T(8,128)(2,1)S(1)}, u32[]{:S(2)}, u32[]{:S(2)}) collective-permute-start(bf16[48,1024]{1,0:T(8,128)(2,1)S(1)} %get-tuple-element.66), channel_id=1, source_target_pairs={{2,4},{4,2},{3,5},{5,3},{6,8},{8,6},{7,9},{9,7},{10,12},{12,10},{1... | collective-permute-start | bytes 294920 | tf_op jit(solution)/shard_map/ppermute | solution.py:233
  195.9 1.8 begin.15
  197.8 3.2 %collective-permute-done.21.refs_2_ = bf16[48,1024]{1,0:T(8,128)(2,1)S(1)} collective-permute-done((bf16[48,1024]{1,0:T(8,128)(2,1)S(1)}, bf16[48,1024]{1,0:T(8,128)(2,1)S(1)}, u32[]{:S(2)}, u32[]{:S(2)}) %collective-permute-start.21) | collective-permute-done | bytes 98336 | tf_op jit(solution)/shard_map/ppermute | solution.py:233
  200.9 2.6 %finish.11 = (bf16[256,1024]{1,0:T(8,128)(2,1)S(1)}, bf16[48,1024]{1,0:T(8,128)(2,1)}, bf16[48,1024]{1,0:T(8,128)(2,1)}) custom-call(f32[256,1024]{1,0:T(8,128)S(1)} %get-tuple-element.64.refs_0_, bf16[48,1024]{1,0:T(8,128)(2,1)S(1)} %collective-permute-done.20.refs_1_, bf16[48,1024]{1,0:T(8,128)(2,1)S(1)} %collective-permute-done.21.refs_2_, ...), custom_call_target="tpu_custom_call" | custom-call | tf_op jit(solution)/shard_map/finish/pallas_call | solution.py:153
  203.6 23.4 %all_to_all.28 = bf16[8,128,1024]{2,1,0:T(8,128)(2,1)S(1)} all-to-all(bf16[8,128,1024]{2,1,0:T(8,128)(2,1)S(1)} %bitcast_dynamic-update-slice_fusion), channel_id=1, replica_groups=mesh['segment'=4,'graph'=128] {'segment'}, dimensions={0} | all-to-all | bytes 4194304 | tf_op jit(solution)/shard_map/all_to_all | solution.py:338
  227.0 1.5 copy.65
  (92 shorter events, 9.3 us)
Async XLA Ops:
  6.5 12.6 %copy-start = (bf16[8,64,1024]{2,1,0:T(8,128)(2,1)S(1)}, bf16[8,64,1024]{2,1,0:T(8,128)(2,1)}, u32[]{:S(2)}) copy-start(bf16[8,64,1024]{2,1,0:T(8,128)(2,1)} %param.10) | copy-start | bytes 3145732
  6.5 15.5 %slice-start = ((bf16[8,8,1024]{2,1,0:T(8,128)(2,1)}), bf16[2,8,1024]{2,1,0:T(8,128)(2,1)S(1)}, s32[]{:S(2)}) async-start(bf16[8,8,1024]{2,1,0:T(8,128)(2,1)} %param.9), calls=%async_computation.4 | async-start | bytes 65536 | tf_op jit(solution)/shard_map/slice | solution.py:216
  6.5 123.4 %all-gather.2.cloned.1.call-start = ((), (), s32[]{:S(2)}) async-start(), calls=%async_computation.3 | async-start | bytes 12681216 | tf_op jit(solution)/shard_map/all_gather | solution.py:212
  9.2 55.4 %collective-permute-start = (bf16[128,1024]{1,0:T(8,128)(2,1)S(1)}, bf16[128,1024]{1,0:T(8,128)(2,1)}, u32[]{:S(2)}, u32[]{:S(2)}) collective-permute-start(bf16[128,1024]{1,0:T(8,128)(2,1)S(1)} %constant_dynamic-slice_fusion.4), channel_id=1, source_target_pairs={{0,1},{1,0},{2,3},{3,2},{4,5},{5,4},{6,7},{7,6},{8,9},{9,8},{10,11... | collective-permute-start | bytes 786440 | tf_op jit(solution)/shard_map/ppermute | solution.py:226
  13.3 27.7 %collective-permute-start.1 = (bf16[256,128]{1,0:T(8,128)(2,1)S(1)}, bf16[256,128]{1,0:T(8,128)(2,1)S(1)}, u32[]{:S(2)}, u32[]{:S(2)}) collective-permute-start(bf16[256,128]{1,0:T(8,128)(2,1)S(1)} %pad_maximum_fusion.2), channel_id=1, source_target_pairs={{0,1},{1,0},{2,3},{3,2},{4,5},{5,4},{6,7},{7,6},{8,9},{9,8},{10,11... | collective-permute-start | bytes 196616 | tf_op jit(solution)/shard_map/ppermute | solution.py:226
  17.3 23.1 %collective-permute-start.2 = (s32[128]{0:T(128)S(1)}, s32[128]{0:T(128)S(1)}, u32[]{:S(2)}, u32[]{:S(2)}) collective-permute-start(s32[128]{0:T(128)S(1)} %pad_add_fusion.4), channel_id=1, source_target_pairs={{0,1},{1,0},{2,3},{3,2},{4,5},{5,4},{6,7},{7,6},{8,9},{9,8},{10,11... | collective-permute-start | bytes 1544 | tf_op jit(solution)/shard_map/ppermute | solution.py:226
  19.7 54.0 %collective-permute-start.3 = (bf16[8,64,1024]{2,1,0:T(8,128)(2,1)S(1)}, bf16[8,64,1024]{2,1,0:T(8,128)(2,1)}, u32[]{:S(2)}, u32[]{:S(2)}) collective-permute-start(bf16[8,64,1024]{2,1,0:T(8,128)(2,1)S(1)} %fusion), channel_id=1, source_target_pairs={{0,1},{1,0},{2,3},{3,2},{4,5},{5,4},{6,7},{7,6},{8,9},{9,8},{10,11... | collective-permute-start | bytes 3145736 | tf_op jit(solution)/shard_map/ppermute | solution.py:226
  22.9 35.2 %all-to-all-start = ((bf16[128,8,256]{2,1,0:T(8,128)(2,1)}), bf16[128,8,256]{2,1,0:T(8,128)(2,1)S(1)}, u32[]{:S(2)}, u32[]{:S(2)}) async-start(bf16[128,8,256]{2,1,0:T(8,128)(2,1)} %bitcast.14), calls=%async_computation | async-start | bytes 1048576 | tf_op jit(solution)/shard_map/all_to_all | solution.py:221
  41.0 24.7 %copy-start.11 = (bf16[48,256]{1,0:T(8,128)(2,1)}, bf16[48,256]{1,0:T(8,128)(2,1)S(1)}, u32[]{:S(2)}) copy-start(bf16[48,256]{1,0:T(8,128)(2,1)S(1)} %get-tuple-element.93) | copy-start | bytes 73732
  41.0 24.7 %copy-start.13 = (bf16[48,256]{1,0:T(8,128)(2,1)}, bf16[48,256]{1,0:T(8,128)(2,1)S(1)}, u32[]{:S(2)}) copy-start(bf16[48,256]{1,0:T(8,128)(2,1)S(1)} %get-tuple-element.94) | copy-start | bytes 73732
  59.6 31.8 %all-to-all-start.1 = ((bf16[4,1024,256]{2,1,0:T(8,128)(2,1)}), bf16[4,1024,256]{2,1,0:T(8,128)(2,1)}, u32[]{:S(2)}, u32[]{:S(2)}) async-start(bf16[4,1024,256]{2,1,0:T(8,128)(2,1)} %broadcast_in_dim.14), calls=%async_computation.1 | async-start | bytes 4194304 | tf_op jit(solution)/shard_map/all_to_all | solution.py:223
  66.0 10.8 %collective-permute-start.4 = (bf16[48,1024]{1,0:T(8,128)(2,1)S(1)}, bf16[48,1024]{1,0:T(8,128)(2,1)S(1)}, u32[]{:S(2)}, u32[]{:S(2)}) collective-permute-start(bf16[48,1024]{1,0:T(8,128)(2,1)S(1)} %get-tuple-element.82), channel_id=1, source_target_pairs={{0,2},{2,0},{1,3},{3,1},{4,6},{6,4},{5,7},{7,5},{8,10},{10,8},{9,1... | collective-permute-start | bytes 294920 | tf_op jit(solution)/shard_map/ppermute | solution.py:233
  68.5 10.2 %collective-permute-start.5 = (bf16[48,1024]{1,0:T(8,128)(2,1)S(1)}, bf16[48,1024]{1,0:T(8,128)(2,1)S(1)}, u32[]{:S(2)}, u32[]{:S(2)}) collective-permute-start(bf16[48,1024]{1,0:T(8,128)(2,1)S(1)} %get-tuple-element.81), channel_id=1, source_target_pairs={{2,4},{4,2},{3,5},{5,3},{6,8},{8,6},{7,9},{9,7},{10,12},{12,10},{1... | collective-permute-start | bytes 294920 | tf_op jit(solution)/shard_map/ppermute | solution.py:233
  78.7 0.6 copy-start.8
  91.4 0.9 copy-start.9
  92.3 4.5 %copy-start.12 = (bf16[48,256]{1,0:T(8,128)(2,1)S(1)}, bf16[48,256]{1,0:T(8,128)(2,1)}, u32[]{:S(2)}) copy-start(bf16[48,256]{1,0:T(8,128)(2,1)} %copy-done.11) | copy-start | bytes 73732
  92.3 4.5 %copy-start.14 = (bf16[48,256]{1,0:T(8,128)(2,1)S(1)}, bf16[48,256]{1,0:T(8,128)(2,1)}, u32[]{:S(2)}) copy-start(bf16[48,256]{1,0:T(8,128)(2,1)} %copy-done.13) | copy-start | bytes 73732
  92.3 13.5 %copy-start.5 = (bf16[128,1024]{1,0:T(8,128)(2,1)S(1)}, bf16[128,1024]{1,0:T(8,128)(2,1)}, u32[]{:S(2)}) copy-start(bf16[128,1024]{1,0:T(8,128)(2,1)} %get-tuple-element.71.refs_3_) | copy-start | bytes 786436
  94.9 3.4 %collective-permute-start.6 = (bf16[256,512]{1,0:T(8,128)(2,1)S(1)}, bf16[256,512]{1,0:T(8,128)(2,1)S(1)}, u32[]{:S(2)}, u32[]{:S(2)}) collective-permute-start(bf16[256,512]{1,0:T(8,128)(2,1)S(1)} %half_finish.2.mine), channel_id=1, source_target_pairs={{0,1},{1,0},{2,3},{3,2},{4,5},{5,4},{6,7},{7,6},{8,9},{9,8},{10,11... | collective-permute-start | bytes 786440 | tf_op jit(solution)/shard_map/ppermute | solution.py:226
  98.6 9.2 %collective-permute-start.7 = (bf16[48,1024]{1,0:T(8,128)(2,1)S(1)}, bf16[48,1024]{1,0:T(8,128)(2,1)S(1)}, u32[]{:S(2)}, u32[]{:S(2)}) collective-permute-start(bf16[48,1024]{1,0:T(8,128)(2,1)S(1)} %get-tuple-element.38), channel_id=1, source_target_pairs={{0,2},{2,0},{1,3},{3,1},{4,6},{6,4},{5,7},{7,5},{8,10},{10,8},{9,1... | collective-permute-start | bytes 294920 | tf_op jit(solution)/shard_map/ppermute | solution.py:233
  101.3 9.8 %collective-permute-start.8 = (bf16[48,1024]{1,0:T(8,128)(2,1)S(1)}, bf16[48,1024]{1,0:T(8,128)(2,1)S(1)}, u32[]{:S(2)}, u32[]{:S(2)}) collective-permute-start(bf16[48,1024]{1,0:T(8,128)(2,1)S(1)} %get-tuple-element.39), channel_id=1, source_target_pairs={{2,4},{4,2},{3,5},{5,3},{6,8},{8,6},{7,9},{9,7},{10,12},{12,10},{1... | collective-permute-start | bytes 294920 | tf_op jit(solution)/shard_map/ppermute | solution.py:233
  113.6 3.4 %collective-permute-start.9 = (bf16[256,512]{1,0:T(8,128)(2,1)S(1)}, bf16[256,512]{1,0:T(8,128)(2,1)S(1)}, u32[]{:S(2)}, u32[]{:S(2)}) collective-permute-start(bf16[256,512]{1,0:T(8,128)(2,1)S(1)} %half_finish.3.mine), channel_id=1, source_target_pairs={{0,1},{1,0},{2,3},{3,2},{4,5},{5,4},{6,7},{7,6},{8,9},{9,8},{10,11... | collective-permute-start | bytes 786440 | tf_op jit(solution)/shard_map/ppermute | solution.py:226
  117.3 8.8 %collective-permute-start.10 = (bf16[48,1024]{1,0:T(8,128)(2,1)S(1)}, bf16[48,1024]{1,0:T(8,128)(2,1)S(1)}, u32[]{:S(2)}, u32[]{:S(2)}) collective-permute-start(bf16[48,1024]{1,0:T(8,128)(2,1)S(1)} %get-tuple-element.41), channel_id=1, source_target_pairs={{0,2},{2,0},{1,3},{3,1},{4,6},{6,4},{5,7},{7,5},{8,10},{10,8},{9,1... | collective-permute-start | bytes 294920 | tf_op jit(solution)/shard_map/ppermute | solution.py:233
  119.2 10.0 %collective-permute-start.11 = (bf16[48,1024]{1,0:T(8,128)(2,1)S(1)}, bf16[48,1024]{1,0:T(8,128)(2,1)S(1)}, u32[]{:S(2)}, u32[]{:S(2)}) collective-permute-start(bf16[48,1024]{1,0:T(8,128)(2,1)S(1)} %get-tuple-element.42), channel_id=1, source_target_pairs={{2,4},{4,2},{3,5},{5,3},{6,8},{8,6},{7,9},{9,7},{10,12},{12,10},{1... | collective-permute-start | bytes 294920 | tf_op jit(solution)/shard_map/ppermute | solution.py:233
  124.0 1.0 copy-start.4
  129.3 0.6 copy-start.6
  129.9 0.9 copy-start.7
  130.8 10.1 %copy-start.3 = (bf16[128,1024]{1,0:T(8,128)(2,1)S(1)}, bf16[128,1024]{1,0:T(8,128)(2,1)}, u32[]{:S(2)}) copy-start(bf16[128,1024]{1,0:T(8,128)(2,1)} %get-tuple-element.73.refs_3_) | copy-start | bytes 786436
  134.2 9.0 %collective-permute-start.12 = (bf16[48,1024]{1,0:T(8,128)(2,1)S(1)}, bf16[48,1024]{1,0:T(8,128)(2,1)S(1)}, u32[]{:S(2)}, u32[]{:S(2)}) collective-permute-start(bf16[48,1024]{1,0:T(8,128)(2,1)S(1)} %get-tuple-element.45), channel_id=1, source_target_pairs={{0,2},{2,0},{1,3},{3,1},{4,6},{6,4},{5,7},{7,5},{8,10},{10,8},{9,1... | collective-permute-start | bytes 294920 | tf_op jit(solution)/shard_map/ppermute | solution.py:233
  136.1 9.8 %collective-permute-start.13 = (bf16[48,1024]{1,0:T(8,128)(2,1)S(1)}, bf16[48,1024]{1,0:T(8,128)(2,1)S(1)}, u32[]{:S(2)}, u32[]{:S(2)}) collective-permute-start(bf16[48,1024]{1,0:T(8,128)(2,1)S(1)} %get-tuple-element.46), channel_id=1, source_target_pairs={{2,4},{4,2},{3,5},{5,3},{6,8},{8,6},{7,9},{9,7},{10,12},{12,10},{1... | collective-permute-start | bytes 294920 | tf_op jit(solution)/shard_map/ppermute | solution.py:233
  140.9 2.2 copy-start.10
  143.2 11.7 %copy-start.2 = (bf16[128,1024]{1,0:T(8,128)(2,1)S(1)}, bf16[128,1024]{1,0:T(8,128)(2,1)}, u32[]{:S(2)}) copy-start(bf16[128,1024]{1,0:T(8,128)(2,1)} %get-tuple-element.74.refs_3_) | copy-start | bytes 786436
  147.9 8.8 %collective-permute-start.14 = (bf16[48,1024]{1,0:T(8,128)(2,1)S(1)}, bf16[48,1024]{1,0:T(8,128)(2,1)S(1)}, u32[]{:S(2)}, u32[]{:S(2)}) collective-permute-start(bf16[48,1024]{1,0:T(8,128)(2,1)S(1)} %get-tuple-element.50), channel_id=1, source_target_pairs={{0,2},{2,0},{1,3},{3,1},{4,6},{6,4},{5,7},{7,5},{8,10},{10,8},{9,1... | collective-permute-start | bytes 294920 | tf_op jit(solution)/shard_map/ppermute | solution.py:233
  149.9 9.8 %collective-permute-start.15 = (bf16[48,1024]{1,0:T(8,128)(2,1)S(1)}, bf16[48,1024]{1,0:T(8,128)(2,1)S(1)}, u32[]{:S(2)}, u32[]{:S(2)}) collective-permute-start(bf16[48,1024]{1,0:T(8,128)(2,1)S(1)} %get-tuple-element.51), channel_id=1, source_target_pairs={{2,4},{4,2},{3,5},{5,3},{6,8},{8,6},{7,9},{9,7},{10,12},{12,10},{1... | collective-permute-start | bytes 294920 | tf_op jit(solution)/shard_map/ppermute | solution.py:233
  156.7 11.7 %copy-start.1 = (bf16[128,1024]{1,0:T(8,128)(2,1)S(1)}, bf16[128,1024]{1,0:T(8,128)(2,1)}, u32[]{:S(2)}) copy-start(bf16[128,1024]{1,0:T(8,128)(2,1)} %get-tuple-element.75.refs_3_) | copy-start | bytes 786436
  161.7 8.6 %collective-permute-start.16 = (bf16[48,1024]{1,0:T(8,128)(2,1)S(1)}, bf16[48,1024]{1,0:T(8,128)(2,1)S(1)}, u32[]{:S(2)}, u32[]{:S(2)}) collective-permute-start(bf16[48,1024]{1,0:T(8,128)(2,1)S(1)} %get-tuple-element.55), channel_id=1, source_target_pairs={{0,2},{2,0},{1,3},{3,1},{4,6},{6,4},{5,7},{7,5},{8,10},{10,8},{9,1... | collective-permute-start | bytes 294920 | tf_op jit(solution)/shard_map/ppermute | solution.py:233
  163.6 9.8 %collective-permute-start.17 = (bf16[48,1024]{1,0:T(8,128)(2,1)S(1)}, bf16[48,1024]{1,0:T(8,128)(2,1)S(1)}, u32[]{:S(2)}, u32[]{:S(2)}) collective-permute-start(bf16[48,1024]{1,0:T(8,128)(2,1)S(1)} %get-tuple-element.56), channel_id=1, source_target_pairs={{2,4},{4,2},{3,5},{5,3},{6,8},{8,6},{7,9},{9,7},{10,12},{12,10},{1... | collective-permute-start | bytes 294920 | tf_op jit(solution)/shard_map/ppermute | solution.py:233
  175.4 8.6 %collective-permute-start.18 = (bf16[48,1024]{1,0:T(8,128)(2,1)S(1)}, bf16[48,1024]{1,0:T(8,128)(2,1)S(1)}, u32[]{:S(2)}, u32[]{:S(2)}) collective-permute-start(bf16[48,1024]{1,0:T(8,128)(2,1)S(1)} %get-tuple-element.60), channel_id=1, source_target_pairs={{0,2},{2,0},{1,3},{3,1},{4,6},{6,4},{5,7},{7,5},{8,10},{10,8},{9,1... | collective-permute-start | bytes 294920 | tf_op jit(solution)/shard_map/ppermute | solution.py:233
  177.4 9.8 %collective-permute-start.19 = (bf16[48,1024]{1,0:T(8,128)(2,1)S(1)}, bf16[48,1024]{1,0:T(8,128)(2,1)S(1)}, u32[]{:S(2)}, u32[]{:S(2)}) collective-permute-start(bf16[48,1024]{1,0:T(8,128)(2,1)S(1)} %get-tuple-element.61), channel_id=1, source_target_pairs={{2,4},{4,2},{3,5},{5,3},{6,8},{8,6},{7,9},{9,7},{10,12},{12,10},{1... | collective-permute-start | bytes 294920 | tf_op jit(solution)/shard_map/ppermute | solution.py:233
  189.2 8.6 %collective-permute-start.20 = (bf16[48,1024]{1,0:T(8,128)(2,1)S(1)}, bf16[48,1024]{1,0:T(8,128)(2,1)S(1)}, u32[]{:S(2)}, u32[]{:S(2)}) collective-permute-start(bf16[48,1024]{1,0:T(8,128)(2,1)S(1)} %get-tuple-element.65), channel_id=1, source_target_pairs={{0,2},{2,0},{1,3},{3,1},{4,6},{6,4},{5,7},{7,5},{8,10},{10,8},{9,1... | collective-permute-start | bytes 294920 | tf_op jit(solution)/shard_map/ppermute | solution.py:233
  191.1 9.8 %collective-permute-start.21 = (bf16[48,1024]{1,0:T(8,128)(2,1)S(1)}, bf16[48,1024]{1,0:T(8,128)(2,1)S(1)}, u32[]{:S(2)}, u32[]{:S(2)}) collective-permute-start(bf16[48,1024]{1,0:T(8,128)(2,1)S(1)} %get-tuple-element.66), channel_id=1, source_target_pairs={{2,4},{4,2},{3,5},{5,3},{6,8},{8,6},{7,9},{9,7},{10,12},{12,10},{1... | collective-permute-start | bytes 294920 | tf_op jit(solution)/shard_map/ppermute | solution.py:233
Sparse Core Ops, SparseCore 0:
  10.6 100.0 all-gather.1

commit v5 on v4

--- a/solution.py
+++ b/solution.py
@@ -46,13 +46,12 @@
 def half_body(layer, strip, core, local, got_a, got_b, far, start, early, out, total, rounded):
     strength = jnp.log(jnp.float32(LAMBDA / (layer + 1.0)) + 1.0)
     add_up(strip, local, got_a, got_b, far, start, total, rounded)
-    parts, _, wide = early.shape
-    piece = wide // EARLY
+    parts, _, piece = early.shape
     half = parts * piece
     low_half = core[0] == 0
     for part in range(parts):
         low = part * piece
-        mixing = dot(rounded[...], early[part, :, layer * piece : (layer + 1) * piece])
+        mixing = dot(rounded[...], early[part])
         support = jnp.where(
             low_half, total[:, low : low + piece], total[:, half + low : half + low + piece]
         )
@@ -109,28 +108,13 @@
     )(core, *in_vmem(mine, theirs, picks))
 
 
-def finish_body(layer, slot, strip, prefetched, *refs):
-    if prefetched:
-        local, got_a, got_b, far, picks, start, weight, new, out_a, out_b, total, rounded = refs
-    else:
-        local, got_a, got_b, far, picks, start, stored = refs[:7]
-        new, out_a, out_b, total, rounded, weight, sems = refs[7:]
-        copies = []
-        for low in range(0, start.shape[1], strip):
-            cols = slice(low, low + strip)
-            copy = pltpu.make_async_copy(
-                stored.at[slot, :, cols], weight.at[:, cols], sems.at[low // strip]
-            )
-            copy.start()
-            copies.append(copy)
-    width = start.shape[1]
+def finish_body(layer, strip, *refs):
+    local, got_a, got_b, far, picks, start, weight, new, out_a, out_b, total, rounded = refs
     edges = got_a.shape[0]
     strength = jnp.log(jnp.float32(LAMBDA / (layer + 1.0)) + 1.0)
     add_up(strip, local, got_a, got_b, far, start, total, rounded)
-    for low in range(0, width, strip):
+    for low in range(0, start.shape[1], strip):
         cols = slice(low, low + strip)
-        if not prefetched:
-            copies[low // strip].wait()
         mixing = dot(rounded[...], weight[:, cols])
         fresh = jax.nn.relu((1.0 - strength) * total[:, cols] + strength * mixing).astype(BF)
         new[:, cols] = fresh
@@ -139,30 +123,22 @@
         out_b[:, cols] = sent[edges:]
 
 
-def finish(layer, local, got_a, got_b, far, picks, start, weight, prefetched):
+def finish(layer, local, got_a, got_b, far, picks, start, weight):
     rows, width = start.shape
     edges = got_a.shape[0]
-    ins = in_vmem(local, got_a, got_b, far, picks, start)
-    scratch = [pltpu.VMEM((rows, width), F32), pltpu.VMEM((rows, width), BF)]
-    if prefetched:
-        ins += in_vmem(weight)
-    else:
-        ins.append(pltpu.with_memory_space_constraint(weight, pltpu.HBM))
-        scratch += [pltpu.VMEM(weight.shape[1:], BF)]
-        scratch += [pltpu.SemaphoreType.DMA((width // min(256, width),))]
     return pl.pallas_call(
-        lambda *refs: finish_body(layer, layer - EARLY, min(256, width), prefetched, *refs),
+        lambda *refs: finish_body(layer, min(256, width), *refs),
         out_shape=(
             pltpu.VMEM((rows, width), BF),
             pltpu.VMEM((edges, width), BF),
             pltpu.VMEM((edges, width), BF),
         ),
-        in_specs=[VM] * 6 + [VM if prefetched else HB],
+        in_specs=[VM] * 7,
         out_specs=(VM, VM, VM),
-        scratch_shapes=scratch,
-        compiler_params=pltpu.CompilerParams(vmem_limit_bytes=10 << 20),
+        scratch_shapes=[pltpu.VMEM((rows, width), F32), pltpu.VMEM((rows, width), BF)],
+        compiler_params=pltpu.CompilerParams(vmem_limit_bytes=6 << 20),
         name="finish",
-    )(*ins)
+    )(*in_vmem(local, got_a, got_b, far, picks, start, weight))
 
 
 def begin_body(layer, strip, *refs):
@@ -208,7 +184,6 @@
     layers, _, width = weights.shape
     rows = own_adj.shape[2]
     edge = send_ids.shape[2]
-    kept = layers // segment_count
     resident = lax.all_gather(weights[EARLY:], "graph", axis=1, tiled=True)
 
     piece = width // (2 * segment_count)
@@ -219,10 +194,15 @@
     spread = jnp.broadcast_to(quarter, (graph_count // 2, 2, wrows, EARLY * piece))
     spread = spread.reshape(graph_count, wrows, EARLY * piece)
     quarter = lax.all_to_all(spread, "graph", 0, 0, tiled=True).reshape(1, width, EARLY * piece)
-    spread = jnp.broadcast_to(quarter, (segment_count, width, EARLY * piece))
-    early = lax.all_to_all(spread, "segment", 0, 0, tiled=True)
-
-    def partner(value):
+
+    def early_weight(layer, after):
+        part = quarter[:, :, layer * piece : (layer + 1) * piece]
+        part = jnp.broadcast_to(part, (segment_count, width, piece))
+        if after is not None:
+            part, after = lax.optimization_barrier((part, after))
+        return lax.all_to_all(part, "segment", 0, 0, tiled=True), after
+
+    def swap(value):
         return lax.ppermute(value, "graph", [(p, p ^ 1) for p in range(graph_count)])
 
     def exchange(value, first):
@@ -246,12 +226,12 @@
     hids = pick_batch(hist_ids)
     tables = jnp.concatenate([own, side, hist], axis=0)
     ids = jnp.concatenate([sids, hids])
-    i0, i1 = by_part(ids, partner(ids))
-    t0, t1 = by_part(tables, partner(tables))
-    x0, x1 = by_part(initial, partner(initial))
+    i0, i1 = by_part(ids, swap(ids))
+    t0, t1 = by_part(tables, swap(tables))
+    x0, x1 = by_part(initial, swap(initial))
 
     looked = jax.vmap(lambda t: dot(one_hot(hids, t.shape[0]), t).astype(BF))(history)
-    g0, g1 = by_part(looked, partner(looked))
+    g0, g1 = by_part(looked, swap(looked))
 
     def split(t, i):
         own = t[:rows]
@@ -317,22 +297,25 @@
     send_a, send_b = sent[: 3 * edge], sent[3 * edge :]
     (local,) = begin(None, current, near, hist_n, looked[0], None)
     place = core.astype(jnp.int32).reshape(1)
-    weight = resident
+    early, _ = early_weight(0, None)
+    weight = None
     own_rows = []
     for layer in range(layers):
         got_b = exchange(send_b, 2)
         got_a = exchange(send_a, 0)
         if layer < EARLY:
             mine = half_finish(layer, place, local, got_a, got_b, far, start, early)
-            current, send_a, send_b = join(place, mine, partner(mine), picks)
+            if layer + 1 < EARLY:
+                early, mine = early_weight(layer + 1, mine)
+            current, send_a, send_b = join(place, mine, swap(mine), picks)
         else:
             current, send_a, send_b = finish(
-                layer, local, got_a, got_b, far, picks, start, weight, layer > EARLY
+                layer, local, got_a, got_b, far, picks, start, weight
             )
         if layer + 1 < layers:
-            brought = layer + 1 - EARLY if layer >= EARLY else None
+            brought = layer + 1 - EARLY if layer + 1 >= EARLY else None
             out = begin(brought, current, near, hist_n, looked[layer + 1], resident)
-            local, weight = (out[0], resident) if brought is None else out
+            local, weight = (out[0], None) if brought is None else out
         own_rows.append(lax.dynamic_slice_in_dim(current, core * rows, rows, 0))
     whole = jnp.stack(own_rows)
     return lax.all_to_all(whole, "segment", 0, 1, tiled=True)

time: 237 us -> 237 us (level)
  waiting for transfers between devices: 56.3 us -> 44.2 us
  local copies, waits for them, and re-layouts: 16.3 us -> 27.6 us
    all_to_all x1 -> x2, waiting for transfers between devices: 12 us -> 2.06 us  [early_weight(): return (lax.all_to_all(part, 'segment', 0, 0, tiled=True), after)]
    unnamed x37 -> x41, local copies, waits for them, and re-layouts: 5.85 us -> 13.9 us
    ppermute x16, starting transfers between devices: 55.1 us -> 50.2 us  [exchange(): return lax.ppermute(value, 'graph', pairs)]
    all_to_all x1 -> x2, starting transfers between devices: 4.43 us -> 7.94 us  [early_weight(): return (lax.all_to_all(part, 'segment', 0, 0, tiled=True), after)]
    pallas_call x2, Pallas kernels: 5.1 us -> 2.52 us  [half_finish(): pl.pallas_call(lambda *refs: half_body(layer, min(256, width), *refs), ou...]
    broadcast_in_dim x1 -> x3, local copies, waits for them, and re-layouts: 1.45 us -> 4.01 us  [early_weight(): part = jnp.broadcast_to(part, (segment_count, width, piece))]
  transfers between devices with their start and end apart: 25 -> 26, of which waited for: 13 -> 11; matrix products, arithmetic and copies ran while one was open for 6% -> 10% of each run, Pallas kernels for 7% -> 7%
where the time goes in v5:
time: 237 us; the launch traced here: 235 us
  starting transfers between devices  88 us (37%)
  waiting for transfers between devices  44.2 us (19%)
  Pallas kernels  28.5 us (12%)
  local copies, waits for them, and re-layouts  27.6 us (12%)
  blocking collectives  24.5 us (10%)
  between operations  14.1 us (6%)
  other arithmetic  6.04 us (3%)
    ppermute x16, starting transfers between devices, exchange(): return lax.ppermute(value, 'graph', pairs)  50.2 us
    ppermute x16, waiting for transfers between devices, exchange(): return lax.ppermute(value, 'graph', pairs)  24.8 us
    all_to_all x1, blocking collectives, shards(): return lax.all_to_all(whole, 'segment', 0, 1, tiled=True)  24.5 us
    all_to_all x1, starting transfers between devices, shards(): lax.all_to_all(spread, 'graph', 0, 0, tiled=True)  17.3 us
    all_to_all x1, waiting for transfers between devices, shards(): lax.all_to_all(spread, 'graph', 0, 0, tiled=True)  14.7 us
    unnamed x41, local copies, waits for them, and re-layouts  13.9 us
    pallas_call x6, Pallas kernels, finish(): pl.pallas_call(lambda *refs: finish_body(layer, min(256, width), *refs),...  12.7 us
    ppermute x6, starting transfers between devices, swap(): lax.ppermute(value, 'graph', [(p, p ^ 1) for p in range(graph_count)])  12.5 us
  transfers between devices with their start and end apart: 26, of which 11 were waited for; matrix products, arithmetic and copies ran while one was open for 10% of the time, Pallas kernels for 7%

profile of v5, /device:TPU:32, one launch (start us, length us, event | category | flops | bytes accessed | tf_op | source)
XLA Modules:
  0.0 235.0 jit_solution(16001155116536947419)
XLA Ops:
  6.5 1.6 slice.130
  10.4 1.9 collective-permute-start.1
  13.0 1.4 fusion
  14.5 2.4 %collective-permute-start.3 = (bf16[8,64,1024]{2,1,0:T(8,128)(2,1)}, bf16[8,64,1024]{2,1,0:T(8,128)(2,1)}, u32[]{:S(2)}, u32[]{:S(2)}) collective-permute-start(bf16[8,64,1024]{2,1,0:T(8,128)(2,1)} %fusion), channel_id=1, source_target_pairs={{0,1},{1,0},{2,3},{3,2},{4,5},{5,4},{6,7},{7,6},{8,9},{9,8},{10,11... | collective-permute-start | bytes 3145736 | tf_op jit(solution)/shard_map/ppermute | solution.py:206
  16.9 1.0 constant_dynamic-slice_fusion.3
  17.9 1.9 collective-permute-start
  20.6 2.4 %collective-permute-start.2 = (s32[128]{0:T(128)S(1)}, s32[128]{0:T(128)S(1)}, u32[]{:S(2)}, u32[]{:S(2)}) collective-permute-start(s32[128]{0:T(128)S(1)} %pad_add_fusion.4), channel_id=1, source_target_pairs={{0,1},{1,0},{2,3},{3,2},{4,5},{5,4},{6,7},{7,6},{8,9},{9,8},{10,11... | collective-permute-start | bytes 1544 | tf_op jit(solution)/shard_map/ppermute | solution.py:206
  23.9 17.3 %all-to-all-start = ((bf16[128,8,256]{2,1,0:T(8,128)(2,1)}), bf16[128,8,256]{2,1,0:T(8,128)(2,1)S(1)}, u32[]{:S(2)}, u32[]{:S(2)}) async-start(bf16[128,8,256]{2,1,0:T(8,128)(2,1)} %bitcast.5), calls=%async_computation | async-start | bytes 1048576 | tf_op jit(solution)/shard_map/all_to_all | solution.py:196
  42.8 1.1 broadcast_select_fusion.3
  44.1 14.7 %all-to-all-done = bf16[128,8,256]{2,1,0:T(8,128)(2,1)S(1)} async-done(((bf16[128,8,256]{2,1,0:T(8,128)(2,1)}), bf16[128,8,256]{2,1,0:T(8,128)(2,1)S(1)}, u32[]{:S(2)}, u32[]{:S(2)}) %all-to-all-start) | async-done | bytes 524320 | tf_op jit(solution)/shard_map/all_to_all | solution.py:196
  59.5 1.1 broadcast_in_dim.40
  60.6 4.4 %all-to-all-start.1 = ((bf16[4,1024,128]{2,1,0:T(8,128)(2,1)}), bf16[4,1024,128]{2,1,0:T(8,128)(2,1)S(1)}, u32[]{:S(2)}, u32[]{:S(2)}) async-start(bf16[4,1024,128]{2,1,0:T(8,128)(2,1)} %broadcast_in_dim.40), calls=%async_computation.1 | async-start | bytes 2097152 | tf_op jit(solution)/shard_map/all_to_all | solution.py:203
  65.0 2.9 %collective-permute-start.4 = (bf16[48,1024]{1,0:T(8,128)(2,1)S(1)}, bf16[48,1024]{1,0:T(8,128)(2,1)S(1)}, u32[]{:S(2)}, u32[]{:S(2)}) collective-permute-start(bf16[48,1024]{1,0:T(8,128)(2,1)S(1)} %get-tuple-element.92), channel_id=1, source_target_pairs={{0,2},{2,0},{1,3},{3,1},{4,6},{6,4},{5,7},{7,5},{8,10},{10,8},{9,1... | collective-permute-start | bytes 294920 | tf_op jit(solution)/shard_map/ppermute | solution.py:213
  67.9 4.9 %collective-permute-start.5 = (bf16[48,1024]{1,0:T(8,128)(2,1)S(1)}, bf16[48,1024]{1,0:T(8,128)(2,1)S(1)}, u32[]{:S(2)}, u32[]{:S(2)}) collective-permute-start(bf16[48,1024]{1,0:T(8,128)(2,1)S(1)} %get-tuple-element.91), channel_id=1, source_target_pairs={{2,4},{4,2},{3,5},{5,3},{6,8},{8,6},{7,9},{9,7},{10,12},{12,10},{1... | collective-permute-start | bytes 294920 | tf_op jit(solution)/shard_map/ppermute | solution.py:213
  72.8 1.0 pad_maximum_fusion.refs_0_.refs_5_
  73.8 2.0 broadcast_select_fusion.1
  75.8 1.2 fusion.8
  78.5 2.1 all-to-all-done.1.refs_6_
  80.6 1.2 copy-done.2
  82.7 2.2 broadcast_in_dim.17
  84.9 3.5 %all-to-all-start.2 = ((bf16[4,1024,128]{2,1,0:T(8,128)(2,1)}), bf16[4,1024,128]{2,1,0:T(8,128)(2,1)S(1)}, u32[]{:S(2)}, u32[]{:S(2)}) async-start(bf16[4,1024,128]{2,1,0:T(8,128)(2,1)} %broadcast_in_dim.17), calls=%async_computation.2 | async-start | bytes 2097152 | tf_op jit(solution)/shard_map/all_to_all | solution.py:203
  88.4 1.9 collective-permute-start.6
  90.3 1.7 collective-permute-done.6.theirs
  93.3 3.1 %collective-permute-start.7 = (bf16[48,1024]{1,0:T(8,128)(2,1)S(1)}, bf16[48,1024]{1,0:T(8,128)(2,1)S(1)}, u32[]{:S(2)}, u32[]{:S(2)}) collective-permute-start(bf16[48,1024]{1,0:T(8,128)(2,1)S(1)} %get-tuple-element.43), channel_id=1, source_target_pairs={{0,2},{2,0},{1,3},{3,1},{4,6},{6,4},{5,7},{7,5},{8,10},{10,8},{9,1... | collective-permute-start | bytes 294920 | tf_op jit(solution)/shard_map/ppermute | solution.py:213
  96.3 3.8 %collective-permute-start.8 = (bf16[48,1024]{1,0:T(8,128)(2,1)S(1)}, bf16[48,1024]{1,0:T(8,128)(2,1)S(1)}, u32[]{:S(2)}, u32[]{:S(2)}) collective-permute-start(bf16[48,1024]{1,0:T(8,128)(2,1)S(1)} %get-tuple-element.44), channel_id=1, source_target_pairs={{2,4},{4,2},{3,5},{5,3},{6,8},{8,6},{7,9},{9,7},{10,12},{12,10},{1... | collective-permute-start | bytes 294920 | tf_op jit(solution)/shard_map/ppermute | solution.py:213
  101.6 1.0 copy-done.3
  102.5 6.2 %collective-permute-done.8.refs_3_ = bf16[48,1024]{1,0:T(8,128)(2,1)S(1)} collective-permute-done((bf16[48,1024]{1,0:T(8,128)(2,1)S(1)}, bf16[48,1024]{1,0:T(8,128)(2,1)S(1)}, u32[]{:S(2)}, u32[]{:S(2)}) %collective-permute-start.8) | collective-permute-done | bytes 98336 | tf_op jit(solution)/shard_map/ppermute | solution.py:213
  109.4 1.2 copy-done.4
  111.5 1.6 half_finish.3.mine
  113.1 1.9 collective-permute-start.9
  115.8 1.0 collective-permute-done.9.theirs
  116.7 1.2 join.3
  118.0 1.9 collective-permute-start.10
  119.9 4.0 %collective-permute-start.11 = (bf16[48,1024]{1,0:T(8,128)(2,1)S(1)}, bf16[48,1024]{1,0:T(8,128)(2,1)S(1)}, u32[]{:S(2)}, u32[]{:S(2)}) collective-permute-start(bf16[48,1024]{1,0:T(8,128)(2,1)S(1)} %get-tuple-element.49), channel_id=1, source_target_pairs={{2,4},{4,2},{3,5},{5,3},{6,8},{8,6},{7,9},{9,7},{10,12},{12,10},{1... | collective-permute-start | bytes 294920 | tf_op jit(solution)/shard_map/ppermute | solution.py:213
  125.5 1.8 begin.10
  127.4 2.5 %collective-permute-done.11.refs_2_ = bf16[48,1024]{1,0:T(8,128)(2,1)S(1)} collective-permute-done((bf16[48,1024]{1,0:T(8,128)(2,1)S(1)}, bf16[48,1024]{1,0:T(8,128)(2,1)S(1)}, u32[]{:S(2)}, u32[]{:S(2)}) %collective-permute-start.11) | collective-permute-done | bytes 98336 | tf_op jit(solution)/shard_map/ppermute | solution.py:213
  129.9 2.0 finish.6
  131.9 1.9 collective-permute-start.12
  133.8 4.0 %collective-permute-start.13 = (bf16[48,1024]{1,0:T(8,128)(2,1)S(1)}, bf16[48,1024]{1,0:T(8,128)(2,1)S(1)}, u32[]{:S(2)}, u32[]{:S(2)}) collective-permute-start(bf16[48,1024]{1,0:T(8,128)(2,1)S(1)} %get-tuple-element.54), channel_id=1, source_target_pairs={{2,4},{4,2},{3,5},{5,3},{6,8},{8,6},{7,9},{9,7},{10,12},{12,10},{1... | collective-permute-start | bytes 294920 | tf_op jit(solution)/shard_map/ppermute | solution.py:213
  137.8 1.8 begin.11
  140.4 3.2 %collective-permute-done.13.refs_2_ = bf16[48,1024]{1,0:T(8,128)(2,1)S(1)} collective-permute-done((bf16[48,1024]{1,0:T(8,128)(2,1)S(1)}, bf16[48,1024]{1,0:T(8,128)(2,1)S(1)}, u32[]{:S(2)}, u32[]{:S(2)}) %collective-permute-start.13) | collective-permute-done | bytes 98336 | tf_op jit(solution)/shard_map/ppermute | solution.py:213
  143.7 2.0 finish.7
  145.7 1.9 collective-permute-start.14
  147.6 4.2 %collective-permute-start.15 = (bf16[48,1024]{1,0:T(8,128)(2,1)S(1)}, bf16[48,1024]{1,0:T(8,128)(2,1)S(1)}, u32[]{:S(2)}, u32[]{:S(2)}) collective-permute-start(bf16[48,1024]{1,0:T(8,128)(2,1)S(1)} %get-tuple-element.59), channel_id=1, source_target_pairs={{2,4},{4,2},{3,5},{5,3},{6,8},{8,6},{7,9},{9,7},{10,12},{12,10},{1... | collective-permute-start | bytes 294920 | tf_op jit(solution)/shard_map/ppermute | solution.py:213
  151.8 1.8 begin.12
  154.4 3.1 %collective-permute-done.15.refs_2_ = bf16[48,1024]{1,0:T(8,128)(2,1)S(1)} collective-permute-done((bf16[48,1024]{1,0:T(8,128)(2,1)S(1)}, bf16[48,1024]{1,0:T(8,128)(2,1)S(1)}, u32[]{:S(2)}, u32[]{:S(2)}) %collective-permute-start.15) | collective-permute-done | bytes 98336 | tf_op jit(solution)/shard_map/ppermute | solution.py:213
  157.4 2.0 finish.8
  159.4 1.9 collective-permute-start.16
  161.4 4.0 %collective-permute-start.17 = (bf16[48,1024]{1,0:T(8,128)(2,1)S(1)}, bf16[48,1024]{1,0:T(8,128)(2,1)S(1)}, u32[]{:S(2)}, u32[]{:S(2)}) collective-permute-start(bf16[48,1024]{1,0:T(8,128)(2,1)S(1)} %get-tuple-element.64), channel_id=1, source_target_pairs={{2,4},{4,2},{3,5},{5,3},{6,8},{8,6},{7,9},{9,7},{10,12},{12,10},{1... | collective-permute-start | bytes 294920 | tf_op jit(solution)/shard_map/ppermute | solution.py:213
  165.4 1.8 begin.13
  168.0 3.2 %collective-permute-done.17.refs_2_ = bf16[48,1024]{1,0:T(8,128)(2,1)S(1)} collective-permute-done((bf16[48,1024]{1,0:T(8,128)(2,1)S(1)}, bf16[48,1024]{1,0:T(8,128)(2,1)S(1)}, u32[]{:S(2)}, u32[]{:S(2)}) %collective-permute-start.17) | collective-permute-done | bytes 98336 | tf_op jit(solution)/shard_map/ppermute | solution.py:213
  171.2 2.0 finish.9
  173.2 1.9 collective-permute-start.18
  175.2 4.0 %collective-permute-start.19 = (bf16[48,1024]{1,0:T(8,128)(2,1)S(1)}, bf16[48,1024]{1,0:T(8,128)(2,1)S(1)}, u32[]{:S(2)}, u32[]{:S(2)}) collective-permute-start(bf16[48,1024]{1,0:T(8,128)(2,1)S(1)} %get-tuple-element.69), channel_id=1, source_target_pairs={{2,4},{4,2},{3,5},{5,3},{6,8},{8,6},{7,9},{9,7},{10,12},{12,10},{1... | collective-permute-start | bytes 294920 | tf_op jit(solution)/shard_map/ppermute | solution.py:213
  179.2 1.8 begin.14
  181.7 3.2 %collective-permute-done.19.refs_2_ = bf16[48,1024]{1,0:T(8,128)(2,1)S(1)} collective-permute-done((bf16[48,1024]{1,0:T(8,128)(2,1)S(1)}, bf16[48,1024]{1,0:T(8,128)(2,1)S(1)}, u32[]{:S(2)}, u32[]{:S(2)}) %collective-permute-start.19) | collective-permute-done | bytes 98336 | tf_op jit(solution)/shard_map/ppermute | solution.py:213
  185.0 2.0 finish.10
  187.0 1.9 collective-permute-start.20
  188.9 4.0 %collective-permute-start.21 = (bf16[48,1024]{1,0:T(8,128)(2,1)S(1)}, bf16[48,1024]{1,0:T(8,128)(2,1)S(1)}, u32[]{:S(2)}, u32[]{:S(2)}) collective-permute-start(bf16[48,1024]{1,0:T(8,128)(2,1)S(1)} %get-tuple-element.74), channel_id=1, source_target_pairs={{2,4},{4,2},{3,5},{5,3},{6,8},{8,6},{7,9},{9,7},{10,12},{12,10},{1... | collective-permute-start | bytes 294920 | tf_op jit(solution)/shard_map/ppermute | solution.py:213
  192.9 1.8 begin.15
  195.5 3.2 %collective-permute-done.21.refs_2_ = bf16[48,1024]{1,0:T(8,128)(2,1)S(1)} collective-permute-done((bf16[48,1024]{1,0:T(8,128)(2,1)S(1)}, bf16[48,1024]{1,0:T(8,128)(2,1)S(1)}, u32[]{:S(2)}, u32[]{:S(2)}) %collective-permute-start.21) | collective-permute-done | bytes 98336 | tf_op jit(solution)/shard_map/ppermute | solution.py:213
  198.8 2.7 %finish.11 = (bf16[256,1024]{1,0:T(8,128)(2,1)S(1)}, bf16[48,1024]{1,0:T(8,128)(2,1)}, bf16[48,1024]{1,0:T(8,128)(2,1)}) custom-call(f32[256,1024]{1,0:T(8,128)S(1)} %get-tuple-element.72.refs_0_, bf16[48,1024]{1,0:T(8,128)(2,1)S(1)} %collective-permute-done.20.refs_1_, bf16[48,1024]{1,0:T(8,128)(2,1)S(1)} %collective-permute-done.21.refs_2_, ...), custom_call_target="tpu_custom_call" | custom-call | tf_op jit(solution)/shard_map/finish/pallas_call | solution.py:129
  202.2 24.5 %all_to_all.33 = bf16[8,128,1024]{2,1,0:T(8,128)(2,1)S(1)} all-to-all(bf16[8,128,1024]{2,1,0:T(8,128)(2,1)} %bitcast_dynamic-update-slice_fusion), channel_id=1, replica_groups=mesh['segment'=4,'graph'=128] {'segment'}, dimensions={0} | all-to-all | bytes 4194304 | tf_op jit(solution)/shard_map/all_to_all | solution.py:321
  226.6 1.5 copy.65
  (100 shorter events, 20.2 us)
Async XLA Ops:
  6.5 6.5 %copy-start = (bf16[8,64,1024]{2,1,0:T(8,128)(2,1)S(1)}, bf16[8,64,1024]{2,1,0:T(8,128)(2,1)}, u32[]{:S(2)}) copy-start(bf16[8,64,1024]{2,1,0:T(8,128)(2,1)} %param.10) | copy-start | bytes 3145732
  6.5 16.5 %slice-start = ((bf16[8,8,1024]{2,1,0:T(8,128)(2,1)}), bf16[2,8,1024]{2,1,0:T(8,128)(2,1)S(1)}, s32[]{:S(2)}) async-start(bf16[8,8,1024]{2,1,0:T(8,128)(2,1)} %param.9), calls=%async_computation.5 | async-start | bytes 65536 | tf_op jit(solution)/shard_map/slice | solution.py:191
  6.5 118.1 %all-gather.2.cloned.1.call-start = ((), (), s32[]{:S(2)}) async-start(), calls=%async_computation.4 | async-start | bytes 12681216 | tf_op jit(solution)/shard_map/all_gather | solution.py:187
  10.4 31.5 %collective-permute-start.1 = (bf16[256,128]{1,0:T(8,128)(2,1)S(1)}, bf16[256,128]{1,0:T(8,128)(2,1)S(1)}, u32[]{:S(2)}, u32[]{:S(2)}) collective-permute-start(bf16[256,128]{1,0:T(8,128)(2,1)S(1)} %pad_maximum_fusion.2), channel_id=1, source_target_pairs={{0,1},{1,0},{2,3},{3,2},{4,5},{5,4},{6,7},{7,6},{8,9},{9,8},{10,11... | collective-permute-start | bytes 196616 | tf_op jit(solution)/shard_map/ppermute | solution.py:206
  14.5 59.3 %collective-permute-start.3 = (bf16[8,64,1024]{2,1,0:T(8,128)(2,1)}, bf16[8,64,1024]{2,1,0:T(8,128)(2,1)}, u32[]{:S(2)}, u32[]{:S(2)}) collective-permute-start(bf16[8,64,1024]{2,1,0:T(8,128)(2,1)} %fusion), channel_id=1, source_target_pairs={{0,1},{1,0},{2,3},{3,2},{4,5},{5,4},{6,7},{7,6},{8,9},{9,8},{10,11... | collective-permute-start | bytes 3145736 | tf_op jit(solution)/shard_map/ppermute | solution.py:206
  17.9 24.9 %collective-permute-start = (bf16[128,1024]{1,0:T(8,128)(2,1)S(1)}, bf16[128,1024]{1,0:T(8,128)(2,1)S(1)}, u32[]{:S(2)}, u32[]{:S(2)}) collective-permute-start(bf16[128,1024]{1,0:T(8,128)(2,1)S(1)} %constant_dynamic-slice_fusion.3), channel_id=1, source_target_pairs={{0,1},{1,0},{2,3},{3,2},{4,5},{5,4},{6,7},{7,6},{8,9},{9,8},{10,11... | collective-permute-start | bytes 786440 | tf_op jit(solution)/shard_map/ppermute | solution.py:206
  20.6 20.7 %collective-permute-start.2 = (s32[128]{0:T(128)S(1)}, s32[128]{0:T(128)S(1)}, u32[]{:S(2)}, u32[]{:S(2)}) collective-permute-start(s32[128]{0:T(128)S(1)} %pad_add_fusion.4), channel_id=1, source_target_pairs={{0,1},{1,0},{2,3},{3,2},{4,5},{5,4},{6,7},{7,6},{8,9},{9,8},{10,11... | collective-permute-start | bytes 1544 | tf_op jit(solution)/shard_map/ppermute | solution.py:206
  23.9 34.8 %all-to-all-start = ((bf16[128,8,256]{2,1,0:T(8,128)(2,1)}), bf16[128,8,256]{2,1,0:T(8,128)(2,1)S(1)}, u32[]{:S(2)}, u32[]{:S(2)}) async-start(bf16[128,8,256]{2,1,0:T(8,128)(2,1)} %bitcast.5), calls=%async_computation | async-start | bytes 1048576 | tf_op jit(solution)/shard_map/all_to_all | solution.py:196
  43.9 16.7 %copy-start.16 = (bf16[128,1024]{1,0:T(8,128)(2,1)}, bf16[128,1024]{1,0:T(8,128)(2,1)S(1)}, u32[]{:S(2)}) copy-start(bf16[128,1024]{1,0:T(8,128)(2,1)S(1)} %get-tuple-element.90) | copy-start | bytes 786436
  60.6 19.9 %all-to-all-start.1 = ((bf16[4,1024,128]{2,1,0:T(8,128)(2,1)}), bf16[4,1024,128]{2,1,0:T(8,128)(2,1)S(1)}, u32[]{:S(2)}, u32[]{:S(2)}) async-start(bf16[4,1024,128]{2,1,0:T(8,128)(2,1)} %broadcast_in_dim.40), calls=%async_computation.1 | async-start | bytes 2097152 | tf_op jit(solution)/shard_map/all_to_all | solution.py:203
  65.0 13.4 %collective-permute-start.4 = (bf16[48,1024]{1,0:T(8,128)(2,1)S(1)}, bf16[48,1024]{1,0:T(8,128)(2,1)S(1)}, u32[]{:S(2)}, u32[]{:S(2)}) collective-permute-start(bf16[48,1024]{1,0:T(8,128)(2,1)S(1)} %get-tuple-element.92), channel_id=1, source_target_pairs={{0,2},{2,0},{1,3},{3,1},{4,6},{6,4},{5,7},{7,5},{8,10},{10,8},{9,1... | collective-permute-start | bytes 294920 | tf_op jit(solution)/shard_map/ppermute | solution.py:213
  67.9 10.6 %collective-permute-start.5 = (bf16[48,1024]{1,0:T(8,128)(2,1)S(1)}, bf16[48,1024]{1,0:T(8,128)(2,1)S(1)}, u32[]{:S(2)}, u32[]{:S(2)}) collective-permute-start(bf16[48,1024]{1,0:T(8,128)(2,1)S(1)} %get-tuple-element.91), channel_id=1, source_target_pairs={{2,4},{4,2},{3,5},{5,3},{6,8},{8,6},{7,9},{9,7},{10,12},{12,10},{1... | collective-permute-start | bytes 294920 | tf_op jit(solution)/shard_map/ppermute | solution.py:213
  77.5 1.0 copy-start.1
  80.5 1.2 copy-start.2
  82.7 7.6 %copy-start.12 = (bf16[256,512]{1,0:T(8,128)(2,1)}, bf16[256,512]{1,0:T(8,128)(2,1)S(1)}, u32[]{:S(2)}) copy-start(bf16[256,512]{1,0:T(8,128)(2,1)S(1)} %half_finish.2.mine) | copy-start | bytes 786436
  84.9 24.5 %all-to-all-start.2 = ((bf16[4,1024,128]{2,1,0:T(8,128)(2,1)}), bf16[4,1024,128]{2,1,0:T(8,128)(2,1)S(1)}, u32[]{:S(2)}, u32[]{:S(2)}) async-start(bf16[4,1024,128]{2,1,0:T(8,128)(2,1)} %broadcast_in_dim.17), calls=%async_computation.2 | async-start | bytes 2097152 | tf_op jit(solution)/shard_map/all_to_all | solution.py:203
  88.4 3.7 %collective-permute-start.6 = (bf16[256,512]{1,0:T(8,128)(2,1)S(1)}, bf16[256,512]{1,0:T(8,128)(2,1)S(1)}, u32[]{:S(2)}, u32[]{:S(2)}) collective-permute-start(bf16[256,512]{1,0:T(8,128)(2,1)S(1)} %half_finish.2.mine), channel_id=1, source_target_pairs={{0,1},{1,0},{2,3},{3,2},{4,5},{5,4},{6,7},{7,6},{8,9},{9,8},{10,11... | collective-permute-start | bytes 786440 | tf_op jit(solution)/shard_map/ppermute | solution.py:206
  92.0 1.0 copy-start.13
  93.3 9.3 %collective-permute-start.7 = (bf16[48,1024]{1,0:T(8,128)(2,1)S(1)}, bf16[48,1024]{1,0:T(8,128)(2,1)S(1)}, u32[]{:S(2)}, u32[]{:S(2)}) collective-permute-start(bf16[48,1024]{1,0:T(8,128)(2,1)S(1)} %get-tuple-element.43), channel_id=1, source_target_pairs={{0,2},{2,0},{1,3},{3,1},{4,6},{6,4},{5,7},{7,5},{8,10},{10,8},{9,1... | collective-permute-start | bytes 294920 | tf_op jit(solution)/shard_map/ppermute | solution.py:213
  96.3 12.4 %collective-permute-start.8 = (bf16[48,1024]{1,0:T(8,128)(2,1)S(1)}, bf16[48,1024]{1,0:T(8,128)(2,1)S(1)}, u32[]{:S(2)}, u32[]{:S(2)}) collective-permute-start(bf16[48,1024]{1,0:T(8,128)(2,1)S(1)} %get-tuple-element.44), channel_id=1, source_target_pairs={{2,4},{4,2},{3,5},{5,3},{6,8},{8,6},{7,9},{9,7},{10,12},{12,10},{1... | collective-permute-start | bytes 294920 | tf_op jit(solution)/shard_map/ppermute | solution.py:213
  100.2 1.0 copy-start.11
  101.6 1.0 copy-start.3
  108.7 0.6 copy-start.14
  109.4 1.2 copy-start.4
  110.6 0.9 copy-start.15
  113.1 3.6 %collective-permute-start.9 = (bf16[256,512]{1,0:T(8,128)(2,1)}, bf16[256,512]{1,0:T(8,128)(2,1)S(1)}, u32[]{:S(2)}, u32[]{:S(2)}) collective-permute-start(bf16[256,512]{1,0:T(8,128)(2,1)} %half_finish.3.mine), channel_id=1, source_target_pairs={{0,1},{1,0},{2,3},{3,2},{4,5},{5,4},{6,7},{7,6},{8,9},{9,8},{10,11... | collective-permute-start | bytes 786440 | tf_op jit(solution)/shard_map/ppermute | solution.py:206
  118.0 9.5 %collective-permute-start.10 = (bf16[48,1024]{1,0:T(8,128)(2,1)S(1)}, bf16[48,1024]{1,0:T(8,128)(2,1)S(1)}, u32[]{:S(2)}, u32[]{:S(2)}) collective-permute-start(bf16[48,1024]{1,0:T(8,128)(2,1)S(1)} %get-tuple-element.48), channel_id=1, source_target_pairs={{0,2},{2,0},{1,3},{3,1},{4,6},{6,4},{5,7},{7,5},{8,10},{10,8},{9,1... | collective-permute-start | bytes 294920 | tf_op jit(solution)/shard_map/ppermute | solution.py:213
  119.9 10.0 %collective-permute-start.11 = (bf16[48,1024]{1,0:T(8,128)(2,1)S(1)}, bf16[48,1024]{1,0:T(8,128)(2,1)S(1)}, u32[]{:S(2)}, u32[]{:S(2)}) collective-permute-start(bf16[48,1024]{1,0:T(8,128)(2,1)S(1)} %get-tuple-element.49), channel_id=1, source_target_pairs={{2,4},{4,2},{3,5},{5,3},{6,8},{8,6},{7,9},{9,7},{10,12},{12,10},{1... | collective-permute-start | bytes 294920 | tf_op jit(solution)/shard_map/ppermute | solution.py:213
  124.6 1.0 copy-start.10
  127.4 10.4 %copy-start.9 = (bf16[128,1024]{1,0:T(8,128)(2,1)S(1)}, bf16[128,1024]{1,0:T(8,128)(2,1)}, u32[]{:S(2)}) copy-start(bf16[128,1024]{1,0:T(8,128)(2,1)} %get-tuple-element.81.refs_3_) | copy-start | bytes 786436
  131.9 8.5 %collective-permute-start.12 = (bf16[48,1024]{1,0:T(8,128)(2,1)S(1)}, bf16[48,1024]{1,0:T(8,128)(2,1)S(1)}, u32[]{:S(2)}, u32[]{:S(2)}) collective-permute-start(bf16[48,1024]{1,0:T(8,128)(2,1)S(1)} %get-tuple-element.53), channel_id=1, source_target_pairs={{0,2},{2,0},{1,3},{3,1},{4,6},{6,4},{5,7},{7,5},{8,10},{10,8},{9,1... | collective-permute-start | bytes 294920 | tf_op jit(solution)/shard_map/ppermute | solution.py:213
  133.8 9.8 %collective-permute-start.13 = (bf16[48,1024]{1,0:T(8,128)(2,1)S(1)}, bf16[48,1024]{1,0:T(8,128)(2,1)S(1)}, u32[]{:S(2)}, u32[]{:S(2)}) collective-permute-start(bf16[48,1024]{1,0:T(8,128)(2,1)S(1)} %get-tuple-element.54), channel_id=1, source_target_pairs={{2,4},{4,2},{3,5},{5,3},{6,8},{8,6},{7,9},{9,7},{10,12},{12,10},{1... | collective-permute-start | bytes 294920 | tf_op jit(solution)/shard_map/ppermute | solution.py:213
  140.4 11.4 %copy-start.8 = (bf16[128,1024]{1,0:T(8,128)(2,1)S(1)}, bf16[128,1024]{1,0:T(8,128)(2,1)}, u32[]{:S(2)}) copy-start(bf16[128,1024]{1,0:T(8,128)(2,1)} %get-tuple-element.82.refs_3_) | copy-start | bytes 786436
  145.7 8.7 %collective-permute-start.14 = (bf16[48,1024]{1,0:T(8,128)(2,1)S(1)}, bf16[48,1024]{1,0:T(8,128)(2,1)S(1)}, u32[]{:S(2)}, u32[]{:S(2)}) collective-permute-start(bf16[48,1024]{1,0:T(8,128)(2,1)S(1)} %get-tuple-element.58), channel_id=1, source_target_pairs={{0,2},{2,0},{1,3},{3,1},{4,6},{6,4},{5,7},{7,5},{8,10},{10,8},{9,1... | collective-permute-start | bytes 294920 | tf_op jit(solution)/shard_map/ppermute | solution.py:213
  147.6 9.8 %collective-permute-start.15 = (bf16[48,1024]{1,0:T(8,128)(2,1)S(1)}, bf16[48,1024]{1,0:T(8,128)(2,1)S(1)}, u32[]{:S(2)}, u32[]{:S(2)}) collective-permute-start(bf16[48,1024]{1,0:T(8,128)(2,1)S(1)} %get-tuple-element.59), channel_id=1, source_target_pairs={{2,4},{4,2},{3,5},{5,3},{6,8},{8,6},{7,9},{9,7},{10,12},{12,10},{1... | collective-permute-start | bytes 294920 | tf_op jit(solution)/shard_map/ppermute | solution.py:213
  154.4 11.0 %copy-start.7 = (bf16[128,1024]{1,0:T(8,128)(2,1)S(1)}, bf16[128,1024]{1,0:T(8,128)(2,1)}, u32[]{:S(2)}) copy-start(bf16[128,1024]{1,0:T(8,128)(2,1)} %get-tuple-element.83.refs_3_) | copy-start | bytes 786436
  159.4 8.5 %collective-permute-start.16 = (bf16[48,1024]{1,0:T(8,128)(2,1)S(1)}, bf16[48,1024]{1,0:T(8,128)(2,1)S(1)}, u32[]{:S(2)}, u32[]{:S(2)}) collective-permute-start(bf16[48,1024]{1,0:T(8,128)(2,1)S(1)} %get-tuple-element.63), channel_id=1, source_target_pairs={{0,2},{2,0},{1,3},{3,1},{4,6},{6,4},{5,7},{7,5},{8,10},{10,8},{9,1... | collective-permute-start | bytes 294920 | tf_op jit(solution)/shard_map/ppermute | solution.py:213
  161.4 9.8 %collective-permute-start.17 = (bf16[48,1024]{1,0:T(8,128)(2,1)S(1)}, bf16[48,1024]{1,0:T(8,128)(2,1)S(1)}, u32[]{:S(2)}, u32[]{:S(2)}) collective-permute-start(bf16[48,1024]{1,0:T(8,128)(2,1)S(1)} %get-tuple-element.64), channel_id=1, source_target_pairs={{2,4},{4,2},{3,5},{5,3},{6,8},{8,6},{7,9},{9,7},{10,12},{12,10},{1... | collective-permute-start | bytes 294920 | tf_op jit(solution)/shard_map/ppermute | solution.py:213
  168.0 11.2 %copy-start.6 = (bf16[128,1024]{1,0:T(8,128)(2,1)S(1)}, bf16[128,1024]{1,0:T(8,128)(2,1)}, u32[]{:S(2)}) copy-start(bf16[128,1024]{1,0:T(8,128)(2,1)} %get-tuple-element.84.refs_3_) | copy-start | bytes 786436
  173.2 8.5 %collective-permute-start.18 = (bf16[48,1024]{1,0:T(8,128)(2,1)S(1)}, bf16[48,1024]{1,0:T(8,128)(2,1)S(1)}, u32[]{:S(2)}, u32[]{:S(2)}) collective-permute-start(bf16[48,1024]{1,0:T(8,128)(2,1)S(1)} %get-tuple-element.68), channel_id=1, source_target_pairs={{0,2},{2,0},{1,3},{3,1},{4,6},{6,4},{5,7},{7,5},{8,10},{10,8},{9,1... | collective-permute-start | bytes 294920 | tf_op jit(solution)/shard_map/ppermute | solution.py:213
  175.2 9.8 %collective-permute-start.19 = (bf16[48,1024]{1,0:T(8,128)(2,1)S(1)}, bf16[48,1024]{1,0:T(8,128)(2,1)S(1)}, u32[]{:S(2)}, u32[]{:S(2)}) collective-permute-start(bf16[48,1024]{1,0:T(8,128)(2,1)S(1)} %get-tuple-element.69), channel_id=1, source_target_pairs={{2,4},{4,2},{3,5},{5,3},{6,8},{8,6},{7,9},{9,7},{10,12},{12,10},{1... | collective-permute-start | bytes 294920 | tf_op jit(solution)/shard_map/ppermute | solution.py:213
  181.7 11.2 %copy-start.5 = (bf16[128,1024]{1,0:T(8,128)(2,1)S(1)}, bf16[128,1024]{1,0:T(8,128)(2,1)}, u32[]{:S(2)}) copy-start(bf16[128,1024]{1,0:T(8,128)(2,1)} %get-tuple-element.77.refs_3_) | copy-start | bytes 786436
  187.0 8.5 %collective-permute-start.20 = (bf16[48,1024]{1,0:T(8,128)(2,1)S(1)}, bf16[48,1024]{1,0:T(8,128)(2,1)S(1)}, u32[]{:S(2)}, u32[]{:S(2)}) collective-permute-start(bf16[48,1024]{1,0:T(8,128)(2,1)S(1)} %get-tuple-element.73), channel_id=1, source_target_pairs={{0,2},{2,0},{1,3},{3,1},{4,6},{6,4},{5,7},{7,5},{8,10},{10,8},{9,1... | collective-permute-start | bytes 294920 | tf_op jit(solution)/shard_map/ppermute | solution.py:213
  188.9 9.8 %collective-permute-start.21 = (bf16[48,1024]{1,0:T(8,128)(2,1)S(1)}, bf16[48,1024]{1,0:T(8,128)(2,1)S(1)}, u32[]{:S(2)}, u32[]{:S(2)}) collective-permute-start(bf16[48,1024]{1,0:T(8,128)(2,1)S(1)} %get-tuple-element.74), channel_id=1, source_target_pairs={{2,4},{4,2},{3,5},{5,3},{6,8},{8,6},{7,9},{9,7},{10,12},{12,10},{1... | collective-permute-start | bytes 294920 | tf_op jit(solution)/shard_map/ppermute | solution.py:213
Sparse Core Ops, SparseCore 0:
  10.6 103.3 all-gather.1

commit v6 on v5

--- a/solution.py
+++ b/solution.py
@@ -224,10 +224,12 @@
     hist = pick_batch(hist_adj)
     sids = pick_batch(send_ids).reshape(-1)
     hids = pick_batch(hist_ids)
-    tables = jnp.concatenate([own, side, hist], axis=0)
-    ids = jnp.concatenate([sids, hids])
-    i0, i1 = by_part(ids, swap(ids))
+    listed = jnp.pad(sids.astype(BF).reshape(4, edge), ((0, 12), (0, rows - edge)))
+    tables = jnp.concatenate([own, side, hist, listed], axis=0)
     t0, t1 = by_part(tables, swap(tables))
+    i0, i1 = [
+        t[-16:-12, :edge].astype(jnp.int32).reshape(-1) for t in (t0, t1)
+    ]
     x0, x1 = by_part(initial, swap(initial))
 
     looked = jax.vmap(lambda t: dot(one_hot(hids, t.shape[0]), t).astype(BF))(history)
@@ -236,7 +238,7 @@
     def split(t, i):
         own = t[:rows]
         side = [t[rows + k * edge : rows + (k + 1) * edge] for k in range(4)]
-        hist = t[rows + 4 * edge :]
+        hist = t[rows + 4 * edge : -16]
         send = [one_hot(i[k * edge : (k + 1) * edge], rows) for k in range(4)]
         return own, side, hist, send
 
@@ -295,18 +297,20 @@
     current = start
     sent = dot(picks, current).astype(BF)
     send_a, send_b = sent[: 3 * edge], sent[3 * edge :]
-    (local,) = begin(None, current, near, hist_n, looked[0], None)
     place = core.astype(jnp.int32).reshape(1)
-    early, _ = early_weight(0, None)
+    early = [early_weight(0, None)[0]]
+    for layer in range(1, EARLY):
+        arriving, early[-1] = early_weight(layer, early[-1])
+        early.append(arriving)
+    held, early[0] = lax.optimization_barrier((current, early[0]))
+    (local,) = begin(None, held, near, hist_n, looked[0], None)
     weight = None
     own_rows = []
     for layer in range(layers):
         got_b = exchange(send_b, 2)
         got_a = exchange(send_a, 0)
         if layer < EARLY:
-            mine = half_finish(layer, place, local, got_a, got_b, far, start, early)
-            if layer + 1 < EARLY:
-                early, mine = early_weight(layer + 1, mine)
+            mine = half_finish(layer, place, local, got_a, got_b, far, start, early[layer])
             current, send_a, send_b = join(place, mine, swap(mine), picks)
         else:
             current, send_a, send_b = finish(
@@ -314,7 +318,10 @@
             )
         if layer + 1 < layers:
             brought = layer + 1 - EARLY if layer + 1 >= EARLY else None
-            out = begin(brought, current, near, hist_n, looked[layer + 1], resident)
+            held = current
+            if layer + 1 < EARLY:
+                held, early[layer + 1] = lax.optimization_barrier((current, early[layer + 1]))
+            out = begin(brought, held, near, hist_n, looked[layer + 1], resident)
             local, weight = (out[0], None) if brought is None else out
         own_rows.append(lax.dynamic_slice_in_dim(current, core * rows, rows, 0))
     whole = jnp.stack(own_rows)

time: 237 us -> 234 us (0.987)
  local copies, waits for them, and re-layouts: 27.6 us -> 17.8 us
  Pallas kernels: 28.5 us -> 32.1 us
    unnamed x41 -> x27, local copies, waits for them, and re-layouts: 13.9 us -> 6.09 us
    all_to_all x2, waiting for transfers between devices: 2.06 us -> 6.05 us  [early_weight(): return (lax.all_to_all(part, 'segment', 0, 0, tiled=True), after)]
    ppermute x16, starting transfers between devices: 50.2 us -> 53.9 us  [exchange(): return lax.ppermute(value, 'graph', pairs)]
    ppermute x16, waiting for transfers between devices: 24.8 us -> 21.5 us  [exchange(): return lax.ppermute(value, 'graph', pairs)]
    ppermute x6 -> x5, starting transfers between devices: 12.5 us -> 10.1 us  [swap(): lax.ppermute(value, 'graph', [(p, p ^ 1) for p in range(graph_count)])]
  transfers between devices with their start and end apart: 26 -> 25, of which waited for: 11 -> 13; matrix products, arithmetic and copies ran while one was open for 10% -> 9% of each run, Pallas kernels for 7% -> 8%
where the time goes in v6:
time: 234 us; the launch traced here: 232 us
  starting transfers between devices  89.9 us (38%)
  waiting for transfers between devices  46.5 us (20%)
  Pallas kernels  32.1 us (14%)
  blocking collectives  24.4 us (10%)
  local copies, waits for them, and re-layouts  17.8 us (8%)
  between operations  14 us (6%)
  other arithmetic  5.33 us (2%)
    ppermute x16, starting transfers between devices, exchange(): return lax.ppermute(value, 'graph', pairs)  53.9 us
    all_to_all x1, blocking collectives, shards(): return lax.all_to_all(whole, 'segment', 0, 1, tiled=True)  24.4 us
    ppermute x16, waiting for transfers between devices, exchange(): return lax.ppermute(value, 'graph', pairs)  21.5 us
    all_to_all x1, starting transfers between devices, shards(): lax.all_to_all(spread, 'graph', 0, 0, tiled=True)  17.4 us
    all_to_all x1, waiting for transfers between devices, shards(): lax.all_to_all(spread, 'graph', 0, 0, tiled=True)  16.3 us
    pallas_call x6, Pallas kernels, finish(): pl.pallas_call(lambda *refs: finish_body(layer, min(256, width), *refs),...  12.7 us
    pallas_call x8, Pallas kernels, begin(): pl.pallas_call(lambda *refs: begin_body(layer, min(256, width), *refs), o...  11.9 us
    ppermute x5, starting transfers between devices, swap(): lax.ppermute(value, 'graph', [(p, p ^ 1) for p in range(graph_count)])  10.1 us
  transfers between devices with their start and end apart: 25, of which 13 were waited for; matrix products, arithmetic and copies ran while one was open for 9% of the time, Pallas kernels for 8%

profile of v6, /device:TPU:32, one launch (start us, length us, event | category | flops | bytes accessed | tf_op | source)
XLA Modules:
  0.0 232.1 jit_solution(11622778393966602179)
XLA Ops:
  6.5 1.6 slice.146
  11.1 1.9 collective-permute-start.1
  13.0 1.0 constant_dynamic-slice_fusion.4
  14.0 2.4 %collective-permute-start = (bf16[128,1024]{1,0:T(8,128)(2,1)S(1)}, bf16[128,1024]{1,0:T(8,128)(2,1)}, u32[]{:S(2)}, u32[]{:S(2)}) collective-permute-start(bf16[128,1024]{1,0:T(8,128)(2,1)S(1)} %constant_dynamic-slice_fusion.4), channel_id=1, source_target_pairs={{0,1},{1,0},{2,3},{3,2},{4,5},{5,4},{6,7},{7,6},{8,9},{9,8},{10,11... | collective-permute-start | bytes 786440 | tf_op jit(solution)/shard_map/ppermute | solution.py:206
  17.1 1.5 fusion
  18.6 1.9 collective-permute-start.2
  21.3 17.4 %all-to-all-start = ((bf16[128,8,256]{2,1,0:T(8,128)(2,1)}), bf16[128,8,256]{2,1,0:T(8,128)(2,1)S(1)}, u32[]{:S(2)}, u32[]{:S(2)}) async-start(bf16[128,8,256]{2,1,0:T(8,128)(2,1)} %bitcast.5), calls=%async_computation | async-start | bytes 1048576 | tf_op jit(solution)/shard_map/all_to_all | solution.py:196
  40.1 16.3 %all-to-all-done = bf16[128,8,256]{2,1,0:T(8,128)(2,1)S(1)} async-done(((bf16[128,8,256]{2,1,0:T(8,128)(2,1)}), bf16[128,8,256]{2,1,0:T(8,128)(2,1)S(1)}, u32[]{:S(2)}, u32[]{:S(2)}) %all-to-all-start) | async-done | bytes 524320 | tf_op jit(solution)/shard_map/all_to_all | solution.py:196
  56.4 1.1 broadcast_in_dim.19
  57.6 4.2 %all-to-all-start.1 = ((bf16[4,1024,128]{2,1,0:T(8,128)(2,1)}), bf16[4,1024,128]{2,1,0:T(8,128)(2,1)S(1)}, u32[]{:S(2)}, u32[]{:S(2)}) async-start(bf16[4,1024,128]{2,1,0:T(8,128)(2,1)} %broadcast_in_dim.19), calls=%async_computation.1 | async-start | bytes 2097152 | tf_op jit(solution)/shard_map/all_to_all | solution.py:203
  61.8 1.2 broadcast_select_fusion.3
  63.9 2.9 %collective-permute-start.3 = (bf16[48,1024]{1,0:T(8,128)(2,1)}, bf16[48,1024]{1,0:T(8,128)(2,1)S(1)}, u32[]{:S(2)}, u32[]{:S(2)}) collective-permute-start(bf16[48,1024]{1,0:T(8,128)(2,1)} %get-tuple-element.100), channel_id=1, source_target_pairs={{0,2},{2,0},{1,3},{3,1},{4,6},{6,4},{5,7},{7,5},{8,10},{10,8},{9,1... | collective-permute-start | bytes 294920 | tf_op jit(solution)/shard_map/ppermute | solution.py:213
  66.8 4.7 %collective-permute-start.4 = (bf16[48,1024]{1,0:T(8,128)(2,1)}, bf16[48,1024]{1,0:T(8,128)(2,1)}, u32[]{:S(2)}, u32[]{:S(2)}) collective-permute-start(bf16[48,1024]{1,0:T(8,128)(2,1)} %get-tuple-element.99), channel_id=1, source_target_pairs={{2,4},{4,2},{3,5},{5,3},{6,8},{8,6},{7,9},{9,7},{10,12},{12,10},{1... | collective-permute-start | bytes 294920 | tf_op jit(solution)/shard_map/ppermute | solution.py:213
  71.5 6.0 %all-to-all-done.1.refs_6_ = bf16[4,1024,128]{2,1,0:T(8,128)(2,1)S(1)} async-done(((bf16[4,1024,128]{2,1,0:T(8,128)(2,1)}), bf16[4,1024,128]{2,1,0:T(8,128)(2,1)S(1)}, u32[]{:S(2)}, u32[]{:S(2)}) %all-to-all-start.1) | async-done | bytes 1048608 | tf_op jit(solution)/shard_map/all_to_all | solution.py:203
  77.6 1.1 broadcast_in_dim.17
  78.7 4.2 %all-to-all-start.2 = ((bf16[4,1024,128]{2,1,0:T(8,128)(2,1)}), bf16[4,1024,128]{2,1,0:T(8,128)(2,1)}, u32[]{:S(2)}, u32[]{:S(2)}) async-start(bf16[4,1024,128]{2,1,0:T(8,128)(2,1)} %broadcast_in_dim.17), calls=%async_computation.2 | async-start | bytes 2097152 | tf_op jit(solution)/shard_map/all_to_all | solution.py:203
  83.0 1.8 broadcast_select_fusion.1
  84.8 1.1 fusion.8
  86.3 1.8 half_finish.2.mine
  88.1 1.9 collective-permute-start.5
  90.1 1.5 collective-permute-done.5.theirs
  91.6 0.9 join.2
  92.5 2.4 %collective-permute-start.6 = (bf16[48,1024]{1,0:T(8,128)(2,1)}, bf16[48,1024]{1,0:T(8,128)(2,1)S(1)}, u32[]{:S(2)}, u32[]{:S(2)}) collective-permute-start(bf16[48,1024]{1,0:T(8,128)(2,1)} %get-tuple-element.51), channel_id=1, source_target_pairs={{0,2},{2,0},{1,3},{3,1},{4,6},{6,4},{5,7},{7,5},{8,10},{10,8},{9,1... | collective-permute-start | bytes 294920 | tf_op jit(solution)/shard_map/ppermute | solution.py:213
  95.0 4.4 %collective-permute-start.7 = (bf16[48,1024]{1,0:T(8,128)(2,1)S(1)}, bf16[48,1024]{1,0:T(8,128)(2,1)S(1)}, u32[]{:S(2)}, u32[]{:S(2)}) collective-permute-start(bf16[48,1024]{1,0:T(8,128)(2,1)S(1)} %get-tuple-element.52), channel_id=1, source_target_pairs={{2,4},{4,2},{3,5},{5,3},{6,8},{8,6},{7,9},{9,7},{10,12},{12,10},{1... | collective-permute-start | bytes 294920 | tf_op jit(solution)/shard_map/ppermute | solution.py:213
  99.4 0.9 copy-done.5
  100.8 1.3 collective-permute-done.6.refs_2_
  102.1 5.2 %collective-permute-done.7.refs_3_ = bf16[48,1024]{1,0:T(8,128)(2,1)S(1)} collective-permute-done((bf16[48,1024]{1,0:T(8,128)(2,1)S(1)}, bf16[48,1024]{1,0:T(8,128)(2,1)S(1)}, u32[]{:S(2)}, u32[]{:S(2)}) %collective-permute-start.7) | collective-permute-done | bytes 98336 | tf_op jit(solution)/shard_map/ppermute | solution.py:213
  107.2 2.9 %half_finish.3.mine = bf16[256,512]{1,0:T(8,128)(2,1)} custom-call(s32[1]{0:T(128)} %bitcast.refs_0_.core, f32[256,1024]{1,0:T(8,128)S(1)} %begin.9.refs_1_, bf16[48,1024]{1,0:T(8,128)(2,1)S(1)} %collective-permute-done.6.refs_2_, bf16[48,1024]{1,0:T(8,128)(2,1)S(1)} %collective-permute-done.7.refs_3_, bf16[256,96]{1,0:T(8,128)(2,1)S(1)} %copy.50.refs_4_.refs_3_, ...), custom_call_target="tpu_custom_call" | custom-call | tf_op jit(solution)/shard_map/half_finish/pallas_call | solution.py:64
  110.1 1.9 collective-permute-start.8
  112.8 1.1 collective-permute-done.8.theirs
  113.9 1.9 join.3
  115.8 4.6 %collective-permute-start.10 = (bf16[48,1024]{1,0:T(8,128)(2,1)}, bf16[48,1024]{1,0:T(8,128)(2,1)S(1)}, u32[]{:S(2)}, u32[]{:S(2)}) collective-permute-start(bf16[48,1024]{1,0:T(8,128)(2,1)} %get-tuple-element.57), channel_id=1, source_target_pairs={{2,4},{4,2},{3,5},{5,3},{6,8},{8,6},{7,9},{9,7},{10,12},{12,10},{1... | collective-permute-start | bytes 294920 | tf_op jit(solution)/shard_map/ppermute | solution.py:213
  120.5 1.9 collective-permute-start.9
  123.1 1.8 begin.10
  125.0 1.2 collective-permute-done.10.refs_2_
  126.2 0.8 collective-permute-done.9.refs_1_
  127.0 2.0 finish.6
  129.0 2.1 collective-permute-start.11
  131.1 4.6 %collective-permute-start.12 = (bf16[48,1024]{1,0:T(8,128)(2,1)S(1)}, bf16[48,1024]{1,0:T(8,128)(2,1)S(1)}, u32[]{:S(2)}, u32[]{:S(2)}) collective-permute-start(bf16[48,1024]{1,0:T(8,128)(2,1)S(1)} %get-tuple-element.62), channel_id=1, source_target_pairs={{2,4},{4,2},{3,5},{5,3},{6,8},{8,6},{7,9},{9,7},{10,12},{12,10},{1... | collective-permute-start | bytes 294920 | tf_op jit(solution)/shard_map/ppermute | solution.py:213
  135.7 1.8 begin.11
  138.3 2.6 %collective-permute-done.12.refs_2_ = bf16[48,1024]{1,0:T(8,128)(2,1)S(1)} collective-permute-done((bf16[48,1024]{1,0:T(8,128)(2,1)S(1)}, bf16[48,1024]{1,0:T(8,128)(2,1)S(1)}, u32[]{:S(2)}, u32[]{:S(2)}) %collective-permute-start.12) | collective-permute-done | bytes 98336 | tf_op jit(solution)/shard_map/ppermute | solution.py:213
  140.9 2.0 finish.7
  143.0 1.9 collective-permute-start.13
  144.9 4.8 %collective-permute-start.14 = (bf16[48,1024]{1,0:T(8,128)(2,1)S(1)}, bf16[48,1024]{1,0:T(8,128)(2,1)S(1)}, u32[]{:S(2)}, u32[]{:S(2)}) collective-permute-start(bf16[48,1024]{1,0:T(8,128)(2,1)S(1)} %get-tuple-element.67), channel_id=1, source_target_pairs={{2,4},{4,2},{3,5},{5,3},{6,8},{8,6},{7,9},{9,7},{10,12},{12,10},{1... | collective-permute-start | bytes 294920 | tf_op jit(solution)/shard_map/ppermute | solution.py:213
  149.7 1.8 begin.12
  152.3 2.4 %collective-permute-done.14.refs_2_ = bf16[48,1024]{1,0:T(8,128)(2,1)S(1)} collective-permute-done((bf16[48,1024]{1,0:T(8,128)(2,1)S(1)}, bf16[48,1024]{1,0:T(8,128)(2,1)S(1)}, u32[]{:S(2)}, u32[]{:S(2)}) %collective-permute-start.14) | collective-permute-done | bytes 98336 | tf_op jit(solution)/shard_map/ppermute | solution.py:213
  154.7 2.0 finish.8
  156.7 1.9 collective-permute-start.15
  158.6 4.6 %collective-permute-start.16 = (bf16[48,1024]{1,0:T(8,128)(2,1)S(1)}, bf16[48,1024]{1,0:T(8,128)(2,1)S(1)}, u32[]{:S(2)}, u32[]{:S(2)}) collective-permute-start(bf16[48,1024]{1,0:T(8,128)(2,1)S(1)} %get-tuple-element.72), channel_id=1, source_target_pairs={{2,4},{4,2},{3,5},{5,3},{6,8},{8,6},{7,9},{9,7},{10,12},{12,10},{1... | collective-permute-start | bytes 294920 | tf_op jit(solution)/shard_map/ppermute | solution.py:213
  163.3 1.8 begin.13
  165.8 2.6 %collective-permute-done.16.refs_2_ = bf16[48,1024]{1,0:T(8,128)(2,1)S(1)} collective-permute-done((bf16[48,1024]{1,0:T(8,128)(2,1)S(1)}, bf16[48,1024]{1,0:T(8,128)(2,1)S(1)}, u32[]{:S(2)}, u32[]{:S(2)}) %collective-permute-start.16) | collective-permute-done | bytes 98336 | tf_op jit(solution)/shard_map/ppermute | solution.py:213
  168.5 2.0 finish.9
  170.5 1.9 collective-permute-start.17
  172.4 4.6 %collective-permute-start.18 = (bf16[48,1024]{1,0:T(8,128)(2,1)S(1)}, bf16[48,1024]{1,0:T(8,128)(2,1)S(1)}, u32[]{:S(2)}, u32[]{:S(2)}) collective-permute-start(bf16[48,1024]{1,0:T(8,128)(2,1)S(1)} %get-tuple-element.77), channel_id=1, source_target_pairs={{2,4},{4,2},{3,5},{5,3},{6,8},{8,6},{7,9},{9,7},{10,12},{12,10},{1... | collective-permute-start | bytes 294920 | tf_op jit(solution)/shard_map/ppermute | solution.py:213
  177.0 1.8 begin.14
  179.6 2.6 %collective-permute-done.18.refs_2_ = bf16[48,1024]{1,0:T(8,128)(2,1)S(1)} collective-permute-done((bf16[48,1024]{1,0:T(8,128)(2,1)S(1)}, bf16[48,1024]{1,0:T(8,128)(2,1)S(1)}, u32[]{:S(2)}, u32[]{:S(2)}) %collective-permute-start.18) | collective-permute-done | bytes 98336 | tf_op jit(solution)/shard_map/ppermute | solution.py:213
  182.3 2.0 finish.10
  184.3 1.9 collective-permute-start.19
  186.2 4.6 %collective-permute-start.20 = (bf16[48,1024]{1,0:T(8,128)(2,1)S(1)}, bf16[48,1024]{1,0:T(8,128)(2,1)S(1)}, u32[]{:S(2)}, u32[]{:S(2)}) collective-permute-start(bf16[48,1024]{1,0:T(8,128)(2,1)S(1)} %get-tuple-element.82), channel_id=1, source_target_pairs={{2,4},{4,2},{3,5},{5,3},{6,8},{8,6},{7,9},{9,7},{10,12},{12,10},{1... | collective-permute-start | bytes 294920 | tf_op jit(solution)/shard_map/ppermute | solution.py:213
  190.8 1.8 begin.15
  193.4 2.6 %collective-permute-done.20.refs_2_ = bf16[48,1024]{1,0:T(8,128)(2,1)S(1)} collective-permute-done((bf16[48,1024]{1,0:T(8,128)(2,1)S(1)}, bf16[48,1024]{1,0:T(8,128)(2,1)S(1)}, u32[]{:S(2)}, u32[]{:S(2)}) %collective-permute-start.20) | collective-permute-done | bytes 98336 | tf_op jit(solution)/shard_map/ppermute | solution.py:213
  196.0 2.7 %finish.11 = (bf16[256,1024]{1,0:T(8,128)(2,1)S(1)}, bf16[48,1024]{1,0:T(8,128)(2,1)}, bf16[48,1024]{1,0:T(8,128)(2,1)}) custom-call(f32[256,1024]{1,0:T(8,128)S(1)} %get-tuple-element.80.refs_0_, bf16[48,1024]{1,0:T(8,128)(2,1)S(1)} %collective-permute-done.19.refs_1_, bf16[48,1024]{1,0:T(8,128)(2,1)S(1)} %collective-permute-done.20.refs_2_, ...), custom_call_target="tpu_custom_call" | custom-call | tf_op jit(solution)/shard_map/finish/pallas_call | solution.py:129
  199.4 24.4 %all_to_all.33 = bf16[8,128,1024]{2,1,0:T(8,128)(2,1)S(1)} all-to-all(bf16[8,128,1024]{2,1,0:T(8,128)(2,1)} %bitcast_dynamic-update-slice_fusion), channel_id=1, replica_groups=mesh['segment'=4,'graph'=128] {'segment'}, dimensions={0} | all-to-all | bytes 4194304 | tf_op jit(solution)/shard_map/all_to_all | solution.py:328
  223.8 1.5 copy.65
  (83 shorter events, 13.4 us)
Async XLA Ops:
  6.5 10.6 %copy-start = (bf16[8,64,1024]{2,1,0:T(8,128)(2,1)S(1)}, bf16[8,64,1024]{2,1,0:T(8,128)(2,1)}, u32[]{:S(2)}) copy-start(bf16[8,64,1024]{2,1,0:T(8,128)(2,1)} %param.10) | copy-start | bytes 3145732
  6.5 13.9 %slice-start = ((bf16[8,8,1024]{2,1,0:T(8,128)(2,1)}), bf16[2,8,1024]{2,1,0:T(8,128)(2,1)S(1)}, s32[]{:S(2)}) async-start(bf16[8,8,1024]{2,1,0:T(8,128)(2,1)} %param.9), calls=%async_computation.5 | async-start | bytes 65536 | tf_op jit(solution)/shard_map/slice | solution.py:191
  6.5 116.6 %all-gather.2.cloned.1.call-start = ((), (), s32[]{:S(2)}) async-start(), calls=%async_computation.4 | async-start | bytes 12681216 | tf_op jit(solution)/shard_map/all_gather | solution.py:187
  11.1 27.7 %collective-permute-start.1 = (bf16[272,128]{1,0:T(8,128)(2,1)S(1)}, bf16[272,128]{1,0:T(8,128)(2,1)S(1)}, u32[]{:S(2)}, u32[]{:S(2)}) collective-permute-start(bf16[272,128]{1,0:T(8,128)(2,1)S(1)} %fusion.19), channel_id=1, source_target_pairs={{0,1},{1,0},{2,3},{3,2},{4,5},{5,4},{6,7},{7,6},{8,9},{9,8},{10,11... | collective-permute-start | bytes 208904 | tf_op jit(solution)/shard_map/ppermute | solution.py:206
  14.0 47.8 %collective-permute-start = (bf16[128,1024]{1,0:T(8,128)(2,1)S(1)}, bf16[128,1024]{1,0:T(8,128)(2,1)}, u32[]{:S(2)}, u32[]{:S(2)}) collective-permute-start(bf16[128,1024]{1,0:T(8,128)(2,1)S(1)} %constant_dynamic-slice_fusion.4), channel_id=1, source_target_pairs={{0,1},{1,0},{2,3},{3,2},{4,5},{5,4},{6,7},{7,6},{8,9},{9,8},{10,11... | collective-permute-start | bytes 786440 | tf_op jit(solution)/shard_map/ppermute | solution.py:206
  18.6 64.4 %collective-permute-start.2 = (bf16[8,64,1024]{2,1,0:T(8,128)(2,1)}, bf16[8,64,1024]{2,1,0:T(8,128)(2,1)}, u32[]{:S(2)}, u32[]{:S(2)}) collective-permute-start(bf16[8,64,1024]{2,1,0:T(8,128)(2,1)} %fusion), channel_id=1, source_target_pairs={{0,1},{1,0},{2,3},{3,2},{4,5},{5,4},{6,7},{7,6},{8,9},{9,8},{10,11... | collective-permute-start | bytes 3145736 | tf_op jit(solution)/shard_map/ppermute | solution.py:206
  21.3 35.1 %all-to-all-start = ((bf16[128,8,256]{2,1,0:T(8,128)(2,1)}), bf16[128,8,256]{2,1,0:T(8,128)(2,1)S(1)}, u32[]{:S(2)}, u32[]{:S(2)}) async-start(bf16[128,8,256]{2,1,0:T(8,128)(2,1)} %bitcast.5), calls=%async_computation | async-start | bytes 1048576 | tf_op jit(solution)/shard_map/all_to_all | solution.py:196
  57.6 20.0 %all-to-all-start.1 = ((bf16[4,1024,128]{2,1,0:T(8,128)(2,1)}), bf16[4,1024,128]{2,1,0:T(8,128)(2,1)S(1)}, u32[]{:S(2)}, u32[]{:S(2)}) async-start(bf16[4,1024,128]{2,1,0:T(8,128)(2,1)} %broadcast_in_dim.19), calls=%async_computation.1 | async-start | bytes 2097152 | tf_op jit(solution)/shard_map/all_to_all | solution.py:203
  61.8 16.9 %copy-start.6 = (bf16[48,256]{1,0:T(8,128)(2,1)}, bf16[48,256]{1,0:T(8,128)(2,1)S(1)}, u32[]{:S(2)}) copy-start(bf16[48,256]{1,0:T(8,128)(2,1)S(1)} %get-tuple-element.111) | copy-start | bytes 73732
  61.8 16.9 %copy-start.8 = (bf16[48,256]{1,0:T(8,128)(2,1)}, bf16[48,256]{1,0:T(8,128)(2,1)S(1)}, u32[]{:S(2)}) copy-start(bf16[48,256]{1,0:T(8,128)(2,1)S(1)} %get-tuple-element.112) | copy-start | bytes 73732
  63.9 22.4 %collective-permute-start.3 = (bf16[48,1024]{1,0:T(8,128)(2,1)}, bf16[48,1024]{1,0:T(8,128)(2,1)S(1)}, u32[]{:S(2)}, u32[]{:S(2)}) collective-permute-start(bf16[48,1024]{1,0:T(8,128)(2,1)} %get-tuple-element.100), channel_id=1, source_target_pairs={{0,2},{2,0},{1,3},{3,1},{4,6},{6,4},{5,7},{7,5},{8,10},{10,8},{9,1... | collective-permute-start | bytes 294920 | tf_op jit(solution)/shard_map/ppermute | solution.py:213
  66.8 19.5 %collective-permute-start.4 = (bf16[48,1024]{1,0:T(8,128)(2,1)}, bf16[48,1024]{1,0:T(8,128)(2,1)}, u32[]{:S(2)}, u32[]{:S(2)}) collective-permute-start(bf16[48,1024]{1,0:T(8,128)(2,1)} %get-tuple-element.99), channel_id=1, source_target_pairs={{2,4},{4,2},{3,5},{5,3},{6,8},{8,6},{7,9},{9,7},{10,12},{12,10},{1... | collective-permute-start | bytes 294920 | tf_op jit(solution)/shard_map/ppermute | solution.py:213
  78.7 20.7 %all-to-all-start.2 = ((bf16[4,1024,128]{2,1,0:T(8,128)(2,1)}), bf16[4,1024,128]{2,1,0:T(8,128)(2,1)}, u32[]{:S(2)}, u32[]{:S(2)}) async-start(bf16[4,1024,128]{2,1,0:T(8,128)(2,1)} %broadcast_in_dim.17), calls=%async_computation.2 | async-start | bytes 2097152 | tf_op jit(solution)/shard_map/all_to_all | solution.py:203
  85.9 4.2 %copy-start.7 = (bf16[48,256]{1,0:T(8,128)(2,1)S(1)}, bf16[48,256]{1,0:T(8,128)(2,1)}, u32[]{:S(2)}) copy-start(bf16[48,256]{1,0:T(8,128)(2,1)} %copy-done.6) | copy-start | bytes 73732
  85.9 4.2 %copy-start.9 = (bf16[48,256]{1,0:T(8,128)(2,1)S(1)}, bf16[48,256]{1,0:T(8,128)(2,1)}, u32[]{:S(2)}) copy-start(bf16[48,256]{1,0:T(8,128)(2,1)} %copy-done.8) | copy-start | bytes 73732
  88.1 3.5 %collective-permute-start.5 = (bf16[256,512]{1,0:T(8,128)(2,1)S(1)}, bf16[256,512]{1,0:T(8,128)(2,1)S(1)}, u32[]{:S(2)}, u32[]{:S(2)}) collective-permute-start(bf16[256,512]{1,0:T(8,128)(2,1)S(1)} %half_finish.2.mine), channel_id=1, source_target_pairs={{0,1},{1,0},{2,3},{3,2},{4,5},{5,4},{6,7},{7,6},{8,9},{9,8},{10,11... | collective-permute-start | bytes 786440 | tf_op jit(solution)/shard_map/ppermute | solution.py:206
  92.5 9.5 %collective-permute-start.6 = (bf16[48,1024]{1,0:T(8,128)(2,1)}, bf16[48,1024]{1,0:T(8,128)(2,1)S(1)}, u32[]{:S(2)}, u32[]{:S(2)}) collective-permute-start(bf16[48,1024]{1,0:T(8,128)(2,1)} %get-tuple-element.51), channel_id=1, source_target_pairs={{0,2},{2,0},{1,3},{3,1},{4,6},{6,4},{5,7},{7,5},{8,10},{10,8},{9,1... | collective-permute-start | bytes 294920 | tf_op jit(solution)/shard_map/ppermute | solution.py:213
  95.0 12.2 %collective-permute-start.7 = (bf16[48,1024]{1,0:T(8,128)(2,1)S(1)}, bf16[48,1024]{1,0:T(8,128)(2,1)S(1)}, u32[]{:S(2)}, u32[]{:S(2)}) collective-permute-start(bf16[48,1024]{1,0:T(8,128)(2,1)S(1)} %get-tuple-element.52), channel_id=1, source_target_pairs={{2,4},{4,2},{3,5},{5,3},{6,8},{8,6},{7,9},{9,7},{10,12},{12,10},{1... | collective-permute-start | bytes 294920 | tf_op jit(solution)/shard_map/ppermute | solution.py:213
  99.4 1.0 copy-start.5
  100.8 22.3 %copy-start.4 = (bf16[128,1024]{1,0:T(8,128)(2,1)S(1)}, bf16[128,1024]{1,0:T(8,128)(2,1)}, u32[]{:S(2)}) copy-start(bf16[128,1024]{1,0:T(8,128)(2,1)} %get-tuple-element.88.refs_3_) | copy-start | bytes 786436
  110.1 3.8 %collective-permute-start.8 = (bf16[256,512]{1,0:T(8,128)(2,1)}, bf16[256,512]{1,0:T(8,128)(2,1)}, u32[]{:S(2)}, u32[]{:S(2)}) collective-permute-start(bf16[256,512]{1,0:T(8,128)(2,1)} %half_finish.3.mine), channel_id=1, source_target_pairs={{0,1},{1,0},{2,3},{3,2},{4,5},{5,4},{6,7},{7,6},{8,9},{9,8},{10,11... | collective-permute-start | bytes 786440 | tf_op jit(solution)/shard_map/ppermute | solution.py:206
  115.8 10.3 %collective-permute-start.10 = (bf16[48,1024]{1,0:T(8,128)(2,1)}, bf16[48,1024]{1,0:T(8,128)(2,1)S(1)}, u32[]{:S(2)}, u32[]{:S(2)}) collective-permute-start(bf16[48,1024]{1,0:T(8,128)(2,1)} %get-tuple-element.57), channel_id=1, source_target_pairs={{2,4},{4,2},{3,5},{5,3},{6,8},{8,6},{7,9},{9,7},{10,12},{12,10},{1... | collective-permute-start | bytes 294920 | tf_op jit(solution)/shard_map/ppermute | solution.py:213
  120.5 6.5 %collective-permute-start.9 = (bf16[48,1024]{1,0:T(8,128)(2,1)S(1)}, bf16[48,1024]{1,0:T(8,128)(2,1)S(1)}, u32[]{:S(2)}, u32[]{:S(2)}) collective-permute-start(bf16[48,1024]{1,0:T(8,128)(2,1)S(1)} %get-tuple-element.56), channel_id=1, source_target_pairs={{0,2},{2,0},{1,3},{3,1},{4,6},{6,4},{5,7},{7,5},{8,10},{10,8},{9,1... | collective-permute-start | bytes 294920 | tf_op jit(solution)/shard_map/ppermute | solution.py:213
  125.0 10.7 %copy-start.3 = (bf16[128,1024]{1,0:T(8,128)(2,1)S(1)}, bf16[128,1024]{1,0:T(8,128)(2,1)}, u32[]{:S(2)}) copy-start(bf16[128,1024]{1,0:T(8,128)(2,1)} %get-tuple-element.89.refs_3_) | copy-start | bytes 786436
  129.0 9.3 %collective-permute-start.11 = (bf16[48,1024]{1,0:T(8,128)(2,1)S(1)}, bf16[48,1024]{1,0:T(8,128)(2,1)S(1)}, u32[]{:S(2)}, u32[]{:S(2)}) collective-permute-start(bf16[48,1024]{1,0:T(8,128)(2,1)S(1)} %get-tuple-element.61), channel_id=1, source_target_pairs={{0,2},{2,0},{1,3},{3,1},{4,6},{6,4},{5,7},{7,5},{8,10},{10,8},{9,1... | collective-permute-start | bytes 294920 | tf_op jit(solution)/shard_map/ppermute | solution.py:213
  131.1 9.8 %collective-permute-start.12 = (bf16[48,1024]{1,0:T(8,128)(2,1)S(1)}, bf16[48,1024]{1,0:T(8,128)(2,1)S(1)}, u32[]{:S(2)}, u32[]{:S(2)}) collective-permute-start(bf16[48,1024]{1,0:T(8,128)(2,1)S(1)} %get-tuple-element.62), channel_id=1, source_target_pairs={{2,4},{4,2},{3,5},{5,3},{6,8},{8,6},{7,9},{9,7},{10,12},{12,10},{1... | collective-permute-start | bytes 294920 | tf_op jit(solution)/shard_map/ppermute | solution.py:213
  138.3 11.4 %copy-start.2 = (bf16[128,1024]{1,0:T(8,128)(2,1)S(1)}, bf16[128,1024]{1,0:T(8,128)(2,1)}, u32[]{:S(2)}) copy-start(bf16[128,1024]{1,0:T(8,128)(2,1)} %get-tuple-element.90.refs_3_) | copy-start | bytes 786436
  143.0 9.3 %collective-permute-start.13 = (bf16[48,1024]{1,0:T(8,128)(2,1)S(1)}, bf16[48,1024]{1,0:T(8,128)(2,1)S(1)}, u32[]{:S(2)}, u32[]{:S(2)}) collective-permute-start(bf16[48,1024]{1,0:T(8,128)(2,1)S(1)} %get-tuple-element.66), channel_id=1, source_target_pairs={{0,2},{2,0},{1,3},{3,1},{4,6},{6,4},{5,7},{7,5},{8,10},{10,8},{9,1... | collective-permute-start | bytes 294920 | tf_op jit(solution)/shard_map/ppermute | solution.py:213
  144.9 9.8 %collective-permute-start.14 = (bf16[48,1024]{1,0:T(8,128)(2,1)S(1)}, bf16[48,1024]{1,0:T(8,128)(2,1)S(1)}, u32[]{:S(2)}, u32[]{:S(2)}) collective-permute-start(bf16[48,1024]{1,0:T(8,128)(2,1)S(1)} %get-tuple-element.67), channel_id=1, source_target_pairs={{2,4},{4,2},{3,5},{5,3},{6,8},{8,6},{7,9},{9,7},{10,12},{12,10},{1... | collective-permute-start | bytes 294920 | tf_op jit(solution)/shard_map/ppermute | solution.py:213
  152.3 11.0 %copy-start.1 = (bf16[128,1024]{1,0:T(8,128)(2,1)S(1)}, bf16[128,1024]{1,0:T(8,128)(2,1)}, u32[]{:S(2)}) copy-start(bf16[128,1024]{1,0:T(8,128)(2,1)} %get-tuple-element.91.refs_3_) | copy-start | bytes 786436
  156.7 9.1 %collective-permute-start.15 = (bf16[48,1024]{1,0:T(8,128)(2,1)S(1)}, bf16[48,1024]{1,0:T(8,128)(2,1)S(1)}, u32[]{:S(2)}, u32[]{:S(2)}) collective-permute-start(bf16[48,1024]{1,0:T(8,128)(2,1)S(1)} %get-tuple-element.71), channel_id=1, source_target_pairs={{0,2},{2,0},{1,3},{3,1},{4,6},{6,4},{5,7},{7,5},{8,10},{10,8},{9,1... | collective-permute-start | bytes 294920 | tf_op jit(solution)/shard_map/ppermute | solution.py:213
  158.6 9.8 %collective-permute-start.16 = (bf16[48,1024]{1,0:T(8,128)(2,1)S(1)}, bf16[48,1024]{1,0:T(8,128)(2,1)S(1)}, u32[]{:S(2)}, u32[]{:S(2)}) collective-permute-start(bf16[48,1024]{1,0:T(8,128)(2,1)S(1)} %get-tuple-element.72), channel_id=1, source_target_pairs={{2,4},{4,2},{3,5},{5,3},{6,8},{8,6},{7,9},{9,7},{10,12},{12,10},{1... | collective-permute-start | bytes 294920 | tf_op jit(solution)/shard_map/ppermute | solution.py:213
  170.5 9.1 %collective-permute-start.17 = (bf16[48,1024]{1,0:T(8,128)(2,1)S(1)}, bf16[48,1024]{1,0:T(8,128)(2,1)S(1)}, u32[]{:S(2)}, u32[]{:S(2)}) collective-permute-start(bf16[48,1024]{1,0:T(8,128)(2,1)S(1)} %get-tuple-element.76), channel_id=1, source_target_pairs={{0,2},{2,0},{1,3},{3,1},{4,6},{6,4},{5,7},{7,5},{8,10},{10,8},{9,1... | collective-permute-start | bytes 294920 | tf_op jit(solution)/shard_map/ppermute | solution.py:213
  172.4 9.8 %collective-permute-start.18 = (bf16[48,1024]{1,0:T(8,128)(2,1)S(1)}, bf16[48,1024]{1,0:T(8,128)(2,1)S(1)}, u32[]{:S(2)}, u32[]{:S(2)}) collective-permute-start(bf16[48,1024]{1,0:T(8,128)(2,1)S(1)} %get-tuple-element.77), channel_id=1, source_target_pairs={{2,4},{4,2},{3,5},{5,3},{6,8},{8,6},{7,9},{9,7},{10,12},{12,10},{1... | collective-permute-start | bytes 294920 | tf_op jit(solution)/shard_map/ppermute | solution.py:213
  184.3 9.1 %collective-permute-start.19 = (bf16[48,1024]{1,0:T(8,128)(2,1)S(1)}, bf16[48,1024]{1,0:T(8,128)(2,1)S(1)}, u32[]{:S(2)}, u32[]{:S(2)}) collective-permute-start(bf16[48,1024]{1,0:T(8,128)(2,1)S(1)} %get-tuple-element.81), channel_id=1, source_target_pairs={{0,2},{2,0},{1,3},{3,1},{4,6},{6,4},{5,7},{7,5},{8,10},{10,8},{9,1... | collective-permute-start | bytes 294920 | tf_op jit(solution)/shard_map/ppermute | solution.py:213
  186.2 9.8 %collective-permute-start.20 = (bf16[48,1024]{1,0:T(8,128)(2,1)S(1)}, bf16[48,1024]{1,0:T(8,128)(2,1)S(1)}, u32[]{:S(2)}, u32[]{:S(2)}) collective-permute-start(bf16[48,1024]{1,0:T(8,128)(2,1)S(1)} %get-tuple-element.82), channel_id=1, source_target_pairs={{2,4},{4,2},{3,5},{5,3},{6,8},{8,6},{7,9},{9,7},{10,12},{12,10},{1... | collective-permute-start | bytes 294920 | tf_op jit(solution)/shard_map/ppermute | solution.py:213
Sparse Core Ops, SparseCore 0:
  10.6 103.2 all-gather.1

commit v7 on v6

--- a/solution.py
+++ b/solution.py
@@ -62,7 +62,7 @@
 def half_finish(layer, core, local, got_a, got_b, far, start, early):
     rows, width = start.shape
     return pl.pallas_call(
-        lambda *refs: half_body(layer, min(256, width), *refs),
+        lambda *refs: half_body(layer, min(512, width), *refs),
         out_shape=pltpu.VMEM((rows, width // 2), BF),
         in_specs=[SM] + [VM] * 6,
         out_specs=VM,
@@ -127,7 +127,7 @@
     rows, width = start.shape
     edges = got_a.shape[0]
     return pl.pallas_call(
-        lambda *refs: finish_body(layer, min(256, width), *refs),
+        lambda *refs: finish_body(layer, min(512, width), *refs),
         out_shape=(
             pltpu.VMEM((rows, width), BF),
             pltpu.VMEM((edges, width), BF),
@@ -136,7 +136,7 @@
         in_specs=[VM] * 7,
         out_specs=(VM, VM, VM),
         scratch_shapes=[pltpu.VMEM((rows, width), F32), pltpu.VMEM((rows, width), BF)],
-        compiler_params=pltpu.CompilerParams(vmem_limit_bytes=6 << 20),
+        compiler_params=pltpu.CompilerParams(vmem_limit_bytes=8 << 20),
         name="finish",
     )(*in_vmem(local, got_a, got_b, far, picks, start, weight))
 

time: 234 us -> 229 us (0.979)
  Pallas kernels: 32.1 us -> 27.6 us
    pallas_call x8, Pallas kernels: 17.4 us -> 12.9 us  [the longest x6 8.17 us: finish(): pl.pallas_call(lambda *refs: finish_body(layer, min(512, width), *refs),...]
  transfers between devices with their start and end apart: 25 -> 25, of which waited for: 13 -> 13; matrix products, arithmetic and copies ran while one was open for 9% -> 9% of each run, Pallas kernels for 8% -> 9%
where the time goes in v7:
time: 229 us; the launch traced here: 228 us
  starting transfers between devices  90 us (39%)
  waiting for transfers between devices  46.4 us (20%)
  Pallas kernels  27.6 us (12%)
  blocking collectives  24.4 us (11%)
  local copies, waits for them, and re-layouts  17.8 us (8%)
  between operations  14.1 us (6%)
  other arithmetic  5.33 us (2%)
    ppermute x16, starting transfers between devices, exchange(): return lax.ppermute(value, 'graph', pairs)  54 us
    all_to_all x1, blocking collectives, shards(): return lax.all_to_all(whole, 'segment', 0, 1, tiled=True)  24.4 us
    ppermute x16, waiting for transfers between devices, exchange(): return lax.ppermute(value, 'graph', pairs)  21.4 us
    all_to_all x1, starting transfers between devices, shards(): lax.all_to_all(spread, 'graph', 0, 0, tiled=True)  17.4 us
    all_to_all x1, waiting for transfers between devices, shards(): lax.all_to_all(spread, 'graph', 0, 0, tiled=True)  16.3 us
    pallas_call x8, Pallas kernels, begin(): pl.pallas_call(lambda *refs: begin_body(layer, min(256, width), *refs), o...  11.8 us
    ppermute x5, starting transfers between devices, swap(): lax.ppermute(value, 'graph', [(p, p ^ 1) for p in range(graph_count)])  10.1 us
    all_to_all x2, starting transfers between devices, early_weight(): return (lax.all_to_all(part, 'segment', 0, 0, tiled=True), after)  8.48 us
  transfers between devices with their start and end apart: 25, of which 13 were waited for; matrix products, arithmetic and copies ran while one was open for 9% of the time, Pallas kernels for 9%

profile of v7, /device:TPU:32, one launch (start us, length us, event | category | flops | bytes accessed | tf_op | source)
XLA Modules:
  0.0 227.6 jit_solution(4137701738934633340)
XLA Ops:
  6.5 1.6 slice.146
  11.1 1.9 collective-permute-start.1
  13.0 1.0 constant_dynamic-slice_fusion.4
  14.0 2.4 %collective-permute-start = (bf16[128,1024]{1,0:T(8,128)(2,1)S(1)}, bf16[128,1024]{1,0:T(8,128)(2,1)}, u32[]{:S(2)}, u32[]{:S(2)}) collective-permute-start(bf16[128,1024]{1,0:T(8,128)(2,1)S(1)} %constant_dynamic-slice_fusion.4), channel_id=1, source_target_pairs={{0,1},{1,0},{2,3},{3,2},{4,5},{5,4},{6,7},{7,6},{8,9},{9,8},{10,11... | collective-permute-start | bytes 786440 | tf_op jit(solution)/shard_map/ppermute | solution.py:206
  17.1 1.5 fusion
  18.6 1.9 collective-permute-start.2
  21.3 17.4 %all-to-all-start = ((bf16[128,8,256]{2,1,0:T(8,128)(2,1)}), bf16[128,8,256]{2,1,0:T(8,128)(2,1)S(1)}, u32[]{:S(2)}, u32[]{:S(2)}) async-start(bf16[128,8,256]{2,1,0:T(8,128)(2,1)} %bitcast.5), calls=%async_computation | async-start | bytes 1048576 | tf_op jit(solution)/shard_map/all_to_all | solution.py:196
  40.1 16.3 %all-to-all-done = bf16[128,8,256]{2,1,0:T(8,128)(2,1)S(1)} async-done(((bf16[128,8,256]{2,1,0:T(8,128)(2,1)}), bf16[128,8,256]{2,1,0:T(8,128)(2,1)S(1)}, u32[]{:S(2)}, u32[]{:S(2)}) %all-to-all-start) | async-done | bytes 524320 | tf_op jit(solution)/shard_map/all_to_all | solution.py:196
  56.4 1.1 broadcast_in_dim.19
  57.6 4.2 %all-to-all-start.1 = ((bf16[4,1024,128]{2,1,0:T(8,128)(2,1)}), bf16[4,1024,128]{2,1,0:T(8,128)(2,1)S(1)}, u32[]{:S(2)}, u32[]{:S(2)}) async-start(bf16[4,1024,128]{2,1,0:T(8,128)(2,1)} %broadcast_in_dim.19), calls=%async_computation.1 | async-start | bytes 2097152 | tf_op jit(solution)/shard_map/all_to_all | solution.py:203
  61.8 1.2 broadcast_select_fusion.3
  63.9 2.9 %collective-permute-start.3 = (bf16[48,1024]{1,0:T(8,128)(2,1)}, bf16[48,1024]{1,0:T(8,128)(2,1)S(1)}, u32[]{:S(2)}, u32[]{:S(2)}) collective-permute-start(bf16[48,1024]{1,0:T(8,128)(2,1)} %get-tuple-element.100), channel_id=1, source_target_pairs={{0,2},{2,0},{1,3},{3,1},{4,6},{6,4},{5,7},{7,5},{8,10},{10,8},{9,1... | collective-permute-start | bytes 294920 | tf_op jit(solution)/shard_map/ppermute | solution.py:213
  66.8 4.7 %collective-permute-start.4 = (bf16[48,1024]{1,0:T(8,128)(2,1)}, bf16[48,1024]{1,0:T(8,128)(2,1)}, u32[]{:S(2)}, u32[]{:S(2)}) collective-permute-start(bf16[48,1024]{1,0:T(8,128)(2,1)} %get-tuple-element.99), channel_id=1, source_target_pairs={{2,4},{4,2},{3,5},{5,3},{6,8},{8,6},{7,9},{9,7},{10,12},{12,10},{1... | collective-permute-start | bytes 294920 | tf_op jit(solution)/shard_map/ppermute | solution.py:213
  71.5 6.0 %all-to-all-done.1.refs_6_ = bf16[4,1024,128]{2,1,0:T(8,128)(2,1)S(1)} async-done(((bf16[4,1024,128]{2,1,0:T(8,128)(2,1)}), bf16[4,1024,128]{2,1,0:T(8,128)(2,1)S(1)}, u32[]{:S(2)}, u32[]{:S(2)}) %all-to-all-start.1) | async-done | bytes 1048608 | tf_op jit(solution)/shard_map/all_to_all | solution.py:203
  77.6 1.1 broadcast_in_dim.17
  78.7 4.2 %all-to-all-start.2 = ((bf16[4,1024,128]{2,1,0:T(8,128)(2,1)}), bf16[4,1024,128]{2,1,0:T(8,128)(2,1)}, u32[]{:S(2)}, u32[]{:S(2)}) async-start(bf16[4,1024,128]{2,1,0:T(8,128)(2,1)} %broadcast_in_dim.17), calls=%async_computation.2 | async-start | bytes 2097152 | tf_op jit(solution)/shard_map/all_to_all | solution.py:203
  83.0 1.8 broadcast_select_fusion.1
  84.8 1.1 fusion.8
  86.3 1.8 half_finish.2.mine
  88.1 1.9 collective-permute-start.5
  90.1 1.5 collective-permute-done.5.theirs
  91.6 0.9 join.2
  92.5 2.4 %collective-permute-start.6 = (bf16[48,1024]{1,0:T(8,128)(2,1)}, bf16[48,1024]{1,0:T(8,128)(2,1)S(1)}, u32[]{:S(2)}, u32[]{:S(2)}) collective-permute-start(bf16[48,1024]{1,0:T(8,128)(2,1)} %get-tuple-element.51), channel_id=1, source_target_pairs={{0,2},{2,0},{1,3},{3,1},{4,6},{6,4},{5,7},{7,5},{8,10},{10,8},{9,1... | collective-permute-start | bytes 294920 | tf_op jit(solution)/shard_map/ppermute | solution.py:213
  95.0 4.4 %collective-permute-start.7 = (bf16[48,1024]{1,0:T(8,128)(2,1)S(1)}, bf16[48,1024]{1,0:T(8,128)(2,1)S(1)}, u32[]{:S(2)}, u32[]{:S(2)}) collective-permute-start(bf16[48,1024]{1,0:T(8,128)(2,1)S(1)} %get-tuple-element.52), channel_id=1, source_target_pairs={{2,4},{4,2},{3,5},{5,3},{6,8},{8,6},{7,9},{9,7},{10,12},{12,10},{1... | collective-permute-start | bytes 294920 | tf_op jit(solution)/shard_map/ppermute | solution.py:213
  99.4 0.9 copy-done.5
  100.8 1.3 collective-permute-done.6.refs_2_
  102.1 5.2 %collective-permute-done.7.refs_3_ = bf16[48,1024]{1,0:T(8,128)(2,1)S(1)} collective-permute-done((bf16[48,1024]{1,0:T(8,128)(2,1)S(1)}, bf16[48,1024]{1,0:T(8,128)(2,1)S(1)}, u32[]{:S(2)}, u32[]{:S(2)}) %collective-permute-start.7) | collective-permute-done | bytes 98336 | tf_op jit(solution)/shard_map/ppermute | solution.py:213
  107.2 2.9 %half_finish.3.mine = bf16[256,512]{1,0:T(8,128)(2,1)} custom-call(s32[1]{0:T(128)} %bitcast.refs_0_.core, f32[256,1024]{1,0:T(8,128)S(1)} %begin.9.refs_1_, bf16[48,1024]{1,0:T(8,128)(2,1)S(1)} %collective-permute-done.6.refs_2_, bf16[48,1024]{1,0:T(8,128)(2,1)S(1)} %collective-permute-done.7.refs_3_, bf16[256,96]{1,0:T(8,128)(2,1)S(1)} %copy.50.refs_4_.refs_3_, ...), custom_call_target="tpu_custom_call" | custom-call | tf_op jit(solution)/shard_map/half_finish/pallas_call | solution.py:64
  110.1 1.9 collective-permute-start.8
  112.8 1.1 collective-permute-done.8.theirs
  113.9 1.9 join.3
  115.8 4.6 %collective-permute-start.10 = (bf16[48,1024]{1,0:T(8,128)(2,1)}, bf16[48,1024]{1,0:T(8,128)(2,1)S(1)}, u32[]{:S(2)}, u32[]{:S(2)}) collective-permute-start(bf16[48,1024]{1,0:T(8,128)(2,1)} %get-tuple-element.57), channel_id=1, source_target_pairs={{2,4},{4,2},{3,5},{5,3},{6,8},{8,6},{7,9},{9,7},{10,12},{12,10},{1... | collective-permute-start | bytes 294920 | tf_op jit(solution)/shard_map/ppermute | solution.py:213
  120.5 1.9 collective-permute-start.9
  123.1 1.8 begin.10
  125.0 1.2 collective-permute-done.10.refs_2_
  126.2 0.8 collective-permute-done.9.refs_1_
  127.0 1.2 finish.6
  128.2 2.1 collective-permute-start.11
  130.4 4.6 %collective-permute-start.12 = (bf16[48,1024]{1,0:T(8,128)(2,1)S(1)}, bf16[48,1024]{1,0:T(8,128)(2,1)S(1)}, u32[]{:S(2)}, u32[]{:S(2)}) collective-permute-start(bf16[48,1024]{1,0:T(8,128)(2,1)S(1)} %get-tuple-element.62), channel_id=1, source_target_pairs={{2,4},{4,2},{3,5},{5,3},{6,8},{8,6},{7,9},{9,7},{10,12},{12,10},{1... | collective-permute-start | bytes 294920 | tf_op jit(solution)/shard_map/ppermute | solution.py:213
  135.0 1.8 begin.11
  137.6 2.6 %collective-permute-done.12.refs_2_ = bf16[48,1024]{1,0:T(8,128)(2,1)S(1)} collective-permute-done((bf16[48,1024]{1,0:T(8,128)(2,1)S(1)}, bf16[48,1024]{1,0:T(8,128)(2,1)S(1)}, u32[]{:S(2)}, u32[]{:S(2)}) %collective-permute-start.12) | collective-permute-done | bytes 98336 | tf_op jit(solution)/shard_map/ppermute | solution.py:213
  140.2 1.3 finish.7
  141.5 1.9 collective-permute-start.13
  143.4 4.6 %collective-permute-start.14 = (bf16[48,1024]{1,0:T(8,128)(2,1)S(1)}, bf16[48,1024]{1,0:T(8,128)(2,1)S(1)}, u32[]{:S(2)}, u32[]{:S(2)}) collective-permute-start(bf16[48,1024]{1,0:T(8,128)(2,1)S(1)} %get-tuple-element.67), channel_id=1, source_target_pairs={{2,4},{4,2},{3,5},{5,3},{6,8},{8,6},{7,9},{9,7},{10,12},{12,10},{1... | collective-permute-start | bytes 294920 | tf_op jit(solution)/shard_map/ppermute | solution.py:213
  148.0 1.8 begin.12
  150.6 2.6 %collective-permute-done.14.refs_2_ = bf16[48,1024]{1,0:T(8,128)(2,1)S(1)} collective-permute-done((bf16[48,1024]{1,0:T(8,128)(2,1)S(1)}, bf16[48,1024]{1,0:T(8,128)(2,1)S(1)}, u32[]{:S(2)}, u32[]{:S(2)}) %collective-permute-start.14) | collective-permute-done | bytes 98336 | tf_op jit(solution)/shard_map/ppermute | solution.py:213
  153.2 1.3 finish.8
  154.5 1.9 collective-permute-start.15
  156.4 4.8 %collective-permute-start.16 = (bf16[48,1024]{1,0:T(8,128)(2,1)S(1)}, bf16[48,1024]{1,0:T(8,128)(2,1)S(1)}, u32[]{:S(2)}, u32[]{:S(2)}) collective-permute-start(bf16[48,1024]{1,0:T(8,128)(2,1)S(1)} %get-tuple-element.72), channel_id=1, source_target_pairs={{2,4},{4,2},{3,5},{5,3},{6,8},{8,6},{7,9},{9,7},{10,12},{12,10},{1... | collective-permute-start | bytes 294920 | tf_op jit(solution)/shard_map/ppermute | solution.py:213
  161.2 1.8 begin.13
  163.8 2.4 %collective-permute-done.16.refs_2_ = bf16[48,1024]{1,0:T(8,128)(2,1)S(1)} collective-permute-done((bf16[48,1024]{1,0:T(8,128)(2,1)S(1)}, bf16[48,1024]{1,0:T(8,128)(2,1)S(1)}, u32[]{:S(2)}, u32[]{:S(2)}) %collective-permute-start.16) | collective-permute-done | bytes 98336 | tf_op jit(solution)/shard_map/ppermute | solution.py:213
  166.2 1.3 finish.9
  167.5 1.9 collective-permute-start.17
  169.4 4.6 %collective-permute-start.18 = (bf16[48,1024]{1,0:T(8,128)(2,1)S(1)}, bf16[48,1024]{1,0:T(8,128)(2,1)S(1)}, u32[]{:S(2)}, u32[]{:S(2)}) collective-permute-start(bf16[48,1024]{1,0:T(8,128)(2,1)S(1)} %get-tuple-element.77), channel_id=1, source_target_pairs={{2,4},{4,2},{3,5},{5,3},{6,8},{8,6},{7,9},{9,7},{10,12},{12,10},{1... | collective-permute-start | bytes 294920 | tf_op jit(solution)/shard_map/ppermute | solution.py:213
  174.0 1.8 begin.14
  176.6 2.6 %collective-permute-done.18.refs_2_ = bf16[48,1024]{1,0:T(8,128)(2,1)S(1)} collective-permute-done((bf16[48,1024]{1,0:T(8,128)(2,1)S(1)}, bf16[48,1024]{1,0:T(8,128)(2,1)S(1)}, u32[]{:S(2)}, u32[]{:S(2)}) %collective-permute-start.18) | collective-permute-done | bytes 98336 | tf_op jit(solution)/shard_map/ppermute | solution.py:213
  179.3 1.3 finish.10
  180.5 1.9 collective-permute-start.19
  182.5 4.6 %collective-permute-start.20 = (bf16[48,1024]{1,0:T(8,128)(2,1)S(1)}, bf16[48,1024]{1,0:T(8,128)(2,1)S(1)}, u32[]{:S(2)}, u32[]{:S(2)}) collective-permute-start(bf16[48,1024]{1,0:T(8,128)(2,1)S(1)} %get-tuple-element.82), channel_id=1, source_target_pairs={{2,4},{4,2},{3,5},{5,3},{6,8},{8,6},{7,9},{9,7},{10,12},{12,10},{1... | collective-permute-start | bytes 294920 | tf_op jit(solution)/shard_map/ppermute | solution.py:213
  187.1 1.8 begin.15
  189.7 2.6 %collective-permute-done.20.refs_2_ = bf16[48,1024]{1,0:T(8,128)(2,1)S(1)} collective-permute-done((bf16[48,1024]{1,0:T(8,128)(2,1)S(1)}, bf16[48,1024]{1,0:T(8,128)(2,1)S(1)}, u32[]{:S(2)}, u32[]{:S(2)}) %collective-permute-start.20) | collective-permute-done | bytes 98336 | tf_op jit(solution)/shard_map/ppermute | solution.py:213
  192.3 1.9 finish.11
  194.9 24.4 %all_to_all.33 = bf16[8,128,1024]{2,1,0:T(8,128)(2,1)S(1)} all-to-all(bf16[8,128,1024]{2,1,0:T(8,128)(2,1)} %bitcast_dynamic-update-slice_fusion), channel_id=1, replica_groups=mesh['segment'=4,'graph'=128] {'segment'}, dimensions={0} | all-to-all | bytes 4194304 | tf_op jit(solution)/shard_map/all_to_all | solution.py:328
  219.3 1.5 copy.65
  (83 shorter events, 13.4 us)
Async XLA Ops:
  6.5 10.6 %copy-start = (bf16[8,64,1024]{2,1,0:T(8,128)(2,1)S(1)}, bf16[8,64,1024]{2,1,0:T(8,128)(2,1)}, u32[]{:S(2)}) copy-start(bf16[8,64,1024]{2,1,0:T(8,128)(2,1)} %param.10) | copy-start | bytes 3145732
  6.5 13.9 %slice-start = ((bf16[8,8,1024]{2,1,0:T(8,128)(2,1)}), bf16[2,8,1024]{2,1,0:T(8,128)(2,1)S(1)}, s32[]{:S(2)}) async-start(bf16[8,8,1024]{2,1,0:T(8,128)(2,1)} %param.9), calls=%async_computation.5 | async-start | bytes 65536 | tf_op jit(solution)/shard_map/slice | solution.py:191
  6.5 116.6 %all-gather.2.cloned.1.call-start = ((), (), s32[]{:S(2)}) async-start(), calls=%async_computation.4 | async-start | bytes 12681216 | tf_op jit(solution)/shard_map/all_gather | solution.py:187
  11.1 27.7 %collective-permute-start.1 = (bf16[272,128]{1,0:T(8,128)(2,1)S(1)}, bf16[272,128]{1,0:T(8,128)(2,1)S(1)}, u32[]{:S(2)}, u32[]{:S(2)}) collective-permute-start(bf16[272,128]{1,0:T(8,128)(2,1)S(1)} %fusion.19), channel_id=1, source_target_pairs={{0,1},{1,0},{2,3},{3,2},{4,5},{5,4},{6,7},{7,6},{8,9},{9,8},{10,11... | collective-permute-start | bytes 208904 | tf_op jit(solution)/shard_map/ppermute | solution.py:206
  14.0 47.8 %collective-permute-start = (bf16[128,1024]{1,0:T(8,128)(2,1)S(1)}, bf16[128,1024]{1,0:T(8,128)(2,1)}, u32[]{:S(2)}, u32[]{:S(2)}) collective-permute-start(bf16[128,1024]{1,0:T(8,128)(2,1)S(1)} %constant_dynamic-slice_fusion.4), channel_id=1, source_target_pairs={{0,1},{1,0},{2,3},{3,2},{4,5},{5,4},{6,7},{7,6},{8,9},{9,8},{10,11... | collective-permute-start | bytes 786440 | tf_op jit(solution)/shard_map/ppermute | solution.py:206
  18.6 64.4 %collective-permute-start.2 = (bf16[8,64,1024]{2,1,0:T(8,128)(2,1)}, bf16[8,64,1024]{2,1,0:T(8,128)(2,1)}, u32[]{:S(2)}, u32[]{:S(2)}) collective-permute-start(bf16[8,64,1024]{2,1,0:T(8,128)(2,1)} %fusion), channel_id=1, source_target_pairs={{0,1},{1,0},{2,3},{3,2},{4,5},{5,4},{6,7},{7,6},{8,9},{9,8},{10,11... | collective-permute-start | bytes 3145736 | tf_op jit(solution)/shard_map/ppermute | solution.py:206
  21.3 35.1 %all-to-all-start = ((bf16[128,8,256]{2,1,0:T(8,128)(2,1)}), bf16[128,8,256]{2,1,0:T(8,128)(2,1)S(1)}, u32[]{:S(2)}, u32[]{:S(2)}) async-start(bf16[128,8,256]{2,1,0:T(8,128)(2,1)} %bitcast.5), calls=%async_computation | async-start | bytes 1048576 | tf_op jit(solution)/shard_map/all_to_all | solution.py:196
  57.6 20.0 %all-to-all-start.1 = ((bf16[4,1024,128]{2,1,0:T(8,128)(2,1)}), bf16[4,1024,128]{2,1,0:T(8,128)(2,1)S(1)}, u32[]{:S(2)}, u32[]{:S(2)}) async-start(bf16[4,1024,128]{2,1,0:T(8,128)(2,1)} %broadcast_in_dim.19), calls=%async_computation.1 | async-start | bytes 2097152 | tf_op jit(solution)/shard_map/all_to_all | solution.py:203
  61.8 16.9 %copy-start.6 = (bf16[48,256]{1,0:T(8,128)(2,1)}, bf16[48,256]{1,0:T(8,128)(2,1)S(1)}, u32[]{:S(2)}) copy-start(bf16[48,256]{1,0:T(8,128)(2,1)S(1)} %get-tuple-element.111) | copy-start | bytes 73732
  61.8 16.9 %copy-start.8 = (bf16[48,256]{1,0:T(8,128)(2,1)}, bf16[48,256]{1,0:T(8,128)(2,1)S(1)}, u32[]{:S(2)}) copy-start(bf16[48,256]{1,0:T(8,128)(2,1)S(1)} %get-tuple-element.112) | copy-start | bytes 73732
  63.9 22.4 %collective-permute-start.3 = (bf16[48,1024]{1,0:T(8,128)(2,1)}, bf16[48,1024]{1,0:T(8,128)(2,1)S(1)}, u32[]{:S(2)}, u32[]{:S(2)}) collective-permute-start(bf16[48,1024]{1,0:T(8,128)(2,1)} %get-tuple-element.100), channel_id=1, source_target_pairs={{0,2},{2,0},{1,3},{3,1},{4,6},{6,4},{5,7},{7,5},{8,10},{10,8},{9,1... | collective-permute-start | bytes 294920 | tf_op jit(solution)/shard_map/ppermute | solution.py:213
  66.8 19.5 %collective-permute-start.4 = (bf16[48,1024]{1,0:T(8,128)(2,1)}, bf16[48,1024]{1,0:T(8,128)(2,1)}, u32[]{:S(2)}, u32[]{:S(2)}) collective-permute-start(bf16[48,1024]{1,0:T(8,128)(2,1)} %get-tuple-element.99), channel_id=1, source_target_pairs={{2,4},{4,2},{3,5},{5,3},{6,8},{8,6},{7,9},{9,7},{10,12},{12,10},{1... | collective-permute-start | bytes 294920 | tf_op jit(solution)/shard_map/ppermute | solution.py:213
  78.7 20.7 %all-to-all-start.2 = ((bf16[4,1024,128]{2,1,0:T(8,128)(2,1)}), bf16[4,1024,128]{2,1,0:T(8,128)(2,1)}, u32[]{:S(2)}, u32[]{:S(2)}) async-start(bf16[4,1024,128]{2,1,0:T(8,128)(2,1)} %broadcast_in_dim.17), calls=%async_computation.2 | async-start | bytes 2097152 | tf_op jit(solution)/shard_map/all_to_all | solution.py:203
  85.9 4.2 %copy-start.7 = (bf16[48,256]{1,0:T(8,128)(2,1)S(1)}, bf16[48,256]{1,0:T(8,128)(2,1)}, u32[]{:S(2)}) copy-start(bf16[48,256]{1,0:T(8,128)(2,1)} %copy-done.6) | copy-start | bytes 73732
  85.9 4.2 %copy-start.9 = (bf16[48,256]{1,0:T(8,128)(2,1)S(1)}, bf16[48,256]{1,0:T(8,128)(2,1)}, u32[]{:S(2)}) copy-start(bf16[48,256]{1,0:T(8,128)(2,1)} %copy-done.8) | copy-start | bytes 73732
  88.1 3.5 %collective-permute-start.5 = (bf16[256,512]{1,0:T(8,128)(2,1)S(1)}, bf16[256,512]{1,0:T(8,128)(2,1)S(1)}, u32[]{:S(2)}, u32[]{:S(2)}) collective-permute-start(bf16[256,512]{1,0:T(8,128)(2,1)S(1)} %half_finish.2.mine), channel_id=1, source_target_pairs={{0,1},{1,0},{2,3},{3,2},{4,5},{5,4},{6,7},{7,6},{8,9},{9,8},{10,11... | collective-permute-start | bytes 786440 | tf_op jit(solution)/shard_map/ppermute | solution.py:206
  92.5 9.5 %collective-permute-start.6 = (bf16[48,1024]{1,0:T(8,128)(2,1)}, bf16[48,1024]{1,0:T(8,128)(2,1)S(1)}, u32[]{:S(2)}, u32[]{:S(2)}) collective-permute-start(bf16[48,1024]{1,0:T(8,128)(2,1)} %get-tuple-element.51), channel_id=1, source_target_pairs={{0,2},{2,0},{1,3},{3,1},{4,6},{6,4},{5,7},{7,5},{8,10},{10,8},{9,1... | collective-permute-start | bytes 294920 | tf_op jit(solution)/shard_map/ppermute | solution.py:213
  95.0 12.2 %collective-permute-start.7 = (bf16[48,1024]{1,0:T(8,128)(2,1)S(1)}, bf16[48,1024]{1,0:T(8,128)(2,1)S(1)}, u32[]{:S(2)}, u32[]{:S(2)}) collective-permute-start(bf16[48,1024]{1,0:T(8,128)(2,1)S(1)} %get-tuple-element.52), channel_id=1, source_target_pairs={{2,4},{4,2},{3,5},{5,3},{6,8},{8,6},{7,9},{9,7},{10,12},{12,10},{1... | collective-permute-start | bytes 294920 | tf_op jit(solution)/shard_map/ppermute | solution.py:213
  99.4 1.0 copy-start.5
  100.8 22.3 %copy-start.4 = (bf16[128,1024]{1,0:T(8,128)(2,1)S(1)}, bf16[128,1024]{1,0:T(8,128)(2,1)}, u32[]{:S(2)}) copy-start(bf16[128,1024]{1,0:T(8,128)(2,1)} %get-tuple-element.88.refs_3_) | copy-start | bytes 786436
  110.1 3.8 %collective-permute-start.8 = (bf16[256,512]{1,0:T(8,128)(2,1)}, bf16[256,512]{1,0:T(8,128)(2,1)}, u32[]{:S(2)}, u32[]{:S(2)}) collective-permute-start(bf16[256,512]{1,0:T(8,128)(2,1)} %half_finish.3.mine), channel_id=1, source_target_pairs={{0,1},{1,0},{2,3},{3,2},{4,5},{5,4},{6,7},{7,6},{8,9},{9,8},{10,11... | collective-permute-start | bytes 786440 | tf_op jit(solution)/shard_map/ppermute | solution.py:206
  115.8 10.3 %collective-permute-start.10 = (bf16[48,1024]{1,0:T(8,128)(2,1)}, bf16[48,1024]{1,0:T(8,128)(2,1)S(1)}, u32[]{:S(2)}, u32[]{:S(2)}) collective-permute-start(bf16[48,1024]{1,0:T(8,128)(2,1)} %get-tuple-element.57), channel_id=1, source_target_pairs={{2,4},{4,2},{3,5},{5,3},{6,8},{8,6},{7,9},{9,7},{10,12},{12,10},{1... | collective-permute-start | bytes 294920 | tf_op jit(solution)/shard_map/ppermute | solution.py:213
  120.5 6.5 %collective-permute-start.9 = (bf16[48,1024]{1,0:T(8,128)(2,1)S(1)}, bf16[48,1024]{1,0:T(8,128)(2,1)S(1)}, u32[]{:S(2)}, u32[]{:S(2)}) collective-permute-start(bf16[48,1024]{1,0:T(8,128)(2,1)S(1)} %get-tuple-element.56), channel_id=1, source_target_pairs={{0,2},{2,0},{1,3},{3,1},{4,6},{6,4},{5,7},{7,5},{8,10},{10,8},{9,1... | collective-permute-start | bytes 294920 | tf_op jit(solution)/shard_map/ppermute | solution.py:213
  125.0 10.0 %copy-start.3 = (bf16[128,1024]{1,0:T(8,128)(2,1)S(1)}, bf16[128,1024]{1,0:T(8,128)(2,1)}, u32[]{:S(2)}) copy-start(bf16[128,1024]{1,0:T(8,128)(2,1)} %get-tuple-element.89.refs_3_) | copy-start | bytes 786436
  128.2 9.3 %collective-permute-start.11 = (bf16[48,1024]{1,0:T(8,128)(2,1)S(1)}, bf16[48,1024]{1,0:T(8,128)(2,1)S(1)}, u32[]{:S(2)}, u32[]{:S(2)}) collective-permute-start(bf16[48,1024]{1,0:T(8,128)(2,1)S(1)} %get-tuple-element.61), channel_id=1, source_target_pairs={{0,2},{2,0},{1,3},{3,1},{4,6},{6,4},{5,7},{7,5},{8,10},{10,8},{9,1... | collective-permute-start | bytes 294920 | tf_op jit(solution)/shard_map/ppermute | solution.py:213
  130.4 9.8 %collective-permute-start.12 = (bf16[48,1024]{1,0:T(8,128)(2,1)S(1)}, bf16[48,1024]{1,0:T(8,128)(2,1)S(1)}, u32[]{:S(2)}, u32[]{:S(2)}) collective-permute-start(bf16[48,1024]{1,0:T(8,128)(2,1)S(1)} %get-tuple-element.62), channel_id=1, source_target_pairs={{2,4},{4,2},{3,5},{5,3},{6,8},{8,6},{7,9},{9,7},{10,12},{12,10},{1... | collective-permute-start | bytes 294920 | tf_op jit(solution)/shard_map/ppermute | solution.py:213
  137.6 10.4 %copy-start.2 = (bf16[128,1024]{1,0:T(8,128)(2,1)S(1)}, bf16[128,1024]{1,0:T(8,128)(2,1)}, u32[]{:S(2)}) copy-start(bf16[128,1024]{1,0:T(8,128)(2,1)} %get-tuple-element.90.refs_3_) | copy-start | bytes 786436
  141.5 9.1 %collective-permute-start.13 = (bf16[48,1024]{1,0:T(8,128)(2,1)S(1)}, bf16[48,1024]{1,0:T(8,128)(2,1)S(1)}, u32[]{:S(2)}, u32[]{:S(2)}) collective-permute-start(bf16[48,1024]{1,0:T(8,128)(2,1)S(1)} %get-tuple-element.66), channel_id=1, source_target_pairs={{0,2},{2,0},{1,3},{3,1},{4,6},{6,4},{5,7},{7,5},{8,10},{10,8},{9,1... | collective-permute-start | bytes 294920 | tf_op jit(solution)/shard_map/ppermute | solution.py:213
  143.4 9.8 %collective-permute-start.14 = (bf16[48,1024]{1,0:T(8,128)(2,1)S(1)}, bf16[48,1024]{1,0:T(8,128)(2,1)S(1)}, u32[]{:S(2)}, u32[]{:S(2)}) collective-permute-start(bf16[48,1024]{1,0:T(8,128)(2,1)S(1)} %get-tuple-element.67), channel_id=1, source_target_pairs={{2,4},{4,2},{3,5},{5,3},{6,8},{8,6},{7,9},{9,7},{10,12},{12,10},{1... | collective-permute-start | bytes 294920 | tf_op jit(solution)/shard_map/ppermute | solution.py:213
  150.6 10.6 %copy-start.1 = (bf16[128,1024]{1,0:T(8,128)(2,1)S(1)}, bf16[128,1024]{1,0:T(8,128)(2,1)}, u32[]{:S(2)}) copy-start(bf16[128,1024]{1,0:T(8,128)(2,1)} %get-tuple-element.91.refs_3_) | copy-start | bytes 786436
  154.5 9.3 %collective-permute-start.15 = (bf16[48,1024]{1,0:T(8,128)(2,1)S(1)}, bf16[48,1024]{1,0:T(8,128)(2,1)S(1)}, u32[]{:S(2)}, u32[]{:S(2)}) collective-permute-start(bf16[48,1024]{1,0:T(8,128)(2,1)S(1)} %get-tuple-element.71), channel_id=1, source_target_pairs={{0,2},{2,0},{1,3},{3,1},{4,6},{6,4},{5,7},{7,5},{8,10},{10,8},{9,1... | collective-permute-start | bytes 294920 | tf_op jit(solution)/shard_map/ppermute | solution.py:213
  156.4 9.8 %collective-permute-start.16 = (bf16[48,1024]{1,0:T(8,128)(2,1)S(1)}, bf16[48,1024]{1,0:T(8,128)(2,1)S(1)}, u32[]{:S(2)}, u32[]{:S(2)}) collective-permute-start(bf16[48,1024]{1,0:T(8,128)(2,1)S(1)} %get-tuple-element.72), channel_id=1, source_target_pairs={{2,4},{4,2},{3,5},{5,3},{6,8},{8,6},{7,9},{9,7},{10,12},{12,10},{1... | collective-permute-start | bytes 294920 | tf_op jit(solution)/shard_map/ppermute | solution.py:213
  167.5 9.1 %collective-permute-start.17 = (bf16[48,1024]{1,0:T(8,128)(2,1)S(1)}, bf16[48,1024]{1,0:T(8,128)(2,1)S(1)}, u32[]{:S(2)}, u32[]{:S(2)}) collective-permute-start(bf16[48,1024]{1,0:T(8,128)(2,1)S(1)} %get-tuple-element.76), channel_id=1, source_target_pairs={{0,2},{2,0},{1,3},{3,1},{4,6},{6,4},{5,7},{7,5},{8,10},{10,8},{9,1... | collective-permute-start | bytes 294920 | tf_op jit(solution)/shard_map/ppermute | solution.py:213
  169.4 9.8 %collective-permute-start.18 = (bf16[48,1024]{1,0:T(8,128)(2,1)S(1)}, bf16[48,1024]{1,0:T(8,128)(2,1)S(1)}, u32[]{:S(2)}, u32[]{:S(2)}) collective-permute-start(bf16[48,1024]{1,0:T(8,128)(2,1)S(1)} %get-tuple-element.77), channel_id=1, source_target_pairs={{2,4},{4,2},{3,5},{5,3},{6,8},{8,6},{7,9},{9,7},{10,12},{12,10},{1... | collective-permute-start | bytes 294920 | tf_op jit(solution)/shard_map/ppermute | solution.py:213
  180.5 9.1 %collective-permute-start.19 = (bf16[48,1024]{1,0:T(8,128)(2,1)S(1)}, bf16[48,1024]{1,0:T(8,128)(2,1)S(1)}, u32[]{:S(2)}, u32[]{:S(2)}) collective-permute-start(bf16[48,1024]{1,0:T(8,128)(2,1)S(1)} %get-tuple-element.81), channel_id=1, source_target_pairs={{0,2},{2,0},{1,3},{3,1},{4,6},{6,4},{5,7},{7,5},{8,10},{10,8},{9,1... | collective-permute-start | bytes 294920 | tf_op jit(solution)/shard_map/ppermute | solution.py:213
  182.5 9.8 %collective-permute-start.20 = (bf16[48,1024]{1,0:T(8,128)(2,1)S(1)}, bf16[48,1024]{1,0:T(8,128)(2,1)S(1)}, u32[]{:S(2)}, u32[]{:S(2)}) collective-permute-start(bf16[48,1024]{1,0:T(8,128)(2,1)S(1)} %get-tuple-element.82), channel_id=1, source_target_pairs={{2,4},{4,2},{3,5},{5,3},{6,8},{8,6},{7,9},{9,7},{10,12},{12,10},{1... | collective-permute-start | bytes 294920 | tf_op jit(solution)/shard_map/ppermute | solution.py:213
Sparse Core Ops, SparseCore 0:
  10.6 103.2 all-gather.1
